TPU v7x, 32 devices: a whole 2x2x4 slice. The times are simulated.
32 devices in a mesh: row: 4 (over y, x), col: 4 (over z), panel: 2 (over core).
Axes of the slice: x: 2, y: 2, z: 4, core: 2. Of those that a mesh axis runs over, the one named last changes fastest.
Arguments:
- basis_values: bfloat16 [512, 2048, 128], P(('row', 'col', 'panel')), may hold values from -6 to 6
- potential: float32 [65536], P(('row', 'col', 'panel')), may hold values from -0.0014648438 to 0.0014648438
- pair_atoms: int32 [2, 4096], P(None, ('row', 'col', 'panel')), may hold values from 0 to 15
- target_device: int32 [4096, 1], P(('row', 'col', 'panel')), may hold values from 0 to 31; in each aligned block of 128 rows (0 to 127, 128 to 255, ...) at most 6 rows name the same one
- target_block: int32 [4096], P(('row', 'col', 'panel')), may hold values from 0 to 1
- density: bfloat16 [1024, 1024], P('row', 'col'), may hold values from -0.3125 to 0.3125
- density_mask: int32 [8, 8], P('row', 'col'), may hold values 0 or 1
- inverse_intersection: bfloat16 [1024, 2048], P('row', 'col'), may hold values from -6 to 6
- inverse_mask: int32 [8, 16], P('row', 'col'), may hold values 0 or 1
Outputs:
- gradient: float32 [1024, 2048], P('row', ('col', 'panel'))
Inputs may be any that keep to these rules, and one draw needn't show every extreme that they name: `target_device`: among the 128 rows of one device no owner appears more than 6 times.
All inputs are finite; a program needn't handle non-finite values. No bound on the sum of `density_mask` or of `inverse_mask` on one device may be relied on, other than what follows from the above.
Results may differ from a plain program's by a relative error of at most 0.0058.
Values may be sent and summed in bfloat16 or wider, within the bound.
No kernel may reach another device: no remote copies, remote signals or barrier semaphores. Data moves between devices by JAX's collectives and lax.ppermute only.
A program may use at most 128 MiB of HBM per device.

v0:
```python
import math

import jax
import jax.numpy as jnp
from jax import lax
from jax.sharding import PartitionSpec as P


def shifted_2(block, axis, distance):
    devices = range(lax.axis_size(axis))
    route = [((i - distance) % len(devices), i) for i in devices]
    return lax.ppermute(block, axis, route)


def masked_blocks(matrix, block_mask, block_size):
    mask_rows, mask_cols = block_mask.shape
    shaped = matrix.reshape(mask_rows, block_size, mask_cols, block_size)
    factor = block_mask.astype(matrix.dtype)[:, None, :, None]
    return (shaped * factor).reshape(mask_rows * block_size, mask_cols * block_size)


def rotate_cols(tile_value, amount, loop_size):
    for bit_number in range((loop_size - 1).bit_length()):
        shifted = shifted_2(tile_value, "col", -(1 << bit_number))
        tile_value = jnp.where((amount >> bit_number) % 2 == 1, shifted, tile_value)
    return tile_value


def rotate_rows(tile_value, amount, loop_size):
    for bit_number in range((loop_size - 1).bit_length()):
        shifted = shifted_2(tile_value, "row", -(1 << bit_number))
        tile_value = jnp.where((amount >> bit_number) % 2 == 1, shifted, tile_value)
    return tile_value


def cannon_product(left_tile, right_tile, offset, step_count):
    loop_size = lax.axis_size("col")
    left_tile = rotate_cols(left_tile, (lax.axis_index("row") + offset) % loop_size, loop_size)
    right_tile = rotate_rows(right_tile, (lax.axis_index("col") + offset) % loop_size, loop_size)
    accumulated = jnp.dot(left_tile, right_tile, preferred_element_type=jnp.float32)

    def advance(turn_index, state_tuple):
        running, left_now, right_now = state_tuple
        left_now = shifted_2(left_now, "col", -1)
        right_now = shifted_2(right_now, "row", -1)
        running = running + jnp.dot(left_now, right_now, preferred_element_type=jnp.float32)
        return (running, left_now, right_now)

    accumulated, left_tile, right_tile = lax.fori_loop(
        0, step_count - 1, advance, (accumulated, left_tile, right_tile)
    )
    return accumulated


def local(
    basis_values,
    potential,
    pair_atoms,
    target_device,
    target_block,
    density,
    density_mask,
    inverse_intersection,
    inverse_mask,
):
    block_size = basis_values.shape[2]
    part_count = pair_atoms.shape[1]
    layers = lax.axis_size("panel")
    devices = lax.axis_size("row") * lax.axis_size("col") * layers
    capacity = max(2, 3 * part_count // (2 * devices))
    weighted = (basis_values.astype(jnp.float32) * potential[None, :, None]).astype(jnp.bfloat16)
    group_size = math.gcd(16, part_count)
    left_groups = pair_atoms[0].reshape(part_count // group_size, group_size)
    right_groups = pair_atoms[1].reshape(part_count // group_size, group_size)

    def one_group(pair_ids):
        left_rows = basis_values[pair_ids[0]]
        right_rows = weighted[pair_ids[1]]
        return jnp.einsum(
            "pgi,pgj->pij", left_rows, right_rows, preferred_element_type=jnp.float32
        ).astype(jnp.bfloat16)

    partials = lax.map(one_group, (left_groups, right_groups)).reshape(
        part_count, block_size, block_size
    )
    target = target_device[:, 0]
    serial = jnp.arange(part_count, dtype=jnp.int32)
    earlier = (target[:, None] == target[None, :]) & (serial[None, :] < serial[:, None])
    position = jnp.sum(earlier.astype(jnp.int32), axis=1)
    slot_index = target * capacity + position
    outgoing = (
        jnp.zeros((devices * capacity, block_size, block_size), jnp.bfloat16)
        .at[slot_index]
        .set(partials)
    )
    labels = jnp.full((devices * capacity,), -1, jnp.int32).at[slot_index].set(target_block)
    incoming, arrived = (
        lax.all_to_all(outgoing, ("row", "col", "panel"), split_axis=0, concat_axis=0, tiled=True),
        lax.all_to_all(labels, ("row", "col", "panel"), split_axis=0, concat_axis=0, tiled=True),
    )
    tile_blocks = density_mask.shape[0]
    half_blocks = tile_blocks // layers
    local_count = half_blocks * tile_blocks
    one_hot = (arrived.reshape(1, -1) == jnp.arange(local_count, dtype=jnp.int32)[:, None]).astype(
        jnp.bfloat16
    )
    summed = jnp.dot(
        one_hot, incoming.reshape(-1, block_size * block_size), preferred_element_type=jnp.float32
    ).astype(jnp.bfloat16)
    half_tile = summed.reshape(half_blocks, tile_blocks, block_size, block_size).transpose(
        0, 2, 1, 3
    )
    half_tile = half_tile.reshape(half_blocks * block_size, tile_blocks * block_size)
    hamiltonian = lax.all_gather(half_tile, "panel", axis=0, tiled=True)
    density_used = masked_blocks(density, density_mask, block_size)
    inverse_used = masked_blocks(inverse_intersection, inverse_mask, block_size)
    loop_size = lax.axis_size("row")
    layer_index = lax.axis_index("panel")
    per_layer = loop_size // layers
    offset = layer_index * per_layer
    product_part = cannon_product(density_used, inverse_used, offset, per_layer)
    panel_product = lax.psum(product_part, "panel").astype(jnp.bfloat16)
    gradient_part = cannon_product(hamiltonian, panel_product, offset, per_layer)
    return lax.psum_scatter(gradient_part, "panel", scatter_dimension=1, tiled=True)


def solution(mesh):
    placed = (
        P(("row", "col", "panel"), None, None),
        P(("row", "col", "panel")),
        P(None, ("row", "col", "panel")),
        P(("row", "col", "panel"), None),
        P(("row", "col", "panel")),
        P("row", "col"),
        P("row", "col"),
        P("row", "col"),
        P("row", "col"),
    )
    return jax.shard_map(
        local, mesh=mesh, in_specs=placed, out_specs=P("row", ("col", "panel")), check_vma=False
    )
```

profile of v0, /device:TPU:0, one launch (start us, length us, event | category | flops | bytes accessed | tf_op | source)
XLA Modules:
  0.0 466.9 jit_solution(15373283749823389173)
XLA Ops:
  9.9 7.3 %all-to-all-start = ((s32[32,6,1]{1,2,0:T(1,128)}), s32[32,6,1]{1,2,0:T(1,128)S(1)}, u32[]{:S(2)}, u32[]{:S(2)}) async-start(s32[32,6,1]{1,2,0:T(1,128)} %bitcast.8), calls=%async_computation | async-start | bytes 32768 | tf_op jit(solution)/shard_map/all_to_all | solution.py:99
  18.2 9.3 %multiply_convert_fusion = bf16[16,2048,128]{2,1,0:T(8,128)(2,1)} fusion(bf16[16,2048,128]{2,1,0:T(8,128)(2,1)} %param.11, f32[2048]{0:T(1024)} %param.12), kind=kLoop, calls=%fused_computation.18 | loop fusion | flops 12582912 | bytes 16785408 | tf_op jit(solution)/shard_map/convert_element_type | solution.py:71
  27.5 202.9 %while.2 = (s32[]{:T(128)}, bf16[8,16,128,128]{3,2,1,0:T(8,128)(2,1)}, s32[8,16]{1,0:T(8,128)S(1)}, bf16[16,2048,128]{2,1,0:T(8,128)(2,1)}, s32[8,16]{1,0:T(8,12...) while((s32[]{:T(128)}, bf16[8,16,128,128]{3,2,1,0:T(8,128)(2,1)}, s32[8,16]{1,0:T(8,128)S(1)}, ...), condition=%wide.region_3.4_spmd, body=%wide.region_2.3_spmd.sunk | while | flops 1074006144 | bytes 50865232 | solution.py:83
  27.5 8.1 %gather_fusion = bf16[16,2048,128]{2,1,0:T(8,128)(2,1)} fusion(bf16[16,2048,128]{2,1,0:T(8,128)(2,1)} %get-tuple-element.136, s32[1024]{0:T(1024)S(1)} %pad_clamp_fusion.4), kind=kCustom, calls=%fused_computation.clone.1 | custom fusion | bytes 16777280 | tf_op jit(solution)/shard_map/while/body/eval_jaxpr/gather | solution.py:77
  35.6 8.1 %gather_fusion.1 = bf16[16,2048,128]{2,1,0:T(8,128)(2,1)} fusion(bf16[16,2048,128]{2,1,0:T(8,128)(2,1)} %get-tuple-element.138, s32[1024]{0:T(1024)S(1)} %pad_clamp_fusion.5), kind=kCustom, calls=%fused_computation.1.clone.1 | custom fusion | bytes 16777280 | tf_op jit(solution)/shard_map/while/body/eval_jaxpr/gather | solution.py:78
  43.7 9.2 %fusion.37 = bf16[8,16,128,128]{3,2,1,0:T(8,128)(2,1)} fusion(bf16[8,16,128,128]{3,2,1,0:T(8,128)(2,1)} %get-tuple-element.127, s32[]{:T(128)} %get-tuple-element.126, bf16[16,2048,128]{2,1,0:T(8,128)(2,1)} %gather_fusion, bf16[16,2048,128]{2,1,0:T(8,128)(2,1)} %gather_fusion.1), kind=kOutput, calls=%fused_computation.6.clone.1 | convolution fusion | flops 1074003968 | bytes 17302016 | tf_op jit(solution)/shard_map/while/body/eval_jaxpr/pgi,pgj->pij/dot_general | solution.py:79
  52.9 8.1 %gather_fusion = bf16[16,2048,128]{2,1,0:T(8,128)(2,1)} fusion(bf16[16,2048,128]{2,1,0:T(8,128)(2,1)} %get-tuple-element.136, s32[1024]{0:T(1024)S(1)} %pad_clamp_fusion.4), kind=kCustom, calls=%fused_computation.clone.1 | custom fusion | bytes 16777280 | tf_op jit(solution)/shard_map/while/body/eval_jaxpr/gather | solution.py:77
  61.0 8.1 %gather_fusion.1 = bf16[16,2048,128]{2,1,0:T(8,128)(2,1)} fusion(bf16[16,2048,128]{2,1,0:T(8,128)(2,1)} %get-tuple-element.138, s32[1024]{0:T(1024)S(1)} %pad_clamp_fusion.5), kind=kCustom, calls=%fused_computation.1.clone.1 | custom fusion | bytes 16777280 | tf_op jit(solution)/shard_map/while/body/eval_jaxpr/gather | solution.py:78
  69.2 9.1 %fusion.37 = bf16[8,16,128,128]{3,2,1,0:T(8,128)(2,1)} fusion(bf16[8,16,128,128]{3,2,1,0:T(8,128)(2,1)} %get-tuple-element.127, s32[]{:T(128)} %get-tuple-element.126, bf16[16,2048,128]{2,1,0:T(8,128)(2,1)} %gather_fusion, bf16[16,2048,128]{2,1,0:T(8,128)(2,1)} %gather_fusion.1), kind=kOutput, calls=%fused_computation.6.clone.1 | convolution fusion | flops 1074003968 | bytes 17302016 | tf_op jit(solution)/shard_map/while/body/eval_jaxpr/pgi,pgj->pij/dot_general | solution.py:79
  78.3 8.1 %gather_fusion = bf16[16,2048,128]{2,1,0:T(8,128)(2,1)} fusion(bf16[16,2048,128]{2,1,0:T(8,128)(2,1)} %get-tuple-element.136, s32[1024]{0:T(1024)S(1)} %pad_clamp_fusion.4), kind=kCustom, calls=%fused_computation.clone.1 | custom fusion | bytes 16777280 | tf_op jit(solution)/shard_map/while/body/eval_jaxpr/gather | solution.py:77
  86.4 8.1 %gather_fusion.1 = bf16[16,2048,128]{2,1,0:T(8,128)(2,1)} fusion(bf16[16,2048,128]{2,1,0:T(8,128)(2,1)} %get-tuple-element.138, s32[1024]{0:T(1024)S(1)} %pad_clamp_fusion.5), kind=kCustom, calls=%fused_computation.1.clone.1 | custom fusion | bytes 16777280 | tf_op jit(solution)/shard_map/while/body/eval_jaxpr/gather | solution.py:78
  94.6 9.1 %fusion.37 = bf16[8,16,128,128]{3,2,1,0:T(8,128)(2,1)} fusion(bf16[8,16,128,128]{3,2,1,0:T(8,128)(2,1)} %get-tuple-element.127, s32[]{:T(128)} %get-tuple-element.126, bf16[16,2048,128]{2,1,0:T(8,128)(2,1)} %gather_fusion, bf16[16,2048,128]{2,1,0:T(8,128)(2,1)} %gather_fusion.1), kind=kOutput, calls=%fused_computation.6.clone.1 | convolution fusion | flops 1074003968 | bytes 17302016 | tf_op jit(solution)/shard_map/while/body/eval_jaxpr/pgi,pgj->pij/dot_general | solution.py:79
  103.7 8.1 %gather_fusion = bf16[16,2048,128]{2,1,0:T(8,128)(2,1)} fusion(bf16[16,2048,128]{2,1,0:T(8,128)(2,1)} %get-tuple-element.136, s32[1024]{0:T(1024)S(1)} %pad_clamp_fusion.4), kind=kCustom, calls=%fused_computation.clone.1 | custom fusion | bytes 16777280 | tf_op jit(solution)/shard_map/while/body/eval_jaxpr/gather | solution.py:77
  111.8 8.1 %gather_fusion.1 = bf16[16,2048,128]{2,1,0:T(8,128)(2,1)} fusion(bf16[16,2048,128]{2,1,0:T(8,128)(2,1)} %get-tuple-element.138, s32[1024]{0:T(1024)S(1)} %pad_clamp_fusion.5), kind=kCustom, calls=%fused_computation.1.clone.1 | custom fusion | bytes 16777280 | tf_op jit(solution)/shard_map/while/body/eval_jaxpr/gather | solution.py:78
  119.9 9.1 %fusion.37 = bf16[8,16,128,128]{3,2,1,0:T(8,128)(2,1)} fusion(bf16[8,16,128,128]{3,2,1,0:T(8,128)(2,1)} %get-tuple-element.127, s32[]{:T(128)} %get-tuple-element.126, bf16[16,2048,128]{2,1,0:T(8,128)(2,1)} %gather_fusion, bf16[16,2048,128]{2,1,0:T(8,128)(2,1)} %gather_fusion.1), kind=kOutput, calls=%fused_computation.6.clone.1 | convolution fusion | flops 1074003968 | bytes 17302016 | tf_op jit(solution)/shard_map/while/body/eval_jaxpr/pgi,pgj->pij/dot_general | solution.py:79
  129.0 8.1 %gather_fusion = bf16[16,2048,128]{2,1,0:T(8,128)(2,1)} fusion(bf16[16,2048,128]{2,1,0:T(8,128)(2,1)} %get-tuple-element.136, s32[1024]{0:T(1024)S(1)} %pad_clamp_fusion.4), kind=kCustom, calls=%fused_computation.clone.1 | custom fusion | bytes 16777280 | tf_op jit(solution)/shard_map/while/body/eval_jaxpr/gather | solution.py:77
  137.1 8.1 %gather_fusion.1 = bf16[16,2048,128]{2,1,0:T(8,128)(2,1)} fusion(bf16[16,2048,128]{2,1,0:T(8,128)(2,1)} %get-tuple-element.138, s32[1024]{0:T(1024)S(1)} %pad_clamp_fusion.5), kind=kCustom, calls=%fused_computation.1.clone.1 | custom fusion | bytes 16777280 | tf_op jit(solution)/shard_map/while/body/eval_jaxpr/gather | solution.py:78
  145.2 9.1 %fusion.37 = bf16[8,16,128,128]{3,2,1,0:T(8,128)(2,1)} fusion(bf16[8,16,128,128]{3,2,1,0:T(8,128)(2,1)} %get-tuple-element.127, s32[]{:T(128)} %get-tuple-element.126, bf16[16,2048,128]{2,1,0:T(8,128)(2,1)} %gather_fusion, bf16[16,2048,128]{2,1,0:T(8,128)(2,1)} %gather_fusion.1), kind=kOutput, calls=%fused_computation.6.clone.1 | convolution fusion | flops 1074003968 | bytes 17302016 | tf_op jit(solution)/shard_map/while/body/eval_jaxpr/pgi,pgj->pij/dot_general | solution.py:79
  154.4 8.1 %gather_fusion = bf16[16,2048,128]{2,1,0:T(8,128)(2,1)} fusion(bf16[16,2048,128]{2,1,0:T(8,128)(2,1)} %get-tuple-element.136, s32[1024]{0:T(1024)S(1)} %pad_clamp_fusion.4), kind=kCustom, calls=%fused_computation.clone.1 | custom fusion | bytes 16777280 | tf_op jit(solution)/shard_map/while/body/eval_jaxpr/gather | solution.py:77
  162.5 8.1 %gather_fusion.1 = bf16[16,2048,128]{2,1,0:T(8,128)(2,1)} fusion(bf16[16,2048,128]{2,1,0:T(8,128)(2,1)} %get-tuple-element.138, s32[1024]{0:T(1024)S(1)} %pad_clamp_fusion.5), kind=kCustom, calls=%fused_computation.1.clone.1 | custom fusion | bytes 16777280 | tf_op jit(solution)/shard_map/while/body/eval_jaxpr/gather | solution.py:78
  170.6 9.1 %fusion.37 = bf16[8,16,128,128]{3,2,1,0:T(8,128)(2,1)} fusion(bf16[8,16,128,128]{3,2,1,0:T(8,128)(2,1)} %get-tuple-element.127, s32[]{:T(128)} %get-tuple-element.126, bf16[16,2048,128]{2,1,0:T(8,128)(2,1)} %gather_fusion, bf16[16,2048,128]{2,1,0:T(8,128)(2,1)} %gather_fusion.1), kind=kOutput, calls=%fused_computation.6.clone.1 | convolution fusion | flops 1074003968 | bytes 17302016 | tf_op jit(solution)/shard_map/while/body/eval_jaxpr/pgi,pgj->pij/dot_general | solution.py:79
  179.8 8.1 %gather_fusion = bf16[16,2048,128]{2,1,0:T(8,128)(2,1)} fusion(bf16[16,2048,128]{2,1,0:T(8,128)(2,1)} %get-tuple-element.136, s32[1024]{0:T(1024)S(1)} %pad_clamp_fusion.4), kind=kCustom, calls=%fused_computation.clone.1 | custom fusion | bytes 16777280 | tf_op jit(solution)/shard_map/while/body/eval_jaxpr/gather | solution.py:77
  187.9 8.1 %gather_fusion.1 = bf16[16,2048,128]{2,1,0:T(8,128)(2,1)} fusion(bf16[16,2048,128]{2,1,0:T(8,128)(2,1)} %get-tuple-element.138, s32[1024]{0:T(1024)S(1)} %pad_clamp_fusion.5), kind=kCustom, calls=%fused_computation.1.clone.1 | custom fusion | bytes 16777280 | tf_op jit(solution)/shard_map/while/body/eval_jaxpr/gather | solution.py:78
  196.0 9.1 %fusion.37 = bf16[8,16,128,128]{3,2,1,0:T(8,128)(2,1)} fusion(bf16[8,16,128,128]{3,2,1,0:T(8,128)(2,1)} %get-tuple-element.127, s32[]{:T(128)} %get-tuple-element.126, bf16[16,2048,128]{2,1,0:T(8,128)(2,1)} %gather_fusion, bf16[16,2048,128]{2,1,0:T(8,128)(2,1)} %gather_fusion.1), kind=kOutput, calls=%fused_computation.6.clone.1 | convolution fusion | flops 1074003968 | bytes 17302016 | tf_op jit(solution)/shard_map/while/body/eval_jaxpr/pgi,pgj->pij/dot_general | solution.py:79
  205.1 8.1 %gather_fusion = bf16[16,2048,128]{2,1,0:T(8,128)(2,1)} fusion(bf16[16,2048,128]{2,1,0:T(8,128)(2,1)} %get-tuple-element.136, s32[1024]{0:T(1024)S(1)} %pad_clamp_fusion.4), kind=kCustom, calls=%fused_computation.clone.1 | custom fusion | bytes 16777280 | tf_op jit(solution)/shard_map/while/body/eval_jaxpr/gather | solution.py:77
  213.2 8.1 %gather_fusion.1 = bf16[16,2048,128]{2,1,0:T(8,128)(2,1)} fusion(bf16[16,2048,128]{2,1,0:T(8,128)(2,1)} %get-tuple-element.138, s32[1024]{0:T(1024)S(1)} %pad_clamp_fusion.5), kind=kCustom, calls=%fused_computation.1.clone.1 | custom fusion | bytes 16777280 | tf_op jit(solution)/shard_map/while/body/eval_jaxpr/gather | solution.py:78
  221.3 9.1 %fusion.37 = bf16[8,16,128,128]{3,2,1,0:T(8,128)(2,1)} fusion(bf16[8,16,128,128]{3,2,1,0:T(8,128)(2,1)} %get-tuple-element.127, s32[]{:T(128)} %get-tuple-element.126, bf16[16,2048,128]{2,1,0:T(8,128)(2,1)} %gather_fusion, bf16[16,2048,128]{2,1,0:T(8,128)(2,1)} %gather_fusion.1), kind=kOutput, calls=%fused_computation.6.clone.1 | convolution fusion | flops 1074003968 | bytes 17302016 | tf_op jit(solution)/shard_map/while/body/eval_jaxpr/pgi,pgj->pij/dot_general | solution.py:79
  234.6 19.6 %scatter_fusion = bf16[192,128,128]{2,1,0:T(8,128)(2,1)} fusion(bf16[192,128,128]{2,1,0:T(8,128)(2,1)} %broadcast_in_dim.13, s32[128]{0:T(128)S(1)} %fusion.15, bf16[128,128,128]{2,1,0:T(8,128)(2,1)} %bitcast.78), kind=kCustom, calls=%fused_computation.3 | custom fusion | bytes 12583424 | tf_op jit(solution)/shard_map/scatter | solution.py:94
  266.9 47.0 %collective-permute-done.4 = bf16[256,512]{1,0:T(8,128)(2,1)S(1)} collective-permute-done((bf16[256,512]{1,0:T(8,128)(2,1)S(1)}, bf16[256,512]{1,0:T(8,128)(2,1)S(1)}, u32[]{:S(2)}, u32[]{:S(2)}) %collective-permute-start.4) | collective-permute-done | bytes 262176 | tf_op jit(solution)/shard_map/ppermute | solution.py:12
  315.3 50.8 %collective-permute-done.2 = bf16[256,256]{1,0:T(8,128)(2,1)S(1)} collective-permute-done((bf16[256,256]{1,0:T(8,128)(2,1)S(1)}, bf16[256,256]{1,0:T(8,128)(2,1)S(1)}, u32[]{:S(2)}, u32[]{:S(2)}) %collective-permute-start.2) | collective-permute-done | bytes 131104 | tf_op jit(solution)/shard_map/ppermute | solution.py:12
  366.1 35.3 %collective-permute-start.3 = (bf16[256,256]{1,0:T(8,128)(2,1)S(1)}, bf16[256,256]{1,0:T(8,128)(2,1)S(1)}, u32[]{:S(2)}, u32[]{:S(2)}) collective-permute-start(bf16[256,256]{1,0:T(8,128)(2,1)S(1)} %broadcast_select_fusion.4), channel_id=1, source_target_pairs={{4,0},{6,2},{0,4},{2,6},{5,1},{7,3},{1,5},{3,7},{12,8},{14,10},{8,... | collective-permute-start | bytes 393224 | tf_op jit(solution)/shard_map/ppermute | solution.py:12
  452.1 8.0 %reduce-scatter.2.cloned.1.call-done = f32[256,256]{1,0:T(8,128)} async-done(((f32[256,512]{1,0:T(8,128)}), f32[256,256]{1,0:T(8,128)}) %reduce-scatter.2.cloned.1.call-update) | async-done | bytes 262160 | tf_op jit(solution)/shard_map/reduce_scatter | solution.py:124
  (94 shorter events, 73.3 us)
Async XLA Ops:
  9.9 244.3 %all-to-all-start = ((s32[32,6,1]{1,2,0:T(1,128)}), s32[32,6,1]{1,2,0:T(1,128)S(1)}, u32[]{:S(2)}, u32[]{:S(2)}) async-start(s32[32,6,1]{1,2,0:T(1,128)} %bitcast.8), calls=%async_computation | async-start | bytes 32768 | tf_op jit(solution)/shard_map/all_to_all | solution.py:99
  254.2 6.2 %copy-start.2 = (s32[2,4]{1,0:T(2,128)S(1)}, s32[2,4]{1,0:T(2,128)}, u32[]{:S(2)}) copy-start(s32[2,4]{1,0:T(2,128)} %param.19) | copy-start | bytes 100
  254.2 6.4 %copy-start = (bf16[256,512]{1,0:T(8,128)(2,1)S(1)}, bf16[256,512]{1,0:T(8,128)(2,1)}, u32[]{:S(2)}) copy-start(bf16[256,512]{1,0:T(8,128)(2,1)} %param.18) | copy-start | bytes 786436
  254.2 9.1 %copy-start.3 = (s32[2,2]{1,0:T(2,128)S(1)}, s32[2,2]{1,0:T(2,128)}, u32[]{:S(2)}) copy-start(s32[2,2]{1,0:T(2,128)} %param.17) | copy-start | bytes 52
  254.2 9.2 %copy-start.1 = (bf16[256,256]{1,0:T(8,128)(2,1)S(1)}, bf16[256,256]{1,0:T(8,128)(2,1)}, u32[]{:S(2)}) copy-start(bf16[256,256]{1,0:T(8,128)(2,1)} %param.16) | copy-start | bytes 393220
  254.2 167.2 %all-to-all-start.1 = ((bf16[192,128,128]{2,1,0:T(8,128)(2,1)}), bf16[192,128,128]{2,1,0:T(8,128)(2,1)}, u32[]{:S(2)}, u32[]{:S(2)}) async-start(bf16[192,128,128]{2,1,0:T(8,128)(2,1)} %scatter_fusion), calls=%async_computation.1 | async-start | bytes 12582912 | tf_op jit(solution)/shard_map/all_to_all | solution.py:98
  260.3 199.7 %reduce-scatter.2.cloned.1.call-start = ((), (), s32[]{:S(2)}) async-start(), calls=%async_computation.3 | async-start | bytes 786432 | tf_op jit(solution)/shard_map/reduce_scatter | solution.py:124
  260.6 53.3 %collective-permute-start.4 = (bf16[256,512]{1,0:T(8,128)(2,1)S(1)}, bf16[256,512]{1,0:T(8,128)(2,1)S(1)}, u32[]{:S(2)}, u32[]{:S(2)}) collective-permute-start(bf16[256,512]{1,0:T(8,128)(2,1)S(1)} %bitcast_multiply_fusion), channel_id=1, source_target_pairs={{8,0},{16,8},{24,16},{0,24},{9,1},{17,9},{25,17},{1,25},{10,2},{18... | collective-permute-start | bytes 786440 | tf_op jit(solution)/shard_map/ppermute | solution.py:12
  263.5 102.6 %collective-permute-start.2 = (bf16[256,256]{1,0:T(8,128)(2,1)S(1)}, bf16[256,256]{1,0:T(8,128)(2,1)S(1)}, u32[]{:S(2)}, u32[]{:S(2)}) collective-permute-start(bf16[256,256]{1,0:T(8,128)(2,1)S(1)} %bitcast_multiply_fusion.1), channel_id=1, source_target_pairs={{2,0},{4,2},{6,4},{0,6},{3,1},{5,3},{7,5},{1,7},{10,8},{12,10},{14... | collective-permute-start | bytes 393224 | tf_op jit(solution)/shard_map/ppermute | solution.py:12
  313.9 87.5 %collective-permute-start.5 = (bf16[256,512]{1,0:T(8,128)(2,1)S(1)}, bf16[256,512]{1,0:T(8,128)(2,1)S(1)}, u32[]{:S(2)}, u32[]{:S(2)}) collective-permute-start(bf16[256,512]{1,0:T(8,128)(2,1)S(1)} %broadcast_select_fusion.1), channel_id=1, source_target_pairs={{16,0},{24,8},{0,16},{8,24},{17,1},{25,9},{1,17},{9,25},{18,2},{26... | collective-permute-start | bytes 786440 | tf_op jit(solution)/shard_map/ppermute | solution.py:12
  366.1 38.5 %collective-permute-start.3 = (bf16[256,256]{1,0:T(8,128)(2,1)S(1)}, bf16[256,256]{1,0:T(8,128)(2,1)S(1)}, u32[]{:S(2)}, u32[]{:S(2)}) collective-permute-start(bf16[256,256]{1,0:T(8,128)(2,1)S(1)} %broadcast_select_fusion.4), channel_id=1, source_target_pairs={{4,0},{6,2},{0,4},{2,6},{5,1},{7,3},{1,5},{3,7},{12,8},{14,10},{8,... | collective-permute-start | bytes 393224 | tf_op jit(solution)/shard_map/ppermute | solution.py:12
  401.4 12.2 %collective-permute-start.7 = (bf16[256,512]{1,0:T(8,128)(2,1)S(1)}, bf16[256,512]{1,0:T(8,128)(2,1)S(1)}, u32[]{:S(2)}, u32[]{:S(2)}) collective-permute-start(bf16[256,512]{1,0:T(8,128)(2,1)S(1)} %broadcast_select_fusion.3), channel_id=1, source_target_pairs={{8,0},{16,8},{24,16},{0,24},{9,1},{17,9},{25,17},{1,25},{10,2},{18... | collective-permute-start | bytes 786440 | tf_op jit(solution)/shard_map/while/body/eval_jaxpr/ppermute | solution.py:12
  404.6 9.0 %collective-permute-start.6 = (bf16[256,256]{1,0:T(8,128)(2,1)S(1)}, bf16[256,256]{1,0:T(8,128)(2,1)S(1)}, u32[]{:S(2)}, u32[]{:S(2)}) collective-permute-start(bf16[256,256]{1,0:T(8,128)(2,1)S(1)} %broadcast_select_fusion.6), channel_id=1, source_target_pairs={{2,0},{4,2},{6,4},{0,6},{3,1},{5,3},{7,5},{1,7},{10,8},{12,10},{14... | collective-permute-start | bytes 393224 | tf_op jit(solution)/shard_map/while/body/eval_jaxpr/ppermute | solution.py:12
  418.9 15.0 %collective-permute-start.8 = (bf16[256,512]{1,0:T(8,128)(2,1)S(1)}, bf16[256,512]{1,0:T(8,128)(2,1)S(1)}, u32[]{:S(2)}, u32[]{:S(2)}) collective-permute-start(bf16[256,512]{1,0:T(8,128)(2,1)S(1)} %all-reduce.1), channel_id=1, source_target_pairs={{8,0},{16,8},{24,16},{0,24},{9,1},{17,9},{25,17},{1,25},{10,2},{18... | collective-permute-start | bytes 786440 | tf_op jit(solution)/shard_map/ppermute | solution.py:12
  429.6 7.4 %collective-permute-start = (bf16[256,256]{1,0:T(8,128)(2,1)S(1)}, bf16[256,256]{1,0:T(8,128)(2,1)S(1)}, u32[]{:S(2)}, u32[]{:S(2)}) collective-permute-start(bf16[256,256]{1,0:T(8,128)(2,1)S(1)} %all_gather.3), channel_id=1, source_target_pairs={{2,0},{4,2},{6,4},{0,6},{3,1},{5,3},{7,5},{1,7},{10,8},{12,10},{14... | collective-permute-start | bytes 393224 | tf_op jit(solution)/shard_map/ppermute | solution.py:12
  433.9 8.2 %collective-permute-start.9 = (bf16[256,512]{1,0:T(8,128)(2,1)S(1)}, bf16[256,512]{1,0:T(8,128)(2,1)S(1)}, u32[]{:S(2)}, u32[]{:S(2)}) collective-permute-start(bf16[256,512]{1,0:T(8,128)(2,1)S(1)} %broadcast_select_fusion), channel_id=1, source_target_pairs={{16,0},{24,8},{0,16},{8,24},{17,1},{25,9},{1,17},{9,25},{18,2},{26... | collective-permute-start | bytes 786440 | tf_op jit(solution)/shard_map/ppermute | solution.py:12
  437.0 8.7 %collective-permute-start.1 = (bf16[256,256]{1,0:T(8,128)(2,1)S(1)}, bf16[256,256]{1,0:T(8,128)(2,1)S(1)}, u32[]{:S(2)}, u32[]{:S(2)}) collective-permute-start(bf16[256,256]{1,0:T(8,128)(2,1)S(1)} %broadcast_select_fusion.5), channel_id=1, source_target_pairs={{4,0},{6,2},{0,4},{2,6},{5,1},{7,3},{1,5},{3,7},{12,8},{14,10},{8,... | collective-permute-start | bytes 393224 | tf_op jit(solution)/shard_map/ppermute | solution.py:12
  442.1 7.3 %collective-permute-start.11 = (bf16[256,512]{1,0:T(8,128)(2,1)S(1)}, bf16[256,512]{1,0:T(8,128)(2,1)S(1)}, u32[]{:S(2)}, u32[]{:S(2)}) collective-permute-start(bf16[256,512]{1,0:T(8,128)(2,1)S(1)} %broadcast_select_fusion.2), channel_id=1, source_target_pairs={{8,0},{16,8},{24,16},{0,24},{9,1},{17,9},{25,17},{1,25},{10,2},{18... | collective-permute-start | bytes 786440 | tf_op jit(solution)/shard_map/while/body/eval_jaxpr/ppermute | solution.py:12
  445.8 5.0 %collective-permute-start.10 = (bf16[256,256]{1,0:T(8,128)(2,1)S(1)}, bf16[256,256]{1,0:T(8,128)(2,1)S(1)}, u32[]{:S(2)}, u32[]{:S(2)}) collective-permute-start(bf16[256,256]{1,0:T(8,128)(2,1)S(1)} %broadcast_select_fusion.7), channel_id=1, source_target_pairs={{2,0},{4,2},{6,4},{0,6},{3,1},{5,3},{7,5},{1,7},{10,8},{12,10},{14... | collective-permute-start | bytes 393224 | tf_op jit(solution)/shard_map/while/body/eval_jaxpr/ppermute | solution.py:12
Sparse Core Ops, SparseCore 0:
  452.2 7.8 reduce-scatter.1
where the time goes:
time: 468 us; the launch traced here: 467 us
  local copies, waits for them, and re-layouts  157 us (34%)
  waiting for transfers between devices  120 us (26%)
  matrix products  80.7 us (17%)
  starting transfers between devices  76.6 us (16%)
  between operations  13.6 us (3%)
  other arithmetic  11.9 us (3%)
  blocking collectives  6.72 us (1%)
    ppermute x12, waiting for transfers between devices, shifted_2(): return lax.ppermute(block, axis, route)  112 us
    dot_general x8, matrix products, one_group(): jnp.einsum('pgi,pgj->pij', left_rows, right_rows, preferred_element_type=...  72.8 us
    gather x8, local copies, waits for them, and re-layouts, one_group(): left_rows = basis_values[pair_ids[0]]  65 us
    gather x8, local copies, waits for them, and re-layouts, one_group(): right_rows = weighted[pair_ids[1]]  64.9 us
    ppermute x12, starting transfers between devices, shifted_2(): return lax.ppermute(block, axis, route)  63.1 us
    scatter x1, local copies, waits for them, and re-layouts, local(): outgoing = jnp.zeros((devices * capacity, block_size, block_size), jnp.bf...  19.6 us
  transfers between devices with their start and end apart: 15, of which 10 were waited for; matrix products, arithmetic and copies ran while one was open for 53% of the time, Pallas kernels for 0%

commit v1 on v0

v1 whole, which is shorter than its diff:
```python
import functools

import jax
import jax.numpy as jnp
from jax import lax
from jax.experimental import pallas as pl
from jax.experimental.pallas import tpu as pltpu
from jax.sharding import PartitionSpec as P

UNROLL = 4
VMEM_LIMIT = 60 * 1024 * 1024


def target(i, s, n):
    return i ^ s if n & (n - 1) == 0 else (i + s) % n


def source(i, s, n):
    return i ^ s if n & (n - 1) == 0 else (i - s) % n


def target_slot(i, j, n):
    return i ^ j if n & (n - 1) == 0 else (j - i) % n


def source_slot(i, j, n):
    return i ^ j if n & (n - 1) == 0 else (i - j) % n


def exchange(value, axis, slot):
    n = lax.axis_size(axis)
    return lax.ppermute(value, axis, [(i, target(i, slot, n)) for i in range(n)])


def masked_blocks(matrix, block_mask, block_size):
    mask_rows, mask_cols = block_mask.shape
    shaped = matrix.reshape(mask_rows, block_size, mask_cols, block_size)
    factor = block_mask.astype(matrix.dtype)[:, None, :, None]
    return (shaped * factor).reshape(mask_rows * block_size, mask_cols * block_size)


def integrate_body(
    blocks, left_ref, right_ref, slot_ref, basis_ref, pot_ref, keep_ref, send_ref,
    basis, weighted, pot_cols, total, sems, pending, unit_left, unit_rights, unit_slots,
):
    atoms, points, size = basis.shape
    parts = left_ref.shape[0]

    def fetch(a):
        return pltpu.make_async_copy(basis_ref.at[a], basis.at[a], sems.at[a])

    for a in range(atoms):
        fetch(a).start()

    for a in range(atoms):
        pending[a] = -1

    def plan(n, count):
        a = left_ref[n]
        earlier = pending[a]
        fresh = earlier < 0
        pending[a] = jnp.where(fresh, n, -1)

        @pl.when(jnp.logical_not(fresh))
        def _():
            unit_left[count] = a
            unit_rights[2 * count] = right_ref[earlier]
            unit_rights[2 * count + 1] = right_ref[n]
            unit_slots[2 * count] = slot_ref[earlier]
            unit_slots[2 * count + 1] = slot_ref[n]

        return count + jnp.where(fresh, 0, 1)

    def plan_single(a, count):
        earlier = pending[a]

        @pl.when(earlier >= 0)
        def _():
            unit_left[count] = a
            unit_rights[2 * count] = right_ref[earlier]
            unit_rights[2 * count + 1] = right_ref[earlier]
            unit_slots[2 * count] = slot_ref[earlier]
            unit_slots[2 * count + 1] = blocks

        return count + jnp.where(earlier >= 0, 1, 0)

    count = lax.fori_loop(0, parts, plan, 0)
    count = lax.fori_loop(0, atoms, plan_single, count)
    for i in range(UNROLL - 1):
        unit_left[count + i] = 0
        for j in range(2):
            unit_rights[2 * (count + i) + j] = 0
            unit_slots[2 * (count + i) + j] = blocks

    for k in range(points // size):
        row = pot_ref[k : k + 1, :]
        pot_cols[k * size : (k + 1) * size, :] = jnp.broadcast_to(row, (size, size)).T

    def clear(i, carry):
        total[i] = jnp.zeros((size, size), jnp.float32)
        return carry

    lax.fori_loop(0, blocks + 1, clear, 0)

    def weigh(a, carry):
        fetch(a).wait()
        for k in range(points // size):
            at = slice(k * size, (k + 1) * size)
            weighted[a, at, :] = (basis[a, at, :].astype(jnp.float32) * pot_cols[at, :]).astype(jnp.bfloat16)
        return carry

    lax.fori_loop(0, atoms, weigh, 0)

    def step(i, carry):
        for j in range(UNROLL):
            u = i * UNROLL + j
            rights = jnp.concatenate([weighted[unit_rights[2 * u]], weighted[unit_rights[2 * u + 1]]], axis=1)
            found = lax.dot_general(
                basis[unit_left[u]], rights, (((0,), (0,)), ((), ())), preferred_element_type=jnp.float32
            )
            total[unit_slots[2 * u]] += found[:, :size]
            total[unit_slots[2 * u + 1]] += found[:, size:]
        return carry

    lax.fori_loop(0, (count + UNROLL - 1) // UNROLL, step, 0)
    half = blocks // 2

    def put(i, carry):
        keep_ref[i] = total[i].astype(jnp.bfloat16)
        send_ref[i] = total[half + i].astype(jnp.bfloat16)
        return carry

    lax.fori_loop(0, half, put, 0)


def integrate(basis_values, potential, left, right, slots, blocks):
    atoms, points, size = basis_values.shape
    parts = left.shape[0]
    most = (parts + atoms) // 2 + UNROLL + 1
    smem = pl.BlockSpec(memory_space=pltpu.SMEM)
    vmem = pl.BlockSpec(memory_space=pltpu.VMEM)
    half = jax.ShapeDtypeStruct((blocks // 2, size, size), jnp.bfloat16)
    return pl.pallas_call(
        functools.partial(integrate_body, blocks),
        out_shape=(half, half),
        in_specs=[smem, smem, smem, pl.BlockSpec(memory_space=pl.ANY), vmem],
        out_specs=(vmem, vmem),
        scratch_shapes=[
            pltpu.VMEM((atoms, points, size), jnp.bfloat16),
            pltpu.VMEM((atoms, points, size), jnp.bfloat16),
            pltpu.VMEM((points, size), jnp.float32),
            pltpu.VMEM((blocks + 1, size, size), jnp.float32),
            pltpu.SemaphoreType.DMA((atoms,)),
            pltpu.SMEM((atoms,), jnp.int32),
            pltpu.SMEM((most,), jnp.int32),
            pltpu.SMEM((2 * most,), jnp.int32),
            pltpu.SMEM((2 * most,), jnp.int32),
        ],
        compiler_params=pltpu.CompilerParams(vmem_limit_bytes=VMEM_LIMIT),
        cost_estimate=pl.CostEstimate(
            flops=2 * parts * points * size * size,
            bytes_accessed=2 * basis_values.size + 2 * blocks * size * size,
            transcendentals=0,
        ),
        name="integrate",
    )(left, right, slots, basis_values, potential.reshape(points // size, size))


def product_body(count, index_ref, *refs):
    lefts, rights, out = refs[:count], refs[count : 2 * count], refs[-2]
    stacked = refs[-1]
    for s in range(count):
        stacked[s] = rights[s][...]
    found = jnp.dot(lefts[0][...], stacked[index_ref[0]], preferred_element_type=jnp.float32)
    for s in range(1, count):
        found += jnp.dot(lefts[s][...], stacked[index_ref[s]], preferred_element_type=jnp.float32)
    out[...] = found.astype(out.dtype)


def product(lefts, rights, index, dtype):
    count = len(lefts)
    rows, columns = lefts[0].shape[0], rights[0].shape[1]
    vmem = pl.BlockSpec(memory_space=pltpu.VMEM)
    return pl.pallas_call(
        functools.partial(product_body, count),
        out_shape=jax.ShapeDtypeStruct((rows, columns), dtype),
        in_specs=[pl.BlockSpec(memory_space=pltpu.SMEM)] + [vmem] * (2 * count),
        out_specs=vmem,
        scratch_shapes=[pltpu.VMEM((count,) + rights[0].shape, rights[0].dtype)],
        cost_estimate=pl.CostEstimate(
            flops=2 * count * rows * columns * rights[0].shape[0],
            bytes_accessed=2 * count * (lefts[0].size + rights[0].size),
            transcendentals=0,
        ),
        name="product",
    )(index, *lefts, *rights)


def gradient_body(count, index_ref, side_ref, own_ref, other_ref, *refs):
    rights, out, stacked = refs[:count], refs[-2], refs[-1]
    for s in range(count):
        stacked[s] = rights[s][...]
    blocks, size = own_ref.shape[1], own_ref.shape[2]
    side = side_ref[0]
    for which, ref in ((side, own_ref), (1 - side, other_ref)):
        found = None
        for s in range(count):
            left = jnp.concatenate([ref[s, b] for b in range(blocks)], axis=1)
            term = jnp.dot(left, stacked[index_ref[s]], preferred_element_type=jnp.float32)
            found = term if found is None else found + term
        out[pl.ds(which * size, size), :] = found


def local(
    basis_values,
    potential,
    pair_atoms,
    target_device,
    target_block,
    density,
    density_mask,
    inverse_intersection,
    inverse_mask,
):
    size = basis_values.shape[2]
    rows, cols, layers = lax.axis_size("row"), lax.axis_size("col"), lax.axis_size("panel")
    row, col, layer = lax.axis_index("row"), lax.axis_index("col"), lax.axis_index("panel")
    tile_blocks = density_mask.shape[0]
    per_owner = tile_blocks // layers * tile_blocks
    blocks = layers * rows * cols * per_owner

    width = inverse_intersection.shape[1] // layers
    mask_width = inverse_mask.shape[1] // layers
    density_used = masked_blocks(density, density_mask, size)
    inverse_used = masked_blocks(
        lax.dynamic_slice_in_dim(inverse_intersection, layer * width, width, 1),
        lax.dynamic_slice_in_dim(inverse_mask, layer * mask_width, mask_width, 1),
        size,
    )
    lefts = [density_used] + [exchange(density_used, "col", s) for s in range(1, cols)]
    rights = [inverse_used] + [exchange(inverse_used, "row", s) for s in range(1, rows)]

    owner = target_device[:, 0]
    there_row, there_col, there_layer = owner // (cols * layers), (owner // layers) % cols, owner % layers
    slots = target_slot(layer, there_layer, layers) * rows + target_slot(row, there_row, rows)
    slots = (slots * cols + target_slot(col, there_col, cols)) * per_owner + target_block
    keep, send = integrate(basis_values, potential, pair_atoms[0], pair_atoms[1], slots, blocks)

    index = jnp.stack([source_slot(row, source(col, s, cols), rows) for s in range(cols)])
    panel_tile = product(lefts, rights, index, jnp.bfloat16)
    panels = [panel_tile] + [exchange(panel_tile, "row", s) for s in range(1, rows)]

    def added(*terms):
        return sum(t.astype(jnp.float32) for t in terms[1:]) + terms[0].astype(jnp.float32)

    got = exchange(send, "panel", 1)
    per_row = cols * per_owner
    parts = [
        added(keep[s * per_row : (s + 1) * per_row], got[s * per_row : (s + 1) * per_row]).astype(jnp.bfloat16)
        for s in range(rows)
    ]
    got = [exchange(parts[s], "row", s) for s in range(1, rows)]
    parts = [
        added(*[p[s * per_owner : (s + 1) * per_owner] for p in [parts[0]] + got]).astype(jnp.bfloat16)
        for s in range(cols)
    ]
    got = [exchange(parts[s], "col", s) for s in range(1, cols)]
    mine = added(parts[0], *got).astype(jnp.bfloat16)
    line = jnp.stack([mine] + [exchange(mine, "col", s) for s in range(1, cols)])
    other = exchange(line, "panel", 1)
    smem = pl.BlockSpec(memory_space=pltpu.SMEM)
    vmem = pl.BlockSpec(memory_space=pltpu.VMEM)
    return pl.pallas_call(
        functools.partial(gradient_body, cols),
        out_shape=jax.ShapeDtypeStruct((layers * size, width), jnp.float32),
        in_specs=[smem, smem] + [vmem] * (2 + cols),
        out_specs=vmem,
        scratch_shapes=[pltpu.VMEM((cols,) + panel_tile.shape, jnp.bfloat16)],
        name="gradient",
    )(index, layer[None], line, other, *panels)


def solution(mesh):
    placed = (
        P(("row", "col", "panel"), None, None),
        P(("row", "col", "panel")),
        P(None, ("row", "col", "panel")),
        P(("row", "col", "panel"), None),
        P(("row", "col", "panel")),
        P("row", "col"),
        P("row", "col"),
        P("row", "col"),
        P("row", "col"),
    )
    return jax.shard_map(
        local, mesh=mesh, in_specs=placed, out_specs=P("row", ("col", "panel")), check_vma=False
    )
```

time: 468 us -> 89.3 us (0.19)
  local copies, waits for them, and re-layouts: 157 us -> 3.03 us
  waiting for transfers between devices: 120 us -> 26.4 us
  matrix products: 80.7 us -> 0 us
  starting transfers between devices: 76.6 us -> 28.8 us
  Pallas kernels: 0 us -> 26.7 us
  between operations: 13.6 us -> 0.25 us
  other arithmetic: 11.9 us -> 3.77 us
  blocking collectives: 6.72 us -> 0 us
    gather x16 -> x0, local copies, waits for them, and re-layouts: 130 us -> none  [the longest x8 65 us: one_group(): left_rows = basis_values[pair_ids[0]]]
    ppermute x12 -> x20, waiting for transfers between devices: 112 us -> 26.4 us  [exchange(): lax.ppermute(value, axis, [(i, target(i, slot, n)) for i in range(n)])]
    dot_general x13 -> x0, matrix products: 80.7 us -> none  [the longest x8 72.8 us: one_group(): jnp.einsum('pgi,pgj->pij', left_rows, right_rows, preferred_element_type=...]
    ppermute x12 -> x20, starting transfers between devices: 63.1 us -> 28.8 us  [exchange(): lax.ppermute(value, axis, [(i, target(i, slot, n)) for i in range(n)])]
    pallas_call x0 -> x3, Pallas kernels: none -> 26.7 us  [the longest x1 22.1 us: integrate(): pl.pallas_call(functools.partial(integrate_body, blocks), out_shape=(half...]
    scatter x2 -> x0, local copies, waits for them, and re-layouts: 20.7 us -> none  [the longest x1 19.6 us: local(): outgoing = jnp.zeros((devices * capacity, block_size, block_size), jnp.bf...]
    all_to_all x2 -> x0, starting transfers between devices: 13.4 us -> none  [the longest x1 7.33 us: local(): lax.all_to_all(labels, ('row', 'col', 'panel'), split_axis=0, concat_axis...]
    reduce_scatter x1 -> x0, waiting for transfers between devices: 8.02 us -> none  [local(): lax.psum_scatter(gradient_part, 'panel', scatter_dimension=1, tiled=True)]
  transfers between devices with their start and end apart: 15 -> 20, of which waited for: 10 -> 13; matrix products, arithmetic and copies ran while one was open for 53% -> 1% of each run, Pallas kernels for 0% -> 3%
where the time goes in v1:
time: 89.3 us; the launch traced here: 89 us
  starting transfers between devices  28.8 us (32%)
  Pallas kernels  26.7 us (30%)
  waiting for transfers between devices  26.4 us (30%)
  other arithmetic  3.77 us (4%)
  local copies, waits for them, and re-layouts  3.03 us (3%)
    ppermute x20, starting transfers between devices, exchange(): lax.ppermute(value, axis, [(i, target(i, slot, n)) for i in range(n)])  28.8 us
    ppermute x20, waiting for transfers between devices, exchange(): lax.ppermute(value, axis, [(i, target(i, slot, n)) for i in range(n)])  26.4 us
    pallas_call x1, Pallas kernels, integrate(): pl.pallas_call(functools.partial(integrate_body, blocks), out_shape=(half...  22.1 us
    pallas_call x1, Pallas kernels, product(): pl.pallas_call(functools.partial(product_body, count), out_shape=jax.Shap...  2.29 us
    pallas_call x1, Pallas kernels, local(): pl.pallas_call(functools.partial(gradient_body, cols), out_shape=jax.Shap...  2.26 us
  transfers between devices with their start and end apart: 20, of which 13 were waited for; matrix products, arithmetic and copies ran while one was open for 1% of the time, Pallas kernels for 3%

profile of v1, /device:TPU:0, one launch (start us, length us, event | category | flops | bytes accessed | tf_op | source)
XLA Modules:
  0.0 89.0 jit_solution(16057209457762388590)
XLA Ops:
  0.0 1.3 %slice_bitcast_fusion = (s32[128]{0:T(128)}, s32[128]{0:T(128)}) fusion(s32[2,128]{1,0:T(2,128)} %param.11), kind=kLoop, calls=%fused_computation.34 | loop fusion | bytes 2048 | tf_op jit(solution)/shard_map/squeeze | solution.py:247
  1.3 1.2 %multiply_add_fusion.slot_ref = s32[128]{0:T(128)} fusion(s32[128]{0:T(128)} %param.13, s32[128,1]{0,1:T(1,128)} %param.12, s32[]{:T(128)S(6)} %axis_index.36, s32[]{:T(128)S(6)} %axis_index.33, s32[]{:T(128)} %axis_index.38), kind=kLoop, calls=%fused_computation.33 | loop fusion | flops 6272 | bytes 1548 | tf_op jit(solution)/shard_map/add | solution.py:246
  2.6 22.1 %integrate.1 = (bf16[32,128,128]{2,1,0:T(8,128)(2,1)}, bf16[32,128,128]{2,1,0:T(8,128)(2,1)}) custom-call(s32[128]{0:T(128)} %get-tuple-element.17.left_ref, s32[128]{0:T(128)} %get-tuple-element.16.right_ref, s32[128]{0:T(128)} %multiply_add_fusion.slot_ref, bf16[16,2048,128]{2,1,0:T(8,128)(2,1)} %basis_ref.1, f32[16,128]{1,0:T(8,128)} %bitcast.40), custom_call_target="tpu_custom_call" | custom-call | flops 8589934592 | bytes 10485760 | tf_op jit(solution)/shard_map/integrate/pallas_call | solution.py:143
  25.2 2.5 %collective-permute-done = bf16[32,128,128]{2,1,0:T(8,128)(2,1)S(1)} collective-permute-done((bf16[32,128,128]{2,1,0:T(8,128)(2,1)}, bf16[32,128,128]{2,1,0:T(8,128)(2,1)S(1)}, u32[]{:S(2)}, u32[]{:S(2)}) %collective-permute-start) | collective-permute-done | bytes 1048608 | tf_op jit(solution)/shard_map/ppermute | solution.py:32
  27.7 1.5 %add_convert_fusion.3 = (bf16[8,128,128]{2,1,0:T(8,128)(2,1)S(1)}, bf16[8,128,128]{2,1,0:T(8,128)(2,1)S(1)}, bf16[8,128,128]{2,1,0:T(8,128)(2,1)S(1)}, bf16[8,128,128]{2,1,0:T(8,128)(2,1)S(1)}) fusion(bf16[32,128,128]{2,1,0:T(8,128)(2,1)S(1)} %collective-permute-done, bf16[32,128,128]{2,1,0:T(8,128)(2,1)} %get-tuple-element.8), kind=kLoop, calls=%fused_computation.3 | loop fusion | flops 2097152 | bytes 3145728 | tf_op jit(solution)/shard_map/convert_element_type | solution.py:259
  29.3 3.9 %collective-permute-start.3 = (bf16[8,128,128]{2,1,0:T(8,128)(2,1)S(1)}, bf16[8,128,128]{2,1,0:T(8,128)(2,1)S(1)}, u32[]{:S(2)}, u32[]{:S(2)}) collective-permute-start(bf16[8,128,128]{2,1,0:T(8,128)(2,1)S(1)} %get-tuple-element.11), channel_id=1, source_target_pairs={{0,24},{8,16},{16,8},{24,0},{1,25},{9,17},{17,9},{25,1},{2,26},{10... | collective-permute-start | bytes 786440 | tf_op jit(solution)/shard_map/ppermute | solution.py:32
  33.2 1.4 %collective-permute-start.2 = (bf16[8,128,128]{2,1,0:T(8,128)(2,1)S(1)}, bf16[8,128,128]{2,1,0:T(8,128)(2,1)S(1)}, u32[]{:S(2)}, u32[]{:S(2)}) collective-permute-start(bf16[8,128,128]{2,1,0:T(8,128)(2,1)S(1)} %get-tuple-element.12), channel_id=1, source_target_pairs={{0,16},{8,24},{16,0},{24,8},{1,17},{9,25},{17,1},{25,9},{2,18},{10... | collective-permute-start | bytes 786440 | tf_op jit(solution)/shard_map/ppermute | solution.py:32
  34.7 2.2 %collective-permute-start.11 = (bf16[256,256]{1,0:T(8,128)(2,1)S(1)}, bf16[256,256]{1,0:T(8,128)(2,1)S(1)}, u32[]{:S(2)}, u32[]{:S(2)}) collective-permute-start(bf16[256,256]{1,0:T(8,128)(2,1)S(1)} %bitcast_multiply_fusion.1.refs_0_), channel_id=1, source_target_pairs={{0,2},{2,0},{4,6},{6,4},{1,3},{3,1},{5,7},{7,5},{8,10},{10,8},{12,... | collective-permute-start | bytes 393224 | tf_op jit(solution)/shard_map/ppermute | solution.py:32
  36.9 1.7 %collective-permute-start.12 = (bf16[256,256]{1,0:T(8,128)(2,1)S(1)}, bf16[256,256]{1,0:T(8,128)(2,1)S(1)}, u32[]{:S(2)}, u32[]{:S(2)}) collective-permute-start(bf16[256,256]{1,0:T(8,128)(2,1)S(1)} %bitcast_multiply_fusion.1.refs_0_), channel_id=1, source_target_pairs={{0,4},{2,6},{4,0},{6,2},{1,5},{3,7},{5,1},{7,3},{8,12},{10,14},{12... | collective-permute-start | bytes 393224 | tf_op jit(solution)/shard_map/ppermute | solution.py:32
  38.6 1.7 %collective-permute-done.3 = bf16[8,128,128]{2,1,0:T(8,128)(2,1)S(1)} collective-permute-done((bf16[8,128,128]{2,1,0:T(8,128)(2,1)S(1)}, bf16[8,128,128]{2,1,0:T(8,128)(2,1)S(1)}, u32[]{:S(2)}, u32[]{:S(2)}) %collective-permute-start.3) | collective-permute-done | bytes 262176 | tf_op jit(solution)/shard_map/ppermute | solution.py:32
  40.4 5.0 %collective-permute-done.2 = bf16[8,128,128]{2,1,0:T(8,128)(2,1)S(1)} collective-permute-done((bf16[8,128,128]{2,1,0:T(8,128)(2,1)S(1)}, bf16[8,128,128]{2,1,0:T(8,128)(2,1)S(1)}, u32[]{:S(2)}, u32[]{:S(2)}) %collective-permute-start.2) | collective-permute-done | bytes 262176 | tf_op jit(solution)/shard_map/ppermute | solution.py:32
  45.8 4.2 %collective-permute-start.6 = (bf16[2,128,128]{2,1,0:T(8,128)(2,1)S(1)}, bf16[2,128,128]{2,1,0:T(8,128)(2,1)S(1)}, u32[]{:S(2)}, u32[]{:S(2)}) collective-permute-start(bf16[2,128,128]{2,1,0:T(8,128)(2,1)S(1)} %get-tuple-element.14), channel_id=1, source_target_pairs={{0,6},{2,4},{4,2},{6,0},{1,7},{3,5},{5,3},{7,1},{8,14},{10,12},{12... | collective-permute-start | bytes 196616 | tf_op jit(solution)/shard_map/ppermute | solution.py:32
  50.0 0.6 collective-permute-start.4
  50.7 2.2 %collective-permute-done.6 = bf16[2,128,128]{2,1,0:T(8,128)(2,1)S(1)} collective-permute-done((bf16[2,128,128]{2,1,0:T(8,128)(2,1)S(1)}, bf16[2,128,128]{2,1,0:T(8,128)(2,1)S(1)}, u32[]{:S(2)}, u32[]{:S(2)}) %collective-permute-start.6) | collective-permute-done | bytes 65568 | tf_op jit(solution)/shard_map/ppermute | solution.py:32
  53.0 2.9 %collective-permute-done.5 = bf16[2,128,128]{2,1,0:T(8,128)(2,1)S(1)} collective-permute-done((bf16[2,128,128]{2,1,0:T(8,128)(2,1)S(1)}, bf16[2,128,128]{2,1,0:T(8,128)(2,1)S(1)}, u32[]{:S(2)}, u32[]{:S(2)}) %collective-permute-start.5) | collective-permute-done | bytes 65568 | tf_op jit(solution)/shard_map/ppermute | solution.py:32
  55.9 2.0 %collective-permute-start.9 = (bf16[2,128,128]{2,1,0:T(8,128)(2,1)S(1)}, bf16[2,128,128]{2,1,0:T(8,128)(2,1)S(1)}, u32[]{:S(2)}, u32[]{:S(2)}) collective-permute-start(bf16[2,128,128]{2,1,0:T(8,128)(2,1)S(1)} %add_convert_fusion.4), channel_id=1, source_target_pairs={{0,6},{2,4},{4,2},{6,0},{1,7},{3,5},{5,3},{7,1},{8,14},{10,12},{12... | collective-permute-start | bytes 196616 | tf_op jit(solution)/shard_map/ppermute | solution.py:32
  58.0 2.4 %collective-permute-start.7 = (bf16[2,128,128]{2,1,0:T(8,128)(2,1)S(1)}, bf16[2,128,128]{2,1,0:T(8,128)(2,1)S(1)}, u32[]{:S(2)}, u32[]{:S(2)}) collective-permute-start(bf16[2,128,128]{2,1,0:T(8,128)(2,1)S(1)} %add_convert_fusion.4), channel_id=1, source_target_pairs={{0,2},{2,0},{4,6},{6,4},{1,3},{3,1},{5,7},{7,5},{8,10},{10,8},{12,... | collective-permute-start | bytes 196616 | tf_op jit(solution)/shard_map/ppermute | solution.py:32
  60.6 2.0 %collective-permute-start.13 = (bf16[256,256]{1,0:T(8,128)(2,1)S(1)}, bf16[256,256]{1,0:T(8,128)(2,1)S(1)}, u32[]{:S(2)}, u32[]{:S(2)}) collective-permute-start(bf16[256,256]{1,0:T(8,128)(2,1)S(1)} %bitcast_multiply_fusion.1.refs_0_), channel_id=1, source_target_pairs={{0,6},{2,4},{4,2},{6,0},{1,7},{3,5},{5,3},{7,1},{8,14},{10,12},{12... | collective-permute-start | bytes 393224 | tf_op jit(solution)/shard_map/ppermute | solution.py:32
  62.8 1.4 %collective-permute-start.14 = (bf16[256,256]{1,0:T(8,128)(2,1)S(1)}, bf16[256,256]{1,0:T(8,128)(2,1)S(1)}, u32[]{:S(2)}, u32[]{:S(2)}) collective-permute-start(bf16[256,256]{1,0:T(8,128)(2,1)S(1)} %bitcast_multiply_fusion.refs_4_), channel_id=1, source_target_pairs={{0,8},{8,0},{16,24},{24,16},{1,9},{9,1},{17,25},{25,17},{2,10},{10... | collective-permute-start | bytes 393224 | tf_op jit(solution)/shard_map/ppermute | solution.py:32
  64.1 3.4 %collective-permute-done.8 = bf16[2,128,128]{2,1,0:T(8,128)(2,1)S(1)} collective-permute-done((bf16[2,128,128]{2,1,0:T(8,128)(2,1)S(1)}, bf16[2,128,128]{2,1,0:T(8,128)(2,1)S(1)}, u32[]{:S(2)}, u32[]{:S(2)}) %collective-permute-start.8) | collective-permute-done | bytes 65568 | tf_op jit(solution)/shard_map/ppermute | solution.py:32
  67.6 1.6 %collective-permute-start.15 = (bf16[256,256]{1,0:T(8,128)(2,1)S(1)}, bf16[256,256]{1,0:T(8,128)(2,1)S(1)}, u32[]{:S(2)}, u32[]{:S(2)}) collective-permute-start(bf16[256,256]{1,0:T(8,128)(2,1)S(1)} %bitcast_multiply_fusion.refs_4_), channel_id=1, source_target_pairs={{0,16},{8,24},{16,0},{24,8},{1,17},{9,25},{17,1},{25,9},{2,18},{10... | collective-permute-start | bytes 393224 | tf_op jit(solution)/shard_map/ppermute | solution.py:32
  69.2 1.3 %collective-permute-start.16 = (bf16[256,256]{1,0:T(8,128)(2,1)S(1)}, bf16[256,256]{1,0:T(8,128)(2,1)S(1)}, u32[]{:S(2)}, u32[]{:S(2)}) collective-permute-start(bf16[256,256]{1,0:T(8,128)(2,1)S(1)} %bitcast_multiply_fusion.refs_4_), channel_id=1, source_target_pairs={{0,24},{8,16},{16,8},{24,0},{1,25},{9,17},{17,9},{25,1},{2,26},{10... | collective-permute-start | bytes 393224 | tf_op jit(solution)/shard_map/ppermute | solution.py:32
  70.6 0.7 pad_add_fusion.index_ref
  71.3 1.3 %collective-permute-done.15.refs_6_ = bf16[256,256]{1,0:T(8,128)(2,1)S(1)} collective-permute-done((bf16[256,256]{1,0:T(8,128)(2,1)S(1)}, bf16[256,256]{1,0:T(8,128)(2,1)S(1)}, u32[]{:S(2)}, u32[]{:S(2)}) %collective-permute-start.15) | collective-permute-done | bytes 131104 | tf_op jit(solution)/shard_map/ppermute | solution.py:32
  72.5 2.5 %collective-permute-done.16.refs_7_ = bf16[256,256]{1,0:T(8,128)(2,1)S(1)} collective-permute-done((bf16[256,256]{1,0:T(8,128)(2,1)S(1)}, bf16[256,256]{1,0:T(8,128)(2,1)S(1)}, u32[]{:S(2)}, u32[]{:S(2)}) %collective-permute-start.16) | collective-permute-done | bytes 131104 | tf_op jit(solution)/shard_map/ppermute | solution.py:32
  75.7 2.3 %product.1.refs_0_ = bf16[256,256]{1,0:T(8,128)(2,1)} custom-call(s32[4]{0:T(128)} %pad_add_fusion.index_ref, bf16[256,256]{1,0:T(8,128)(2,1)} %copy-done.1, bf16[256,256]{1,0:T(8,128)(2,1)} %copy-done.5, bf16[256,256]{1,0:T(8,128)(2,1)} %copy-done.6, bf16[256,256]{1,0:T(8,128)(2,1)} %copy-done.7, bf16[256,256]{1,0:T(8,128)(2,1)} %copy-done.2, ...), custom_call_target="tpu_custom_call" | custom-call | flops 134217728 | bytes 1048576 | tf_op jit(solution)/shard_map/product/pallas_call | solution.py:184
  78.6 1.3 %collective-permute-start.18 = (bf16[256,256]{1,0:T(8,128)(2,1)}, bf16[256,256]{1,0:T(8,128)(2,1)S(1)}, u32[]{:S(2)}, u32[]{:S(2)}) collective-permute-start(bf16[256,256]{1,0:T(8,128)(2,1)} %product.1.refs_0_), channel_id=1, source_target_pairs={{0,16},{8,24},{16,0},{24,8},{1,17},{9,25},{17,1},{25,9},{2,18},{10... | collective-permute-start | bytes 393224 | tf_op jit(solution)/shard_map/ppermute | solution.py:32
  79.9 1.6 %collective-permute-start.19 = (bf16[256,256]{1,0:T(8,128)(2,1)}, bf16[256,256]{1,0:T(8,128)(2,1)S(1)}, u32[]{:S(2)}, u32[]{:S(2)}) collective-permute-start(bf16[256,256]{1,0:T(8,128)(2,1)} %product.1.refs_0_), channel_id=1, source_target_pairs={{0,24},{8,16},{16,8},{24,0},{1,25},{9,17},{17,9},{25,1},{2,26},{10... | collective-permute-start | bytes 393224 | tf_op jit(solution)/shard_map/ppermute | solution.py:32
  81.5 1.7 %collective-permute-done.17.refs_1_ = bf16[256,256]{1,0:T(8,128)(2,1)S(1)} collective-permute-done((bf16[256,256]{1,0:T(8,128)(2,1)}, bf16[256,256]{1,0:T(8,128)(2,1)S(1)}, u32[]{:S(2)}, u32[]{:S(2)}) %collective-permute-start.17) | collective-permute-done | bytes 131104 | tf_op jit(solution)/shard_map/ppermute | solution.py:32
  83.2 0.7 collective-permute-done.18.refs_2_
  83.9 2.0 %collective-permute-done.19.refs_3_ = bf16[256,256]{1,0:T(8,128)(2,1)S(1)} collective-permute-done((bf16[256,256]{1,0:T(8,128)(2,1)}, bf16[256,256]{1,0:T(8,128)(2,1)S(1)}, u32[]{:S(2)}, u32[]{:S(2)}) %collective-permute-start.19) | collective-permute-done | bytes 131104 | tf_op jit(solution)/shard_map/ppermute | solution.py:32
  86.7 2.3 %gradient.1 = f32[256,256]{1,0:T(8,128)} custom-call(s32[4]{0:T(128)} %pad_add_fusion.index_ref, s32[1]{0:T(128)} %bitcast.4.side_ref, bf16[4,2,128,128]{3,2,1,0:T(8,128)(2,1)} %copy-done, bf16[4,2,128,128]{3,2,1,0:T(8,128)(2,1)} %copy-done.3, bf16[256,256]{1,0:T(8,128)(2,1)} %product.1.refs_0_, bf16[256,256]{1,0:T(8,128)(2,1)} %copy-done.11, ...), custom_call_target="tpu_custom_call" | custom-call | tf_op jit(solution)/shard_map/gradient/pallas_call | solution.py:273
  (58 shorter events, 3.7 us)
Async XLA Ops:
  2.6 32.0 %copy-start.16 = (s32[2,2]{1,0:T(2,128)S(1)}, s32[2,2]{1,0:T(2,128)}, u32[]{:S(2)}) copy-start(s32[2,2]{1,0:T(2,128)} %param.15) | copy-start | bytes 52
  2.6 32.1 %copy-start.4 = (bf16[256,256]{1,0:T(8,128)(2,1)S(1)}, bf16[256,256]{1,0:T(8,128)(2,1)}, u32[]{:S(2)}) copy-start(bf16[256,256]{1,0:T(8,128)(2,1)} %param.14) | copy-start | bytes 393220
  2.6 48.1 %copy-start.15 = (s32[2,4]{1,0:T(2,128)S(1)}, s32[2,4]{1,0:T(2,128)}, u32[]{:S(2)}) copy-start(s32[2,4]{1,0:T(2,128)} %param.17) | copy-start | bytes 100
  2.6 58.0 %copy-start.14 = (bf16[256,512]{1,0:T(8,128)(2,1)S(1)}, bf16[256,512]{1,0:T(8,128)(2,1)}, u32[]{:S(2)}) copy-start(bf16[256,512]{1,0:T(8,128)(2,1)} %param.16) | copy-start | bytes 786436
  24.7 3.1 %collective-permute-start = (bf16[32,128,128]{2,1,0:T(8,128)(2,1)}, bf16[32,128,128]{2,1,0:T(8,128)(2,1)S(1)}, u32[]{:S(2)}, u32[]{:S(2)}) collective-permute-start(bf16[32,128,128]{2,1,0:T(8,128)(2,1)} %get-tuple-element.7), channel_id=1, source_target_pairs={{0,1},{1,0},{2,3},{3,2},{4,5},{5,4},{6,7},{7,6},{8,9},{9,8},{10,11... | collective-permute-start | bytes 3145736 | tf_op jit(solution)/shard_map/ppermute | solution.py:32
  29.3 11.1 %collective-permute-start.3 = (bf16[8,128,128]{2,1,0:T(8,128)(2,1)S(1)}, bf16[8,128,128]{2,1,0:T(8,128)(2,1)S(1)}, u32[]{:S(2)}, u32[]{:S(2)}) collective-permute-start(bf16[8,128,128]{2,1,0:T(8,128)(2,1)S(1)} %get-tuple-element.11), channel_id=1, source_target_pairs={{0,24},{8,16},{16,8},{24,0},{1,25},{9,17},{17,9},{25,1},{2,26},{10... | collective-permute-start | bytes 786440 | tf_op jit(solution)/shard_map/ppermute | solution.py:32
  33.2 12.2 %collective-permute-start.2 = (bf16[8,128,128]{2,1,0:T(8,128)(2,1)S(1)}, bf16[8,128,128]{2,1,0:T(8,128)(2,1)S(1)}, u32[]{:S(2)}, u32[]{:S(2)}) collective-permute-start(bf16[8,128,128]{2,1,0:T(8,128)(2,1)S(1)} %get-tuple-element.12), channel_id=1, source_target_pairs={{0,16},{8,24},{16,0},{24,8},{1,17},{9,25},{17,1},{25,9},{2,18},{10... | collective-permute-start | bytes 786440 | tf_op jit(solution)/shard_map/ppermute | solution.py:32
  34.5 11.1 %collective-permute-start.1 = (bf16[8,128,128]{2,1,0:T(8,128)(2,1)S(1)}, bf16[8,128,128]{2,1,0:T(8,128)(2,1)S(1)}, u32[]{:S(2)}, u32[]{:S(2)}) collective-permute-start(bf16[8,128,128]{2,1,0:T(8,128)(2,1)S(1)} %get-tuple-element.9), channel_id=1, source_target_pairs={{0,8},{8,0},{16,24},{24,16},{1,9},{9,1},{17,25},{25,17},{2,10},{10... | collective-permute-start | bytes 786440 | tf_op jit(solution)/shard_map/ppermute | solution.py:32
  34.7 40.3 %copy-start.1 = (bf16[256,256]{1,0:T(8,128)(2,1)}, bf16[256,256]{1,0:T(8,128)(2,1)S(1)}, u32[]{:S(2)}) copy-start(bf16[256,256]{1,0:T(8,128)(2,1)S(1)} %bitcast_multiply_fusion.1.refs_0_) | copy-start | bytes 393220
  34.7 25.9 %collective-permute-start.11 = (bf16[256,256]{1,0:T(8,128)(2,1)S(1)}, bf16[256,256]{1,0:T(8,128)(2,1)S(1)}, u32[]{:S(2)}, u32[]{:S(2)}) collective-permute-start(bf16[256,256]{1,0:T(8,128)(2,1)S(1)} %bitcast_multiply_fusion.1.refs_0_), channel_id=1, source_target_pairs={{0,2},{2,0},{4,6},{6,4},{1,3},{3,1},{5,7},{7,5},{8,10},{10,8},{12,... | collective-permute-start | bytes 393224 | tf_op jit(solution)/shard_map/ppermute | solution.py:32
  36.9 33.6 %collective-permute-start.12 = (bf16[256,256]{1,0:T(8,128)(2,1)S(1)}, bf16[256,256]{1,0:T(8,128)(2,1)S(1)}, u32[]{:S(2)}, u32[]{:S(2)}) collective-permute-start(bf16[256,256]{1,0:T(8,128)(2,1)S(1)} %bitcast_multiply_fusion.1.refs_0_), channel_id=1, source_target_pairs={{0,4},{2,6},{4,0},{6,2},{1,5},{3,7},{5,1},{7,3},{8,12},{10,14},{12... | collective-permute-start | bytes 393224 | tf_op jit(solution)/shard_map/ppermute | solution.py:32
  45.8 7.2 %collective-permute-start.6 = (bf16[2,128,128]{2,1,0:T(8,128)(2,1)S(1)}, bf16[2,128,128]{2,1,0:T(8,128)(2,1)S(1)}, u32[]{:S(2)}, u32[]{:S(2)}) collective-permute-start(bf16[2,128,128]{2,1,0:T(8,128)(2,1)S(1)} %get-tuple-element.14), channel_id=1, source_target_pairs={{0,6},{2,4},{4,2},{6,0},{1,7},{3,5},{5,3},{7,1},{8,14},{10,12},{12... | collective-permute-start | bytes 196616 | tf_op jit(solution)/shard_map/ppermute | solution.py:32
  50.0 5.8 %collective-permute-start.5 = (bf16[2,128,128]{2,1,0:T(8,128)(2,1)S(1)}, bf16[2,128,128]{2,1,0:T(8,128)(2,1)S(1)}, u32[]{:S(2)}, u32[]{:S(2)}) collective-permute-start(bf16[2,128,128]{2,1,0:T(8,128)(2,1)S(1)} %get-tuple-element.15), channel_id=1, source_target_pairs={{0,4},{2,6},{4,0},{6,2},{1,5},{3,7},{5,1},{7,3},{8,12},{10,14},{12... | collective-permute-start | bytes 196616 | tf_op jit(solution)/shard_map/ppermute | solution.py:32
  50.0 5.8 %collective-permute-start.4 = (bf16[2,128,128]{2,1,0:T(8,128)(2,1)S(1)}, bf16[2,128,128]{2,1,0:T(8,128)(2,1)S(1)}, u32[]{:S(2)}, u32[]{:S(2)}) collective-permute-start(bf16[2,128,128]{2,1,0:T(8,128)(2,1)S(1)} %get-tuple-element.13), channel_id=1, source_target_pairs={{0,2},{2,0},{4,6},{6,4},{1,3},{3,1},{5,7},{7,5},{8,10},{10,8},{12,... | collective-permute-start | bytes 196616 | tf_op jit(solution)/shard_map/ppermute | solution.py:32
  55.9 6.8 %collective-permute-start.9 = (bf16[2,128,128]{2,1,0:T(8,128)(2,1)S(1)}, bf16[2,128,128]{2,1,0:T(8,128)(2,1)S(1)}, u32[]{:S(2)}, u32[]{:S(2)}) collective-permute-start(bf16[2,128,128]{2,1,0:T(8,128)(2,1)S(1)} %add_convert_fusion.4), channel_id=1, source_target_pairs={{0,6},{2,4},{4,2},{6,0},{1,7},{3,5},{5,3},{7,1},{8,14},{10,12},{12... | collective-permute-start | bytes 196616 | tf_op jit(solution)/shard_map/ppermute | solution.py:32
  58.0 9.6 %collective-permute-start.8 = (bf16[2,128,128]{2,1,0:T(8,128)(2,1)S(1)}, bf16[2,128,128]{2,1,0:T(8,128)(2,1)S(1)}, u32[]{:S(2)}, u32[]{:S(2)}) collective-permute-start(bf16[2,128,128]{2,1,0:T(8,128)(2,1)S(1)} %add_convert_fusion.4), channel_id=1, source_target_pairs={{0,4},{2,6},{4,0},{6,2},{1,5},{3,7},{5,1},{7,3},{8,12},{10,14},{12... | collective-permute-start | bytes 196616 | tf_op jit(solution)/shard_map/ppermute | solution.py:32
  58.0 11.2 %collective-permute-start.7 = (bf16[2,128,128]{2,1,0:T(8,128)(2,1)S(1)}, bf16[2,128,128]{2,1,0:T(8,128)(2,1)S(1)}, u32[]{:S(2)}, u32[]{:S(2)}) collective-permute-start(bf16[2,128,128]{2,1,0:T(8,128)(2,1)S(1)} %add_convert_fusion.4), channel_id=1, source_target_pairs={{0,2},{2,0},{4,6},{6,4},{1,3},{3,1},{5,7},{7,5},{8,10},{10,8},{12,... | collective-permute-start | bytes 196616 | tf_op jit(solution)/shard_map/ppermute | solution.py:32
  60.6 14.4 %copy-start.2 = (bf16[256,256]{1,0:T(8,128)(2,1)}, bf16[256,256]{1,0:T(8,128)(2,1)S(1)}, u32[]{:S(2)}) copy-start(bf16[256,256]{1,0:T(8,128)(2,1)S(1)} %bitcast_multiply_fusion.refs_4_) | copy-start | bytes 393220
  60.6 14.4 %copy-start.5 = (bf16[256,256]{1,0:T(8,128)(2,1)}, bf16[256,256]{1,0:T(8,128)(2,1)S(1)}, u32[]{:S(2)}) copy-start(bf16[256,256]{1,0:T(8,128)(2,1)S(1)} %collective-permute-done.11.refs_1_) | copy-start | bytes 393220
  60.6 10.6 %collective-permute-start.13 = (bf16[256,256]{1,0:T(8,128)(2,1)S(1)}, bf16[256,256]{1,0:T(8,128)(2,1)S(1)}, u32[]{:S(2)}, u32[]{:S(2)}) collective-permute-start(bf16[256,256]{1,0:T(8,128)(2,1)S(1)} %bitcast_multiply_fusion.1.refs_0_), channel_id=1, source_target_pairs={{0,6},{2,4},{4,2},{6,0},{1,7},{3,5},{5,3},{7,1},{8,14},{10,12},{12... | collective-permute-start | bytes 393224 | tf_op jit(solution)/shard_map/ppermute | solution.py:32
  62.8 8.5 %collective-permute-start.14 = (bf16[256,256]{1,0:T(8,128)(2,1)S(1)}, bf16[256,256]{1,0:T(8,128)(2,1)S(1)}, u32[]{:S(2)}, u32[]{:S(2)}) collective-permute-start(bf16[256,256]{1,0:T(8,128)(2,1)S(1)} %bitcast_multiply_fusion.refs_4_), channel_id=1, source_target_pairs={{0,8},{8,0},{16,24},{24,16},{1,9},{9,1},{17,25},{25,17},{2,10},{10... | collective-permute-start | bytes 393224 | tf_op jit(solution)/shard_map/ppermute | solution.py:32
  67.6 5.0 %collective-permute-start.15 = (bf16[256,256]{1,0:T(8,128)(2,1)S(1)}, bf16[256,256]{1,0:T(8,128)(2,1)S(1)}, u32[]{:S(2)}, u32[]{:S(2)}) collective-permute-start(bf16[256,256]{1,0:T(8,128)(2,1)S(1)} %bitcast_multiply_fusion.refs_4_), channel_id=1, source_target_pairs={{0,16},{8,24},{16,0},{24,8},{1,17},{9,25},{17,1},{25,9},{2,18},{10... | collective-permute-start | bytes 393224 | tf_op jit(solution)/shard_map/ppermute | solution.py:32
  69.2 5.9 %collective-permute-start.16 = (bf16[256,256]{1,0:T(8,128)(2,1)S(1)}, bf16[256,256]{1,0:T(8,128)(2,1)S(1)}, u32[]{:S(2)}, u32[]{:S(2)}) collective-permute-start(bf16[256,256]{1,0:T(8,128)(2,1)S(1)} %bitcast_multiply_fusion.refs_4_), channel_id=1, source_target_pairs={{0,24},{8,16},{16,8},{24,0},{1,25},{9,17},{17,9},{25,1},{2,26},{10... | collective-permute-start | bytes 393224 | tf_op jit(solution)/shard_map/ppermute | solution.py:32
  70.5 15.5 %copy-start = (bf16[4,2,128,128]{3,2,1,0:T(8,128)(2,1)}, bf16[4,2,128,128]{3,2,1,0:T(8,128)(2,1)S(1)}, u32[]{:S(2)}) copy-start(bf16[4,2,128,128]{3,2,1,0:T(8,128)(2,1)S(1)} %pad_maximum_fusion.own_ref) | copy-start | bytes 786436
  70.5 4.5 %copy-start.6 = (bf16[256,256]{1,0:T(8,128)(2,1)}, bf16[256,256]{1,0:T(8,128)(2,1)S(1)}, u32[]{:S(2)}) copy-start(bf16[256,256]{1,0:T(8,128)(2,1)S(1)} %collective-permute-done.12.refs_2_) | copy-start | bytes 393220
  70.5 15.4 %collective-permute-start.10 = (bf16[4,2,128,128]{3,2,1,0:T(8,128)(2,1)S(1)}, bf16[4,2,128,128]{3,2,1,0:T(8,128)(2,1)S(1)}, u32[]{:S(2)}, u32[]{:S(2)}) collective-permute-start(bf16[4,2,128,128]{3,2,1,0:T(8,128)(2,1)S(1)} %pad_maximum_fusion.own_ref), channel_id=1, source_target_pairs={{0,1},{1,0},{2,3},{3,2},{4,5},{5,4},{6,7},{7,6},{8,9},{9,8},{10,11... | collective-permute-start | bytes 786440 | tf_op jit(solution)/shard_map/ppermute | solution.py:32
  71.3 3.8 %copy-start.7 = (bf16[256,256]{1,0:T(8,128)(2,1)}, bf16[256,256]{1,0:T(8,128)(2,1)S(1)}, u32[]{:S(2)}) copy-start(bf16[256,256]{1,0:T(8,128)(2,1)S(1)} %collective-permute-done.13.refs_3_) | copy-start | bytes 393220
  71.3 3.8 %copy-start.8 = (bf16[256,256]{1,0:T(8,128)(2,1)}, bf16[256,256]{1,0:T(8,128)(2,1)S(1)}, u32[]{:S(2)}) copy-start(bf16[256,256]{1,0:T(8,128)(2,1)S(1)} %collective-permute-done.14.refs_5_) | copy-start | bytes 393220
  78.0 5.2 %collective-permute-start.17 = (bf16[256,256]{1,0:T(8,128)(2,1)}, bf16[256,256]{1,0:T(8,128)(2,1)S(1)}, u32[]{:S(2)}, u32[]{:S(2)}) collective-permute-start(bf16[256,256]{1,0:T(8,128)(2,1)} %product.1.refs_0_), channel_id=1, source_target_pairs={{0,8},{8,0},{16,24},{24,16},{1,9},{9,1},{17,25},{25,17},{2,10},{10... | collective-permute-start | bytes 393224 | tf_op jit(solution)/shard_map/ppermute | solution.py:32
  78.6 5.3 %collective-permute-start.18 = (bf16[256,256]{1,0:T(8,128)(2,1)}, bf16[256,256]{1,0:T(8,128)(2,1)S(1)}, u32[]{:S(2)}, u32[]{:S(2)}) collective-permute-start(bf16[256,256]{1,0:T(8,128)(2,1)} %product.1.refs_0_), channel_id=1, source_target_pairs={{0,16},{8,24},{16,0},{24,8},{1,17},{9,25},{17,1},{25,9},{2,18},{10... | collective-permute-start | bytes 393224 | tf_op jit(solution)/shard_map/ppermute | solution.py:32
  79.9 6.1 %collective-permute-start.19 = (bf16[256,256]{1,0:T(8,128)(2,1)}, bf16[256,256]{1,0:T(8,128)(2,1)S(1)}, u32[]{:S(2)}, u32[]{:S(2)}) collective-permute-start(bf16[256,256]{1,0:T(8,128)(2,1)} %product.1.refs_0_), channel_id=1, source_target_pairs={{0,24},{8,16},{16,8},{24,0},{1,25},{9,17},{17,9},{25,1},{2,26},{10... | collective-permute-start | bytes 393224 | tf_op jit(solution)/shard_map/ppermute | solution.py:32
  83.2 2.8 %copy-start.11 = (bf16[256,256]{1,0:T(8,128)(2,1)}, bf16[256,256]{1,0:T(8,128)(2,1)S(1)}, u32[]{:S(2)}) copy-start(bf16[256,256]{1,0:T(8,128)(2,1)S(1)} %collective-permute-done.17.refs_1_) | copy-start | bytes 393220
  (5 other events, 6.6 us)

commit v2 on v1

v2 whole, which is shorter than its diff:
```python
import functools

import jax
import jax.numpy as jnp
from jax import lax
from jax.experimental import pallas as pl
from jax.experimental.pallas import tpu as pltpu
from jax.sharding import PartitionSpec as P


UNROLL = 4
WORDS = 8
VMEM_LIMIT = 28 * 1024 * 1024
VMEM_MARGIN = 4 * 1024 * 1024


def target(i, s, n):
    return i ^ s if n & (n - 1) == 0 else (i + s) % n


def source(i, s, n):
    return i ^ s if n & (n - 1) == 0 else (i - s) % n


def target_slot(i, j, n):
    return i ^ j if n & (n - 1) == 0 else (j - i) % n


def source_slot(i, j, n):
    return i ^ j if n & (n - 1) == 0 else (i - j) % n


def exchange(value, axis, slot):
    n = lax.axis_size(axis)
    return lax.ppermute(value, axis, [(i, target(i, slot, n)) for i in range(n)])


def masked_blocks(matrix, block_mask, block_size):
    mask_rows, mask_cols = block_mask.shape
    shaped = matrix.reshape(mask_rows, block_size, mask_cols, block_size)
    factor = block_mask.astype(matrix.dtype)[:, None, :, None]
    return (shaped * factor).reshape(mask_rows * block_size, mask_cols * block_size)


def place_of(sizes, per_owner, owner, block):
    rows, cols, layers = sizes
    far_layer = target_slot(lax.axis_index("panel"), owner % layers, layers)
    far_col = target_slot(lax.axis_index("col"), (owner // layers) % cols, cols)
    far_row = target_slot(lax.axis_index("row"), owner // (layers * cols), rows)
    near = far_row == 0
    at = jnp.where(near, far_layer, far_layer * (rows - 1) + far_row - 1)
    return near, (at * cols + far_col) * per_owner + block


def accumulate(chunk, table, basis, weighted, total):
    size = basis.shape[2]
    most = (table.shape[0] - 2 * WORDS) // (2 * WORDS)

    def step(i, carry):
        for j in range(UNROLL):
            at = (chunk * most + i * UNROLL + j) * WORDS
            rights = jnp.concatenate([weighted[table[at + 1]], weighted[table[at + 2]]], axis=1)
            found = lax.dot_general(
                basis[table[at]], rights, (((0,), (0,)), ((), ())), preferred_element_type=jnp.float32
            )
            total[table[at + 3]] += found[:, :size]
            total[table[at + 4]] += found[:, size:]
        return carry

    count = table[(2 * most + chunk) * WORDS]
    lax.fori_loop(0, (count + UNROLL - 1) // UNROLL, step, 0)


def clear(total):
    def zero(i, carry):
        total[i] = jnp.zeros(total.shape[1:], jnp.float32)
        return carry

    lax.fori_loop(0, total.shape[0], zero, 0)


def put(total, keep_ref, send_ref):
    half = keep_ref.shape[0]

    def one(i, carry):
        keep_ref[i] = total[i].astype(jnp.bfloat16)
        send_ref[i] = total[half + i].astype(jnp.bfloat16)
        return carry

    lax.fori_loop(0, half, one, 0)


def integrate_far_body(
    sizes, per_owner, trash, pair_ref, owner_ref, block_ref, basis_ref, pot_ref,
    weighted, table, keep_ref, send_ref, basis, pot_cols, total, pending, arrived,
):
    atoms, points, size = basis.shape
    parts = block_ref.shape[0]
    most = (table.shape[0] - 2 * WORDS) // (2 * WORDS)
    radix = pl.next_power_of_2(max(trash) + 1)

    def fetch(a):
        return pltpu.make_async_copy(basis_ref.at[a], basis.at[a], arrived.at[a])

    for a in range(atoms):
        fetch(a).start()
    for k in range(2 * atoms):
        pending[k] = -1
    clear(total)
    for k in range(points // size):
        row = pot_ref[k : k + 1, :]
        pot_cols[k * size : (k + 1) * size, :] = jnp.broadcast_to(row, (size, size)).T

    def unit(chunk, count, left, first, second, first_slot, second_slot):
        at = (jnp.where(chunk, most, 0) + count) * WORDS
        for k, word in enumerate((left, first, second, first_slot, second_slot)):
            table[at + k] = word

    def weigh_and_plan(a, counts):
        fetch(a).wait()
        for k in range(points // size):
            at = slice(k * size, (k + 1) * size)
            weighted[a, at, :] = (basis[a, at, :].astype(jnp.float32) * pot_cols[at, :]).astype(jnp.bfloat16)
        far_count, near_count = counts
        for k in range(parts // atoms):
            n = a * (parts // atoms) + k
            left, right = pair_ref[0, n], pair_ref[1, n]
            near, slot = place_of(sizes, per_owner, owner_ref[0, n], block_ref[n])
            key = left + jnp.where(near, atoms, 0)
            earlier = pending[key]
            fresh = earlier < 0
            pending[key] = jnp.where(fresh, right * radix + slot, -1)
            unit(near, jnp.where(near, near_count, far_count), left, earlier // radix, right, earlier % radix, slot)
            far_count += jnp.where(fresh | near, 0, 1)
            near_count += jnp.where(fresh | jnp.logical_not(near), 0, 1)
        return far_count, near_count

    counts = lax.fori_loop(0, atoms, weigh_and_plan, (jnp.int32(0), jnp.int32(0)))
    for chunk in range(2):

        def single(left, count):
            earlier = pending[chunk * atoms + left]
            right, slot = earlier // radix, earlier % radix
            unit(bool(chunk), count, left, right, right, slot, trash[chunk])
            return count + jnp.where(earlier < 0, 0, 1)

        count = lax.fori_loop(0, atoms, single, counts[chunk])
        for k in range(UNROLL - 1):
            unit(bool(chunk), count + k, 0, 0, 0, trash[chunk], trash[chunk])
        table[(2 * most + chunk) * WORDS] = count
    accumulate(0, table, basis, weighted, total)
    put(total, keep_ref, send_ref)


def integrate_near_body(table, basis, weighted, keep_ref, send_ref, total):
    clear(total)
    accumulate(1, table, basis, weighted, total)
    put(total, keep_ref, send_ref)


def integrate(basis_values, potential, pair_atoms, target_device, target_block, sizes, per_owner):
    atoms, points, size = basis_values.shape
    parts = target_block.shape[0]
    rows, cols, layers = sizes
    per_row = cols * per_owner
    trash = layers * (rows - 1) * per_row, layers * per_row
    most = (parts + atoms) // 2 + UNROLL + 1
    smem = pl.BlockSpec(memory_space=pltpu.SMEM)
    vmem = pl.BlockSpec(memory_space=pltpu.VMEM)

    def half(blocks):
        return jax.ShapeDtypeStruct((blocks // 2, size, size), jnp.bfloat16)

    def total(blocks):
        return pltpu.VMEM((blocks + 1, size, size), jnp.float32)

    def options(share):
        return dict(
            compiler_params=pltpu.CompilerParams(vmem_limit_bytes=VMEM_LIMIT),
            cost_estimate=pl.CostEstimate(
                flops=int(4 * parts * points * size * size * share),
                bytes_accessed=4 * basis_values.size,
                transcendentals=0,
            ),
        )

    weighted, table, far_keep, far_send = pl.pallas_call(
        functools.partial(integrate_far_body, sizes, per_owner, trash),
        out_shape=(
            jax.ShapeDtypeStruct(basis_values.shape, jnp.bfloat16),
            jax.ShapeDtypeStruct(((2 * most + 2) * WORDS,), jnp.int32),
            half(trash[0]),
            half(trash[0]),
        ),
        in_specs=[smem, smem, smem, pl.BlockSpec(memory_space=pltpu.HBM), vmem],
        out_specs=(vmem, smem, vmem, vmem),
        scratch_shapes=[
            pltpu.VMEM(basis_values.shape, jnp.bfloat16),
            pltpu.VMEM((points, size), jnp.float32),
            total(trash[0]),
            pltpu.SMEM((2 * atoms,), jnp.int32),
            pltpu.SemaphoreType.DMA((atoms,)),
        ],
        name="integrate_far",
        **options(1 - 1 / rows),
    )(
        pair_atoms,
        target_device.reshape(1, parts),
        target_block,
        pltpu.with_memory_space_constraint(basis_values, pltpu.HBM),
        potential.reshape(points // size, size),
    )
    near_keep, near_send = pl.pallas_call(
        integrate_near_body,
        out_shape=(half(trash[1]), half(trash[1])),
        in_specs=[smem, vmem, vmem],
        out_specs=(vmem, vmem),
        scratch_shapes=[total(trash[1])],
        name="integrate_near",
        **options(1 / rows),
    )(table, basis_values, weighted)
    return far_keep, far_send, near_keep, near_send


def index_of(row, col, s, count):
    return source_slot(row, source(col, s, count), count)


def product_body(count, *refs):
    lefts, rights, out = refs[:count], refs[count : 2 * count], refs[-2]
    stacked = refs[-1]
    for s in range(count):
        stacked[s] = rights[s][...]
    row, col = lax.axis_index("row"), lax.axis_index("col")
    found = None
    for s in range(count):
        term = jnp.dot(lefts[s][...], stacked[index_of(row, col, s, count)], preferred_element_type=jnp.float32)
        found = term if found is None else found + term
    out[...] = found.astype(out.dtype)


def product(lefts, rights, dtype):
    count = len(lefts)
    rows, columns = lefts[0].shape[0], rights[0].shape[1]
    vmem = pl.BlockSpec(memory_space=pltpu.VMEM)
    return pl.pallas_call(
        functools.partial(product_body, count),
        out_shape=jax.ShapeDtypeStruct((rows, columns), dtype),
        in_specs=[vmem] * (2 * count),
        out_specs=vmem,
        scratch_shapes=[pltpu.VMEM((count,) + rights[0].shape, rights[0].dtype)],
        cost_estimate=pl.CostEstimate(
            flops=2 * count * rows * columns * rights[0].shape[0],
            bytes_accessed=2 * count * (lefts[0].size + rights[0].size),
            transcendentals=0,
        ),
        compiler_params=pltpu.CompilerParams(vmem_limit_bytes=2 * VMEM_MARGIN),
        name="product",
    )(*lefts, *rights)


def gradient_body(count, own_ref, other_ref, *refs):
    rights, out, stacked = refs[:count], refs[-2], refs[-1]
    for s in range(count):
        stacked[s] = rights[s][...]
    blocks, size = own_ref.shape[1], own_ref.shape[2]
    row, col, side = lax.axis_index("row"), lax.axis_index("col"), lax.axis_index("panel")
    for which, ref in ((side, own_ref), (1 - side, other_ref)):
        found = None
        for s in range(count):
            left = jnp.concatenate([ref[s, b] for b in range(blocks)], axis=1)
            term = jnp.dot(left, stacked[index_of(row, col, s, count)], preferred_element_type=jnp.float32)
            found = term if found is None else found + term
        out[pl.ds(which * size, size), :] = found


def program(
    basis_values,
    potential,
    pair_atoms,
    target_device,
    target_block,
    density,
    density_mask,
    inverse_intersection,
    inverse_mask,
):
    size = basis_values.shape[2]
    rows, cols, layers = lax.axis_size("row"), lax.axis_size("col"), lax.axis_size("panel")
    layer = lax.axis_index("panel")
    tile_blocks = density_mask.shape[0]
    per_owner = tile_blocks // layers * tile_blocks

    width = inverse_intersection.shape[1] // layers
    mask_width = inverse_mask.shape[1] // layers
    density_used = masked_blocks(density, density_mask, size)
    inverse_used = masked_blocks(
        lax.dynamic_slice_in_dim(inverse_intersection, layer * width, width, 1),
        lax.dynamic_slice_in_dim(inverse_mask, layer * mask_width, mask_width, 1),
        size,
    )
    lefts = [density_used] + [exchange(density_used, "col", s) for s in range(1, cols)]
    rights = [inverse_used] + [exchange(inverse_used, "row", s) for s in range(1, rows)]

    far_keep, far_send, near_keep, near_send = integrate(
        basis_values, potential, pair_atoms, target_device, target_block, (rows, cols, layers), per_owner
    )

    panel_tile = product(lefts, rights, jnp.bfloat16)
    panels = [panel_tile] + [exchange(panel_tile, "row", s) for s in range(1, rows)]

    def added(*terms):
        return sum(t.astype(jnp.float32) for t in terms[1:]) + terms[0].astype(jnp.float32)

    per_row = cols * per_owner
    far_got = exchange(far_send, "panel", 1)
    near_got = exchange(near_send, "panel", 1)
    parts = [added(near_keep, near_got).astype(jnp.bfloat16)] + [
        added(far_keep[s * per_row : (s + 1) * per_row], far_got[s * per_row : (s + 1) * per_row]).astype(jnp.bfloat16)
        for s in range(rows - 1)
    ]
    got = [exchange(parts[s], "row", s) for s in range(1, rows)]
    parts = [
        added(*[p[s * per_owner : (s + 1) * per_owner] for p in [parts[0]] + got]).astype(jnp.bfloat16)
        for s in range(cols)
    ]
    got = [exchange(parts[s], "col", s) for s in range(1, cols)]
    mine = added(parts[0], *got).astype(jnp.bfloat16)
    line = jnp.stack([mine] + [exchange(mine, "col", s) for s in range(1, cols)])
    other = exchange(line, "panel", 1)
    vmem = pl.BlockSpec(memory_space=pltpu.VMEM)
    return pl.pallas_call(
        functools.partial(gradient_body, cols),
        out_shape=jax.ShapeDtypeStruct((layers * size, width), jnp.float32),
        in_specs=[vmem] * (2 + cols),
        out_specs=vmem,
        scratch_shapes=[pltpu.VMEM((cols,) + panel_tile.shape, jnp.bfloat16)],
        compiler_params=pltpu.CompilerParams(vmem_limit_bytes=2 * VMEM_MARGIN),
        name="gradient",
    )(line, other, *panels)


def solution(mesh):
    placed = (
        P(("row", "col", "panel"), None, None),
        P(("row", "col", "panel")),
        P(None, ("row", "col", "panel")),
        P(("row", "col", "panel"), None),
        P(("row", "col", "panel")),
        P("row", "col"),
        P("row", "col"),
        P("row", "col"),
        P("row", "col"),
    )
    return jax.shard_map(program, mesh=mesh, in_specs=placed, out_specs=P("row", ("col", "panel")), check_vma=False)
```

time: 89.3 us -> 86.3 us (0.966)
  starting transfers between devices: 28.8 us -> 24.3 us
  waiting for transfers between devices: 26.4 us -> 30.3 us
  other arithmetic: 3.77 us -> 0.7 us
  Pallas kernels: 26.7 us -> 27.7 us
    ppermute x20 -> x21, starting transfers between devices: 28.8 us -> 24.3 us  [exchange(): lax.ppermute(value, axis, [(i, target(i, slot, n)) for i in range(n)])]
    ppermute x20 -> x21, waiting for transfers between devices: 26.4 us -> 30.3 us  [exchange(): lax.ppermute(value, axis, [(i, target(i, slot, n)) for i in range(n)])]
    pallas_call x2 -> x3, Pallas kernels: 24.4 us -> 27.4 us  [the longest x1 20 us: integrate(): pl.pallas_call(functools.partial(integrate_far_body, sizes, per_owner, tr...]
    pallas_call x1, Pallas kernels: 2.29 us -> 0.34 us  [product(): pl.pallas_call(functools.partial(product_body, count), out_shape=jax.Shap...]
    squeeze x1 -> x0, local copies, waits for them, and re-layouts: 1.35 us -> none  [local(): pair_atoms[1]]
    unnamed x34 -> x18, local copies, waits for them, and re-layouts: 1.41 us -> 2.71 us
    add x1 -> x0, other arithmetic: 1.21 us -> none  [local(): (slots * cols + target_slot(col, there_col, cols)) * per_owner]
    convert_element_type x3 -> x4, other arithmetic: 1.72 us -> 0.52 us  [the longest x1 0.27 us: program(): added(far_keep[s * per_row:(s + 1) * per_row], far_got[s * per_row:(s + 1...]
  transfers between devices with their start and end apart: 20 -> 21, of which waited for: 13 -> 11; matrix products, arithmetic and copies ran while one was open for 1% -> 1% of each run, Pallas kernels for 3% -> 8%
where the time goes in v2:
time: 86.3 us; the launch traced here: 86.1 us
  waiting for transfers between devices  30.3 us (35%)
  Pallas kernels  27.7 us (32%)
  starting transfers between devices  24.3 us (28%)
  local copies, waits for them, and re-layouts  2.98 us (3%)
    ppermute x21, waiting for transfers between devices, exchange(): lax.ppermute(value, axis, [(i, target(i, slot, n)) for i in range(n)])  30.3 us
    ppermute x21, starting transfers between devices, exchange(): lax.ppermute(value, axis, [(i, target(i, slot, n)) for i in range(n)])  24.3 us
    pallas_call x1, Pallas kernels, integrate(): pl.pallas_call(functools.partial(integrate_far_body, sizes, per_owner, tr...  20 us
    pallas_call x1, Pallas kernels, integrate(): pl.pallas_call(integrate_near_body, out_shape=(half(trash[1]), half(trash...  6.35 us
    unnamed x18, local copies, waits for them, and re-layouts  2.71 us
  transfers between devices with their start and end apart: 21, of which 11 were waited for; matrix products, arithmetic and copies ran while one was open for 1% of the time, Pallas kernels for 8%

profile of v2, /device:TPU:0, one launch (start us, length us, event | category | flops | bytes accessed | tf_op | source)
XLA Modules:
  0.0 86.1 jit_solution(16334542176514194585)
XLA Ops:
  0.0 0.7 copy-done.1
  0.7 0.7 copy-done.2
  1.4 0.7 copy-done.3
  2.0 0.7 copy-done.4
  2.7 20.0 %integrate_far.1 = (bf16[16,2048,128]{2,1,0:T(8,128)(2,1)S(1)}, s32[1248]{0:T(1024)S(1)}, bf16[24,128,128]{2,1,0:T(8,128)(2,1)S(1)}, bf16[24,128,128]{2,1,0:T(8,128)(2,1)S(1)}) custom-call(s32[2,128]{1,0:T(2,128)S(1)} %copy-done.2, s32[1,128]{1,0:T(1,128)S(1)} %bitcast.15, s32[128]{0:T(128)S(1)} %copy-done.4, bf16[16,2048,128]{2,1,0:T(8,128)(2,1)} %basis.1, ...), custom_call_target="tpu_custom_call" | custom-call | flops 12884901888 | bytes 16777216 | tf_op jit(solution)/shard_map/integrate_far/pallas_call | solution.py:187
  22.7 1.5 %collective-permute-start = (bf16[24,128,128]{2,1,0:T(8,128)(2,1)S(1)}, bf16[24,128,128]{2,1,0:T(8,128)(2,1)S(1)}, u32[]{:S(2)}, u32[]{:S(2)}) collective-permute-start(bf16[24,128,128]{2,1,0:T(8,128)(2,1)S(1)} %get-tuple-element.11), channel_id=1, source_target_pairs={{0,1},{1,0},{2,3},{3,2},{4,5},{5,4},{6,7},{7,6},{8,9},{9,8},{10,11... | collective-permute-start | bytes 2359304 | tf_op jit(solution)/shard_map/ppermute | solution.py:35
  24.2 6.4 %integrate_near.1 = (bf16[8,128,128]{2,1,0:T(8,128)(2,1)S(1)}, bf16[8,128,128]{2,1,0:T(8,128)(2,1)S(1)}) custom-call(s32[1248]{0:T(1024)S(1)} %get-tuple-element.13.table, bf16[16,2048,128]{2,1,0:T(8,128)(2,1)S(1)} %copy-done, bf16[16,2048,128]{2,1,0:T(8,128)(2,1)S(1)} %get-tuple-element.14.weighted), custom_call_target="tpu_custom_call" | custom-call | flops 4294967296 | bytes 16777216 | tf_op jit(solution)/shard_map/integrate_near/pallas_call | solution.py:213
  30.9 1.2 %collective-permute-start.1 = (bf16[8,128,128]{2,1,0:T(8,128)(2,1)S(1)}, bf16[8,128,128]{2,1,0:T(8,128)(2,1)S(1)}, u32[]{:S(2)}, u32[]{:S(2)}) collective-permute-start(bf16[8,128,128]{2,1,0:T(8,128)(2,1)S(1)} %get-tuple-element.17), channel_id=1, source_target_pairs={{0,8},{8,0},{16,24},{24,16},{1,9},{9,1},{17,25},{25,17},{2,10},{10... | collective-permute-start | bytes 786440 | tf_op jit(solution)/shard_map/ppermute | solution.py:35
  32.1 2.7 %collective-permute-start.2 = (bf16[8,128,128]{2,1,0:T(8,128)(2,1)S(1)}, bf16[8,128,128]{2,1,0:T(8,128)(2,1)S(1)}, u32[]{:S(2)}, u32[]{:S(2)}) collective-permute-start(bf16[8,128,128]{2,1,0:T(8,128)(2,1)S(1)} %get-tuple-element.19), channel_id=1, source_target_pairs={{0,16},{8,24},{16,0},{24,8},{1,17},{9,25},{17,1},{25,9},{2,18},{10... | collective-permute-start | bytes 786440 | tf_op jit(solution)/shard_map/ppermute | solution.py:35
  34.9 5.2 %collective-permute-done.1 = bf16[8,128,128]{2,1,0:T(8,128)(2,1)S(1)} collective-permute-done((bf16[8,128,128]{2,1,0:T(8,128)(2,1)S(1)}, bf16[8,128,128]{2,1,0:T(8,128)(2,1)S(1)}, u32[]{:S(2)}, u32[]{:S(2)}) %collective-permute-start.1) | collective-permute-done | bytes 262176 | tf_op jit(solution)/shard_map/ppermute | solution.py:35
  40.1 6.9 %collective-permute-done.2 = bf16[8,128,128]{2,1,0:T(8,128)(2,1)S(1)} collective-permute-done((bf16[8,128,128]{2,1,0:T(8,128)(2,1)S(1)}, bf16[8,128,128]{2,1,0:T(8,128)(2,1)S(1)}, u32[]{:S(2)}, u32[]{:S(2)}) %collective-permute-start.2) | collective-permute-done | bytes 262176 | tf_op jit(solution)/shard_map/ppermute | solution.py:35
  47.2 1.1 %collective-permute-start.5 = (bf16[2,128,128]{2,1,0:T(8,128)(2,1)S(1)}, bf16[2,128,128]{2,1,0:T(8,128)(2,1)S(1)}, u32[]{:S(2)}, u32[]{:S(2)}) collective-permute-start(bf16[2,128,128]{2,1,0:T(8,128)(2,1)S(1)} %get-tuple-element.20), channel_id=1, source_target_pairs={{0,2},{2,0},{4,6},{6,4},{1,3},{3,1},{5,7},{7,5},{8,10},{10,8},{12,... | collective-permute-start | bytes 196616 | tf_op jit(solution)/shard_map/ppermute | solution.py:35
  48.3 2.6 %collective-permute-start.6 = (bf16[2,128,128]{2,1,0:T(8,128)(2,1)S(1)}, bf16[2,128,128]{2,1,0:T(8,128)(2,1)S(1)}, u32[]{:S(2)}, u32[]{:S(2)}) collective-permute-start(bf16[2,128,128]{2,1,0:T(8,128)(2,1)S(1)} %get-tuple-element.22), channel_id=1, source_target_pairs={{0,4},{2,6},{4,0},{6,2},{1,5},{3,7},{5,1},{7,3},{8,12},{10,14},{12... | collective-permute-start | bytes 196616 | tf_op jit(solution)/shard_map/ppermute | solution.py:35
  51.0 0.8 collective-permute-start.7
  51.9 1.4 %collective-permute-start.15 = (bf16[256,256]{1,0:T(8,128)(2,1)S(1)}, bf16[256,256]{1,0:T(8,128)(2,1)S(1)}, u32[]{:S(2)}, u32[]{:S(2)}) collective-permute-start(bf16[256,256]{1,0:T(8,128)(2,1)S(1)} %bitcast_multiply_fusion.refs_4_), channel_id=1, source_target_pairs={{0,8},{8,0},{16,24},{24,16},{1,9},{9,1},{17,25},{25,17},{2,10},{10... | collective-permute-start | bytes 393224 | tf_op jit(solution)/shard_map/ppermute | solution.py:35
  54.0 1.8 %collective-permute-done.6 = bf16[2,128,128]{2,1,0:T(8,128)(2,1)S(1)} collective-permute-done((bf16[2,128,128]{2,1,0:T(8,128)(2,1)S(1)}, bf16[2,128,128]{2,1,0:T(8,128)(2,1)S(1)}, u32[]{:S(2)}, u32[]{:S(2)}) %collective-permute-start.6) | collective-permute-done | bytes 65568 | tf_op jit(solution)/shard_map/ppermute | solution.py:35
  55.8 1.3 %collective-permute-done.7 = bf16[2,128,128]{2,1,0:T(8,128)(2,1)S(1)} collective-permute-done((bf16[2,128,128]{2,1,0:T(8,128)(2,1)S(1)}, bf16[2,128,128]{2,1,0:T(8,128)(2,1)S(1)}, u32[]{:S(2)}, u32[]{:S(2)}) %collective-permute-start.7) | collective-permute-done | bytes 65568 | tf_op jit(solution)/shard_map/ppermute | solution.py:35
  57.2 0.8 collective-permute-start.8
  58.0 1.7 %collective-permute-start.9 = (bf16[2,128,128]{2,1,0:T(8,128)(2,1)S(1)}, bf16[2,128,128]{2,1,0:T(8,128)(2,1)S(1)}, u32[]{:S(2)}, u32[]{:S(2)}) collective-permute-start(bf16[2,128,128]{2,1,0:T(8,128)(2,1)S(1)} %add_convert_fusion.4), channel_id=1, source_target_pairs={{0,4},{2,6},{4,0},{6,2},{1,5},{3,7},{5,1},{7,3},{8,12},{10,14},{12... | collective-permute-start | bytes 196616 | tf_op jit(solution)/shard_map/ppermute | solution.py:35
  59.7 2.0 %collective-permute-start.10 = (bf16[2,128,128]{2,1,0:T(8,128)(2,1)S(1)}, bf16[2,128,128]{2,1,0:T(8,128)(2,1)S(1)}, u32[]{:S(2)}, u32[]{:S(2)}) collective-permute-start(bf16[2,128,128]{2,1,0:T(8,128)(2,1)S(1)} %add_convert_fusion.4), channel_id=1, source_target_pairs={{0,6},{2,4},{4,2},{6,0},{1,7},{3,5},{5,3},{7,1},{8,14},{10,12},{12... | collective-permute-start | bytes 196616 | tf_op jit(solution)/shard_map/ppermute | solution.py:35
  61.9 1.6 %collective-permute-start.17 = (bf16[256,256]{1,0:T(8,128)(2,1)S(1)}, bf16[256,256]{1,0:T(8,128)(2,1)S(1)}, u32[]{:S(2)}, u32[]{:S(2)}) collective-permute-start(bf16[256,256]{1,0:T(8,128)(2,1)S(1)} %bitcast_multiply_fusion.refs_4_), channel_id=1, source_target_pairs={{0,24},{8,16},{16,8},{24,0},{1,25},{9,17},{17,9},{25,1},{2,26},{10... | collective-permute-start | bytes 393224 | tf_op jit(solution)/shard_map/ppermute | solution.py:35
  63.5 1.5 %collective-permute-done.9 = bf16[2,128,128]{2,1,0:T(8,128)(2,1)S(1)} collective-permute-done((bf16[2,128,128]{2,1,0:T(8,128)(2,1)S(1)}, bf16[2,128,128]{2,1,0:T(8,128)(2,1)S(1)}, u32[]{:S(2)}, u32[]{:S(2)}) %collective-permute-start.9) | collective-permute-done | bytes 65568 | tf_op jit(solution)/shard_map/ppermute | solution.py:35
  65.5 0.9 %collective-permute-done.10 = bf16[2,128,128]{2,1,0:T(8,128)(2,1)S(1)} collective-permute-done((bf16[2,128,128]{2,1,0:T(8,128)(2,1)S(1)}, bf16[2,128,128]{2,1,0:T(8,128)(2,1)S(1)}, u32[]{:S(2)}, u32[]{:S(2)}) %collective-permute-start.10) | collective-permute-done | bytes 65568 | tf_op jit(solution)/shard_map/ppermute | solution.py:35
  66.5 2.0 %collective-permute-start.14 = (bf16[256,256]{1,0:T(8,128)(2,1)S(1)}, bf16[256,256]{1,0:T(8,128)(2,1)S(1)}, u32[]{:S(2)}, u32[]{:S(2)}) collective-permute-start(bf16[256,256]{1,0:T(8,128)(2,1)S(1)} %bitcast_multiply_fusion.1.refs_0_), channel_id=1, source_target_pairs={{0,6},{2,4},{4,2},{6,0},{1,7},{3,5},{5,3},{7,1},{8,14},{10,12},{12... | collective-permute-start | bytes 393224 | tf_op jit(solution)/shard_map/ppermute | solution.py:35
  68.6 0.7 collective-permute-done.12.refs_1_
  69.3 6.8 %collective-permute-done.13.refs_2_ = bf16[256,256]{1,0:T(8,128)(2,1)S(1)} collective-permute-done((bf16[256,256]{1,0:T(8,128)(2,1)S(1)}, bf16[256,256]{1,0:T(8,128)(2,1)S(1)}, u32[]{:S(2)}, u32[]{:S(2)}) %collective-permute-start.13) | collective-permute-done | bytes 131104 | tf_op jit(solution)/shard_map/ppermute | solution.py:35
  76.5 2.6 %collective-permute-start.19 = (bf16[256,256]{1,0:T(8,128)(2,1)S(1)}, bf16[256,256]{1,0:T(8,128)(2,1)S(1)}, u32[]{:S(2)}, u32[]{:S(2)}) collective-permute-start(bf16[256,256]{1,0:T(8,128)(2,1)S(1)} %product.1.refs_0_), channel_id=1, source_target_pairs={{0,16},{8,24},{16,0},{24,8},{1,17},{9,25},{17,1},{25,9},{2,18},{10... | collective-permute-start | bytes 393224 | tf_op jit(solution)/shard_map/ppermute | solution.py:35
  79.2 0.8 collective-permute-start.20
  80.0 1.5 %collective-permute-done.18.refs_1_ = bf16[256,256]{1,0:T(8,128)(2,1)S(1)} collective-permute-done((bf16[256,256]{1,0:T(8,128)(2,1)S(1)}, bf16[256,256]{1,0:T(8,128)(2,1)S(1)}, u32[]{:S(2)}, u32[]{:S(2)}) %collective-permute-start.18) | collective-permute-done | bytes 131104 | tf_op jit(solution)/shard_map/ppermute | solution.py:35
  81.5 1.6 %collective-permute-done.19.refs_2_ = bf16[256,256]{1,0:T(8,128)(2,1)S(1)} collective-permute-done((bf16[256,256]{1,0:T(8,128)(2,1)S(1)}, bf16[256,256]{1,0:T(8,128)(2,1)S(1)}, u32[]{:S(2)}, u32[]{:S(2)}) %collective-permute-start.19) | collective-permute-done | bytes 131104 | tf_op jit(solution)/shard_map/ppermute | solution.py:35
  83.1 1.9 %collective-permute-done.20.refs_3_ = bf16[256,256]{1,0:T(8,128)(2,1)S(1)} collective-permute-done((bf16[256,256]{1,0:T(8,128)(2,1)S(1)}, bf16[256,256]{1,0:T(8,128)(2,1)S(1)}, u32[]{:S(2)}, u32[]{:S(2)}) %collective-permute-start.20) | collective-permute-done | bytes 131104 | tf_op jit(solution)/shard_map/ppermute | solution.py:35
  85.1 1.1 %gradient.1 = f32[256,256]{1,0:T(8,128)} custom-call(bf16[4,2,128,128]{3,2,1,0:T(8,128)(2,1)S(1)} %pad_maximum_fusion.own_ref, bf16[4,2,128,128]{3,2,1,0:T(8,128)(2,1)S(1)} %collective-permute-done.11.other_ref, bf16[256,256]{1,0:T(8,128)(2,1)S(1)} %product.1.refs_0_, bf16[256,256]{1,0:T(8,128)(2,1)S(1)} %collective-permute-done.18.refs_1_, ...), custom_call_target="tpu_custom_call" | custom-call | tf_op jit(solution)/shard_map/gradient/pallas_call | solution.py:332
  (43 shorter events, 2.8 us)
Async XLA Ops:
  0.0 0.7 copy-start.1
  0.7 0.7 copy-start.2
  1.4 0.7 copy-start.3
  2.0 0.7 copy-start.4
  2.7 21.4 %copy-start = (bf16[16,2048,128]{2,1,0:T(8,128)(2,1)S(1)}, bf16[16,2048,128]{2,1,0:T(8,128)(2,1)}, u32[]{:S(2)}) copy-start(bf16[16,2048,128]{2,1,0:T(8,128)(2,1)} %basis.1) | copy-start | bytes 25165828
  22.7 8.0 %collective-permute-start = (bf16[24,128,128]{2,1,0:T(8,128)(2,1)S(1)}, bf16[24,128,128]{2,1,0:T(8,128)(2,1)S(1)}, u32[]{:S(2)}, u32[]{:S(2)}) collective-permute-start(bf16[24,128,128]{2,1,0:T(8,128)(2,1)S(1)} %get-tuple-element.11), channel_id=1, source_target_pairs={{0,1},{1,0},{2,3},{3,2},{4,5},{5,4},{6,7},{7,6},{8,9},{9,8},{10,11... | collective-permute-start | bytes 2359304 | tf_op jit(solution)/shard_map/ppermute | solution.py:35
  24.1 10.7 %copy-start.7 = (s32[2,4]{1,0:T(2,128)S(1)}, s32[2,4]{1,0:T(2,128)}, u32[]{:S(2)}) copy-start(s32[2,4]{1,0:T(2,128)} %param.17) | copy-start | bytes 100
  24.1 27.8 %copy-start.6 = (bf16[256,512]{1,0:T(8,128)(2,1)S(1)}, bf16[256,512]{1,0:T(8,128)(2,1)}, u32[]{:S(2)}) copy-start(bf16[256,512]{1,0:T(8,128)(2,1)} %param.16) | copy-start | bytes 786436
  24.1 29.9 %copy-start.8 = (s32[2,2]{1,0:T(2,128)S(1)}, s32[2,2]{1,0:T(2,128)}, u32[]{:S(2)}) copy-start(s32[2,2]{1,0:T(2,128)} %param.15) | copy-start | bytes 52
  24.1 37.7 %copy-start.5 = (bf16[256,256]{1,0:T(8,128)(2,1)S(1)}, bf16[256,256]{1,0:T(8,128)(2,1)}, u32[]{:S(2)}) copy-start(bf16[256,256]{1,0:T(8,128)(2,1)} %param.14) | copy-start | bytes 393220
  30.5 4.3 %collective-permute-start.4 = (bf16[8,128,128]{2,1,0:T(8,128)(2,1)S(1)}, bf16[8,128,128]{2,1,0:T(8,128)(2,1)S(1)}, u32[]{:S(2)}, u32[]{:S(2)}) collective-permute-start(bf16[8,128,128]{2,1,0:T(8,128)(2,1)S(1)} %get-tuple-element.15), channel_id=1, source_target_pairs={{0,1},{1,0},{2,3},{3,2},{4,5},{5,4},{6,7},{7,6},{8,9},{9,8},{10,11... | collective-permute-start | bytes 786440 | tf_op jit(solution)/shard_map/ppermute | solution.py:35
  30.9 9.2 %collective-permute-start.1 = (bf16[8,128,128]{2,1,0:T(8,128)(2,1)S(1)}, bf16[8,128,128]{2,1,0:T(8,128)(2,1)S(1)}, u32[]{:S(2)}, u32[]{:S(2)}) collective-permute-start(bf16[8,128,128]{2,1,0:T(8,128)(2,1)S(1)} %get-tuple-element.17), channel_id=1, source_target_pairs={{0,8},{8,0},{16,24},{24,16},{1,9},{9,1},{17,25},{25,17},{2,10},{10... | collective-permute-start | bytes 786440 | tf_op jit(solution)/shard_map/ppermute | solution.py:35
  32.1 15.0 %collective-permute-start.2 = (bf16[8,128,128]{2,1,0:T(8,128)(2,1)S(1)}, bf16[8,128,128]{2,1,0:T(8,128)(2,1)S(1)}, u32[]{:S(2)}, u32[]{:S(2)}) collective-permute-start(bf16[8,128,128]{2,1,0:T(8,128)(2,1)S(1)} %get-tuple-element.19), channel_id=1, source_target_pairs={{0,16},{8,24},{16,0},{24,8},{1,17},{9,25},{17,1},{25,9},{2,18},{10... | collective-permute-start | bytes 786440 | tf_op jit(solution)/shard_map/ppermute | solution.py:35
  34.8 12.3 %collective-permute-start.3 = (bf16[8,128,128]{2,1,0:T(8,128)(2,1)S(1)}, bf16[8,128,128]{2,1,0:T(8,128)(2,1)S(1)}, u32[]{:S(2)}, u32[]{:S(2)}) collective-permute-start(bf16[8,128,128]{2,1,0:T(8,128)(2,1)S(1)} %get-tuple-element.18), channel_id=1, source_target_pairs={{0,24},{8,16},{16,8},{24,0},{1,25},{9,17},{17,9},{25,1},{2,26},{10... | collective-permute-start | bytes 786440 | tf_op jit(solution)/shard_map/ppermute | solution.py:35
  47.2 6.8 %collective-permute-start.5 = (bf16[2,128,128]{2,1,0:T(8,128)(2,1)S(1)}, bf16[2,128,128]{2,1,0:T(8,128)(2,1)S(1)}, u32[]{:S(2)}, u32[]{:S(2)}) collective-permute-start(bf16[2,128,128]{2,1,0:T(8,128)(2,1)S(1)} %get-tuple-element.20), channel_id=1, source_target_pairs={{0,2},{2,0},{4,6},{6,4},{1,3},{3,1},{5,7},{7,5},{8,10},{10,8},{12,... | collective-permute-start | bytes 196616 | tf_op jit(solution)/shard_map/ppermute | solution.py:35
  48.3 7.5 %collective-permute-start.6 = (bf16[2,128,128]{2,1,0:T(8,128)(2,1)S(1)}, bf16[2,128,128]{2,1,0:T(8,128)(2,1)S(1)}, u32[]{:S(2)}, u32[]{:S(2)}) collective-permute-start(bf16[2,128,128]{2,1,0:T(8,128)(2,1)S(1)} %get-tuple-element.22), channel_id=1, source_target_pairs={{0,4},{2,6},{4,0},{6,2},{1,5},{3,7},{5,1},{7,3},{8,12},{10,14},{12... | collective-permute-start | bytes 196616 | tf_op jit(solution)/shard_map/ppermute | solution.py:35
  51.0 6.2 %collective-permute-start.7 = (bf16[2,128,128]{2,1,0:T(8,128)(2,1)S(1)}, bf16[2,128,128]{2,1,0:T(8,128)(2,1)S(1)}, u32[]{:S(2)}, u32[]{:S(2)}) collective-permute-start(bf16[2,128,128]{2,1,0:T(8,128)(2,1)S(1)} %get-tuple-element.21), channel_id=1, source_target_pairs={{0,6},{2,4},{4,2},{6,0},{1,7},{3,5},{5,3},{7,1},{8,14},{10,12},{12... | collective-permute-start | bytes 196616 | tf_op jit(solution)/shard_map/ppermute | solution.py:35
  51.9 9.9 %collective-permute-start.15 = (bf16[256,256]{1,0:T(8,128)(2,1)S(1)}, bf16[256,256]{1,0:T(8,128)(2,1)S(1)}, u32[]{:S(2)}, u32[]{:S(2)}) collective-permute-start(bf16[256,256]{1,0:T(8,128)(2,1)S(1)} %bitcast_multiply_fusion.refs_4_), channel_id=1, source_target_pairs={{0,8},{8,0},{16,24},{24,16},{1,9},{9,1},{17,25},{25,17},{2,10},{10... | collective-permute-start | bytes 393224 | tf_op jit(solution)/shard_map/ppermute | solution.py:35
  53.4 15.1 %collective-permute-start.16 = (bf16[256,256]{1,0:T(8,128)(2,1)S(1)}, bf16[256,256]{1,0:T(8,128)(2,1)S(1)}, u32[]{:S(2)}, u32[]{:S(2)}) collective-permute-start(bf16[256,256]{1,0:T(8,128)(2,1)S(1)} %bitcast_multiply_fusion.refs_4_), channel_id=1, source_target_pairs={{0,16},{8,24},{16,0},{24,8},{1,17},{9,25},{17,1},{25,9},{2,18},{10... | collective-permute-start | bytes 393224 | tf_op jit(solution)/shard_map/ppermute | solution.py:35
  57.2 6.3 %collective-permute-start.8 = (bf16[2,128,128]{2,1,0:T(8,128)(2,1)S(1)}, bf16[2,128,128]{2,1,0:T(8,128)(2,1)S(1)}, u32[]{:S(2)}, u32[]{:S(2)}) collective-permute-start(bf16[2,128,128]{2,1,0:T(8,128)(2,1)S(1)} %add_convert_fusion.4), channel_id=1, source_target_pairs={{0,2},{2,0},{4,6},{6,4},{1,3},{3,1},{5,7},{7,5},{8,10},{10,8},{12,... | collective-permute-start | bytes 196616 | tf_op jit(solution)/shard_map/ppermute | solution.py:35
  58.0 7.0 %collective-permute-start.9 = (bf16[2,128,128]{2,1,0:T(8,128)(2,1)S(1)}, bf16[2,128,128]{2,1,0:T(8,128)(2,1)S(1)}, u32[]{:S(2)}, u32[]{:S(2)}) collective-permute-start(bf16[2,128,128]{2,1,0:T(8,128)(2,1)S(1)} %add_convert_fusion.4), channel_id=1, source_target_pairs={{0,4},{2,6},{4,0},{6,2},{1,5},{3,7},{5,1},{7,3},{8,12},{10,14},{12... | collective-permute-start | bytes 196616 | tf_op jit(solution)/shard_map/ppermute | solution.py:35
  59.7 6.8 %collective-permute-start.10 = (bf16[2,128,128]{2,1,0:T(8,128)(2,1)S(1)}, bf16[2,128,128]{2,1,0:T(8,128)(2,1)S(1)}, u32[]{:S(2)}, u32[]{:S(2)}) collective-permute-start(bf16[2,128,128]{2,1,0:T(8,128)(2,1)S(1)} %add_convert_fusion.4), channel_id=1, source_target_pairs={{0,6},{2,4},{4,2},{6,0},{1,7},{3,5},{5,3},{7,1},{8,14},{10,12},{12... | collective-permute-start | bytes 196616 | tf_op jit(solution)/shard_map/ppermute | solution.py:35
  61.9 6.7 %collective-permute-start.17 = (bf16[256,256]{1,0:T(8,128)(2,1)S(1)}, bf16[256,256]{1,0:T(8,128)(2,1)S(1)}, u32[]{:S(2)}, u32[]{:S(2)}) collective-permute-start(bf16[256,256]{1,0:T(8,128)(2,1)S(1)} %bitcast_multiply_fusion.refs_4_), channel_id=1, source_target_pairs={{0,24},{8,16},{16,8},{24,0},{1,25},{9,17},{17,9},{25,1},{2,26},{10... | collective-permute-start | bytes 393224 | tf_op jit(solution)/shard_map/ppermute | solution.py:35
  63.5 5.8 %collective-permute-start.12 = (bf16[256,256]{1,0:T(8,128)(2,1)S(1)}, bf16[256,256]{1,0:T(8,128)(2,1)S(1)}, u32[]{:S(2)}, u32[]{:S(2)}) collective-permute-start(bf16[256,256]{1,0:T(8,128)(2,1)S(1)} %bitcast_multiply_fusion.1.refs_0_), channel_id=1, source_target_pairs={{0,2},{2,0},{4,6},{6,4},{1,3},{3,1},{5,7},{7,5},{8,10},{10,8},{12,... | collective-permute-start | bytes 393224 | tf_op jit(solution)/shard_map/ppermute | solution.py:35
  65.0 11.1 %collective-permute-start.13 = (bf16[256,256]{1,0:T(8,128)(2,1)S(1)}, bf16[256,256]{1,0:T(8,128)(2,1)S(1)}, u32[]{:S(2)}, u32[]{:S(2)}) collective-permute-start(bf16[256,256]{1,0:T(8,128)(2,1)S(1)} %bitcast_multiply_fusion.1.refs_0_), channel_id=1, source_target_pairs={{0,4},{2,6},{4,0},{6,2},{1,5},{3,7},{5,1},{7,3},{8,12},{10,14},{12... | collective-permute-start | bytes 393224 | tf_op jit(solution)/shard_map/ppermute | solution.py:35
  66.5 9.6 %collective-permute-start.14 = (bf16[256,256]{1,0:T(8,128)(2,1)S(1)}, bf16[256,256]{1,0:T(8,128)(2,1)S(1)}, u32[]{:S(2)}, u32[]{:S(2)}) collective-permute-start(bf16[256,256]{1,0:T(8,128)(2,1)S(1)} %bitcast_multiply_fusion.1.refs_0_), channel_id=1, source_target_pairs={{0,6},{2,4},{4,2},{6,0},{1,7},{3,5},{5,3},{7,1},{8,14},{10,12},{12... | collective-permute-start | bytes 393224 | tf_op jit(solution)/shard_map/ppermute | solution.py:35
  68.5 16.6 %collective-permute-start.11 = (bf16[4,2,128,128]{3,2,1,0:T(8,128)(2,1)S(1)}, bf16[4,2,128,128]{3,2,1,0:T(8,128)(2,1)S(1)}, u32[]{:S(2)}, u32[]{:S(2)}) collective-permute-start(bf16[4,2,128,128]{3,2,1,0:T(8,128)(2,1)S(1)} %pad_maximum_fusion.own_ref), channel_id=1, source_target_pairs={{0,1},{1,0},{2,3},{3,2},{4,5},{5,4},{6,7},{7,6},{8,9},{9,8},{10,11... | collective-permute-start | bytes 786440 | tf_op jit(solution)/shard_map/ppermute | solution.py:35
  76.5 5.0 %collective-permute-start.18 = (bf16[256,256]{1,0:T(8,128)(2,1)S(1)}, bf16[256,256]{1,0:T(8,128)(2,1)S(1)}, u32[]{:S(2)}, u32[]{:S(2)}) collective-permute-start(bf16[256,256]{1,0:T(8,128)(2,1)S(1)} %product.1.refs_0_), channel_id=1, source_target_pairs={{0,8},{8,0},{16,24},{24,16},{1,9},{9,1},{17,25},{25,17},{2,10},{10... | collective-permute-start | bytes 393224 | tf_op jit(solution)/shard_map/ppermute | solution.py:35
  76.5 6.6 %collective-permute-start.19 = (bf16[256,256]{1,0:T(8,128)(2,1)S(1)}, bf16[256,256]{1,0:T(8,128)(2,1)S(1)}, u32[]{:S(2)}, u32[]{:S(2)}) collective-permute-start(bf16[256,256]{1,0:T(8,128)(2,1)S(1)} %product.1.refs_0_), channel_id=1, source_target_pairs={{0,16},{8,24},{16,0},{24,8},{1,17},{9,25},{17,1},{25,9},{2,18},{10... | collective-permute-start | bytes 393224 | tf_op jit(solution)/shard_map/ppermute | solution.py:35
  79.2 5.9 %collective-permute-start.20 = (bf16[256,256]{1,0:T(8,128)(2,1)S(1)}, bf16[256,256]{1,0:T(8,128)(2,1)S(1)}, u32[]{:S(2)}, u32[]{:S(2)}) collective-permute-start(bf16[256,256]{1,0:T(8,128)(2,1)S(1)} %product.1.refs_0_), channel_id=1, source_target_pairs={{0,24},{8,16},{16,8},{24,0},{1,25},{9,17},{17,9},{25,1},{2,26},{10... | collective-permute-start | bytes 393224 | tf_op jit(solution)/shard_map/ppermute | solution.py:35

commit v3 on v2

--- a/solution.py
+++ b/solution.py
@@ -9,8 +9,7 @@
 
 
 UNROLL = 4
-WORDS = 8
-VMEM_LIMIT = 28 * 1024 * 1024
+VMEM_LIMIT = 36 * 1024 * 1024
 VMEM_MARGIN = 4 * 1024 * 1024
 
 
@@ -47,27 +46,62 @@
     far_layer = target_slot(lax.axis_index("panel"), owner % layers, layers)
     far_col = target_slot(lax.axis_index("col"), (owner // layers) % cols, cols)
     far_row = target_slot(lax.axis_index("row"), owner // (layers * cols), rows)
-    near = far_row == 0
-    at = jnp.where(near, far_layer, far_layer * (rows - 1) + far_row - 1)
-    return near, (at * cols + far_col) * per_owner + block
-
-
-def accumulate(chunk, table, basis, weighted, total):
-    size = basis.shape[2]
-    most = (table.shape[0] - 2 * WORDS) // (2 * WORDS)
+    near = (far_row == 0).astype(jnp.int32)
+    at = jnp.where(near == 1, far_layer, far_layer * (rows - 1) + far_row - 1)
+    return near, (at * cols + far_col) * per_owner + block + 1
+
+
+def across(row):
+    return jnp.broadcast_to(row, (row.shape[1], row.shape[1])).T
+
+
+def most_units(parts, atoms):
+    return (parts + atoms) // 2 + UNROLL
+
+
+def plan(sizes, per_owner, atoms, radix, pairs, owner, block):
+    parts = owner.shape[1]
+    left, right = pairs[0:1, :], pairs[1:2, :]
+    near, slot = place_of(sizes, per_owner, owner, block)
+    key = left + near * atoms
+    lane = lax.broadcasted_iota(jnp.int32, (parts, parts), 1)
+    sublane = lax.broadcasted_iota(jnp.int32, (parts, parts), 0)
+    earlier = (across(key) == key) & (sublane < lane)
+    rank = jnp.sum(earlier.astype(jnp.int32), axis=0, keepdims=True)
+    which = lax.broadcasted_iota(jnp.int32, (2 * atoms, parts), 0)
+    members = jnp.sum((which == key).astype(jnp.int32), axis=1, keepdims=True)
+    units = (members + 1) // 2
+    before = (which < key) & ((which >= atoms) == (near == 1))
+    start = jnp.sum(jnp.where(before, units, 0), axis=0, keepdims=True)
+    entries = 2 * most_units(parts, atoms)
+    at = 2 * start + rank + near * entries
+    width = -(-(2 * entries + 2) // parts) * parts
+    code = (left * radix + right) * radix + slot
+    place = lax.broadcasted_iota(jnp.int32, (parts, width), 1)
+    here = jnp.concatenate([across(at)] * (width // parts), axis=1) == place
+    table = jnp.sum(jnp.where(here, jnp.concatenate([across(code)] * (width // parts), axis=1), 0), axis=0, keepdims=True)
+    far_units = jnp.sum(jnp.where(which[:, 0:1] < atoms, units, 0), axis=0, keepdims=True)
+    near_units = jnp.sum(jnp.where(which[:, 0:1] < atoms, 0, units), axis=0, keepdims=True)
+    place = place[0:1, :]
+    return jnp.where(place == width - 2, far_units, jnp.where(place == width - 1, near_units, table))
+
+
+def accumulate(chunk, entries, radix, table, lefts, weighted, total):
+    size = lefts.shape[1]
 
     def step(i, carry):
         for j in range(UNROLL):
-            at = (chunk * most + i * UNROLL + j) * WORDS
-            rights = jnp.concatenate([weighted[table[at + 1]], weighted[table[at + 2]]], axis=1)
-            found = lax.dot_general(
-                basis[table[at]], rights, (((0,), (0,)), ((), ())), preferred_element_type=jnp.float32
+            at = chunk * entries + 2 * (i * UNROLL + j)
+            one, two = table[0, at], table[0, at + 1]
+            rights = jnp.concatenate(
+                [weighted[(one // radix) % radix], weighted[(two // radix) % radix]], axis=1
             )
-            total[table[at + 3]] += found[:, :size]
-            total[table[at + 4]] += found[:, size:]
+            found = jnp.dot(lefts[one // (radix * radix)], rights, preferred_element_type=jnp.float32)
+            total[one % radix] += found[:, :size]
+            total[two % radix] += found[:, size:]
         return carry
 
-    count = table[(2 * most + chunk) * WORDS]
+    count = table[0, table.shape[1] - 2 + chunk]
     lax.fori_loop(0, (count + UNROLL - 1) // UNROLL, step, 0)
 
 
@@ -83,78 +117,60 @@
     half = keep_ref.shape[0]
 
     def one(i, carry):
-        keep_ref[i] = total[i].astype(jnp.bfloat16)
-        send_ref[i] = total[half + i].astype(jnp.bfloat16)
+        keep_ref[i] = total[i + 1].astype(jnp.bfloat16)
+        send_ref[i] = total[half + i + 1].astype(jnp.bfloat16)
         return carry
 
     lax.fori_loop(0, half, one, 0)
 
 
 def integrate_far_body(
-    sizes, per_owner, trash, pair_ref, owner_ref, block_ref, basis_ref, pot_ref,
-    weighted, table, keep_ref, send_ref, basis, pot_cols, total, pending, arrived,
+    sizes, per_owner, entries, radix, pair_ref, owner_ref, block_ref, basis_ref, pot_ref,
+    lefts, weighted, table_ref, keep_ref, send_ref,
+    pairs, owner, block, pot, basis, pot_cols, total, table, small_sems, arrived,
 ):
     atoms, points, size = basis.shape
-    parts = block_ref.shape[0]
-    most = (table.shape[0] - 2 * WORDS) // (2 * WORDS)
-    radix = pl.next_power_of_2(max(trash) + 1)
+    small = [
+        pltpu.make_async_copy(source_ref, to, small_sems.at[k])
+        for k, (source_ref, to) in enumerate(
+            ((pair_ref, pairs), (owner_ref, owner), (block_ref, block), (pot_ref, pot))
+        )
+    ]
+    for copy in small:
+        copy.start()
 
     def fetch(a):
         return pltpu.make_async_copy(basis_ref.at[a], basis.at[a], arrived.at[a])
 
     for a in range(atoms):
         fetch(a).start()
-    for k in range(2 * atoms):
-        pending[k] = -1
     clear(total)
+    for copy in small:
+        copy.wait()
+    table_ref[...] = plan(sizes, per_owner, atoms, radix, pairs[...], owner[...], block[...])
+    to_scalar = pltpu.make_async_copy(table_ref, table, small_sems.at[4])
+    to_scalar.start()
     for k in range(points // size):
-        row = pot_ref[k : k + 1, :]
-        pot_cols[k * size : (k + 1) * size, :] = jnp.broadcast_to(row, (size, size)).T
-
-    def unit(chunk, count, left, first, second, first_slot, second_slot):
-        at = (jnp.where(chunk, most, 0) + count) * WORDS
-        for k, word in enumerate((left, first, second, first_slot, second_slot)):
-            table[at + k] = word
-
-    def weigh_and_plan(a, counts):
+        pot_cols[k * size : (k + 1) * size, :] = across(pot[k : k + 1, :])
+
+    def weigh(a, carry):
         fetch(a).wait()
         for k in range(points // size):
             at = slice(k * size, (k + 1) * size)
-            weighted[a, at, :] = (basis[a, at, :].astype(jnp.float32) * pot_cols[at, :]).astype(jnp.bfloat16)
-        far_count, near_count = counts
-        for k in range(parts // atoms):
-            n = a * (parts // atoms) + k
-            left, right = pair_ref[0, n], pair_ref[1, n]
-            near, slot = place_of(sizes, per_owner, owner_ref[0, n], block_ref[n])
-            key = left + jnp.where(near, atoms, 0)
-            earlier = pending[key]
-            fresh = earlier < 0
-            pending[key] = jnp.where(fresh, right * radix + slot, -1)
-            unit(near, jnp.where(near, near_count, far_count), left, earlier // radix, right, earlier % radix, slot)
-            far_count += jnp.where(fresh | near, 0, 1)
-            near_count += jnp.where(fresh | jnp.logical_not(near), 0, 1)
-        return far_count, near_count
-
-    counts = lax.fori_loop(0, atoms, weigh_and_plan, (jnp.int32(0), jnp.int32(0)))
-    for chunk in range(2):
-
-        def single(left, count):
-            earlier = pending[chunk * atoms + left]
-            right, slot = earlier // radix, earlier % radix
-            unit(bool(chunk), count, left, right, right, slot, trash[chunk])
-            return count + jnp.where(earlier < 0, 0, 1)
-
-        count = lax.fori_loop(0, atoms, single, counts[chunk])
-        for k in range(UNROLL - 1):
-            unit(bool(chunk), count + k, 0, 0, 0, trash[chunk], trash[chunk])
-        table[(2 * most + chunk) * WORDS] = count
-    accumulate(0, table, basis, weighted, total)
+            values = basis[a, at, :]
+            weighted[a, at, :] = (values.astype(jnp.float32) * pot_cols[at, :]).astype(jnp.bfloat16)
+            lefts[a, :, at] = values.T
+        return carry
+
+    lax.fori_loop(0, atoms, weigh, 0)
+    to_scalar.wait()
+    accumulate(0, entries, radix, table, lefts, weighted, total)
     put(total, keep_ref, send_ref)
 
 
-def integrate_near_body(table, basis, weighted, keep_ref, send_ref, total):
+def integrate_near_body(entries, radix, table, lefts, weighted, keep_ref, send_ref, total):
     clear(total)
-    accumulate(1, table, basis, weighted, total)
+    accumulate(1, entries, radix, table, lefts, weighted, total)
     put(total, keep_ref, send_ref)
 
 
@@ -163,10 +179,12 @@
     parts = target_block.shape[0]
     rows, cols, layers = sizes
     per_row = cols * per_owner
-    trash = layers * (rows - 1) * per_row, layers * per_row
-    most = (parts + atoms) // 2 + UNROLL + 1
-    smem = pl.BlockSpec(memory_space=pltpu.SMEM)
+    far, near = layers * (rows - 1) * per_row, layers * per_row
+    entries = 2 * most_units(parts, atoms)
+    width = -(-(2 * entries + 2) // parts) * parts
+    radix = pl.next_power_of_2(max(far + 1, near + 1, atoms))
     vmem = pl.BlockSpec(memory_space=pltpu.VMEM)
+    hbm = pl.BlockSpec(memory_space=pltpu.HBM)
 
     def half(blocks):
         return jax.ShapeDtypeStruct((blocks // 2, size, size), jnp.bfloat16)
@@ -184,41 +202,50 @@
             ),
         )
 
-    weighted, table, far_keep, far_send = pl.pallas_call(
-        functools.partial(integrate_far_body, sizes, per_owner, trash),
+    def in_hbm(array):
+        return pltpu.with_memory_space_constraint(array, pltpu.HBM)
+
+    lefts, weighted, table, far_keep, far_send = pl.pallas_call(
+        functools.partial(integrate_far_body, sizes, per_owner, entries, radix),
         out_shape=(
-            jax.ShapeDtypeStruct(basis_values.shape, jnp.bfloat16),
-            jax.ShapeDtypeStruct(((2 * most + 2) * WORDS,), jnp.int32),
-            half(trash[0]),
-            half(trash[0]),
+            jax.ShapeDtypeStruct((atoms, size, points), jnp.bfloat16),
+            jax.ShapeDtypeStruct((atoms, points, size), jnp.bfloat16),
+            jax.ShapeDtypeStruct((1, width), jnp.int32),
+            half(far),
+            half(far),
         ),
-        in_specs=[smem, smem, smem, pl.BlockSpec(memory_space=pltpu.HBM), vmem],
-        out_specs=(vmem, smem, vmem, vmem),
+        in_specs=[hbm] * 5,
+        out_specs=(vmem,) * 5,
         scratch_shapes=[
-            pltpu.VMEM(basis_values.shape, jnp.bfloat16),
+            pltpu.VMEM((2, parts), jnp.int32),
+            pltpu.VMEM((1, parts), jnp.int32),
+            pltpu.VMEM((1, parts), jnp.int32),
+            pltpu.VMEM((points // size, size), jnp.float32),
+            pltpu.VMEM((atoms, points, size), jnp.bfloat16),
             pltpu.VMEM((points, size), jnp.float32),
-            total(trash[0]),
-            pltpu.SMEM((2 * atoms,), jnp.int32),
+            total(far),
+            pltpu.SMEM((1, width), jnp.int32),
+            pltpu.SemaphoreType.DMA((5,)),
             pltpu.SemaphoreType.DMA((atoms,)),
         ],
         name="integrate_far",
         **options(1 - 1 / rows),
     )(
-        pair_atoms,
-        target_device.reshape(1, parts),
-        target_block,
-        pltpu.with_memory_space_constraint(basis_values, pltpu.HBM),
-        potential.reshape(points // size, size),
+        in_hbm(pair_atoms),
+        in_hbm(target_device.reshape(1, parts)),
+        in_hbm(target_block.reshape(1, parts)),
+        in_hbm(basis_values),
+        in_hbm(potential.reshape(points // size, size)),
     )
     near_keep, near_send = pl.pallas_call(
-        integrate_near_body,
-        out_shape=(half(trash[1]), half(trash[1])),
-        in_specs=[smem, vmem, vmem],
+        functools.partial(integrate_near_body, entries, radix),
+        out_shape=(half(near), half(near)),
+        in_specs=[pl.BlockSpec(memory_space=pltpu.SMEM), vmem, vmem],
         out_specs=(vmem, vmem),
-        scratch_shapes=[total(trash[1])],
+        scratch_shapes=[total(near)],
         name="integrate_near",
         **options(1 / rows),
-    )(table, basis_values, weighted)
+    )(table, lefts, weighted)
     return far_keep, far_send, near_keep, near_send
 
 

time: 86.3 us -> 80 us (0.927)
  Pallas kernels: 27.7 us -> 24.6 us
  local copies, waits for them, and re-layouts: 2.98 us -> 0.29 us
    pallas_call x2, Pallas kernels: 26.3 us -> 23.2 us  [the longest x1 17.7 us: integrate(): pl.pallas_call(functools.partial(integrate_far_body, sizes, per_owner, en...]
    unnamed x18 -> x8, local copies, waits for them, and re-layouts: 2.71 us -> 0.01 us
  transfers between devices with their start and end apart: 21 -> 21, of which waited for: 11 -> 11; matrix products, arithmetic and copies ran while one was open for 1% -> 1% of each run, Pallas kernels for 8% -> 7%
where the time goes in v3:
time: 80 us; the launch traced here: 79.9 us
  waiting for transfers between devices  30.1 us (38%)
  Pallas kernels  24.6 us (31%)
  starting transfers between devices  24.1 us (30%)
    ppermute x21, waiting for transfers between devices, exchange(): lax.ppermute(value, axis, [(i, target(i, slot, n)) for i in range(n)])  30.1 us
    ppermute x21, starting transfers between devices, exchange(): lax.ppermute(value, axis, [(i, target(i, slot, n)) for i in range(n)])  24.1 us
    pallas_call x1, Pallas kernels, integrate(): pl.pallas_call(functools.partial(integrate_far_body, sizes, per_owner, en...  17.7 us
    pallas_call x1, Pallas kernels, integrate(): pl.pallas_call(functools.partial(integrate_near_body, entries, radix), ou...  5.54 us
  transfers between devices with their start and end apart: 21, of which 11 were waited for; matrix products, arithmetic and copies ran while one was open for 1% of the time, Pallas kernels for 7%

profile of v3, /device:TPU:0, one launch (start us, length us, event | category | flops | bytes accessed | tf_op | source)
XLA Modules:
  0.0 79.9 jit_solution(17431559052128804550)
XLA Ops:
  0.0 17.7 %integrate_far.1 = (bf16[16,128,2048]{2,1,0:T(8,128)(2,1)S(1)}, bf16[16,2048,128]{2,1,0:T(8,128)(2,1)S(1)}, s32[1,384]{1,0:T(1,128)S(1)}, bf16[24,128,128]{2,1,0:T(8,128)(2,1)S(1)}, bf16[24,128,128]{2,1,0:T(8,128)(2,1)S(1)}) custom-call(s32[2,128]{1,0:T(2,128)} %pair_ref.1, s32[1,128]{1,0:T(1,128)} %bitcast.22, s32[1,128]{1,0:T(1,128)} %bitcast.23, ...), custom_call_target="tpu_custom_call" | custom-call | flops 12884901888 | bytes 16777216 | tf_op jit(solution)/shard_map/integrate_far/pallas_call | solution.py:208
  17.7 1.4 %collective-permute-start = (bf16[24,128,128]{2,1,0:T(8,128)(2,1)S(1)}, bf16[24,128,128]{2,1,0:T(8,128)(2,1)S(1)}, u32[]{:S(2)}, u32[]{:S(2)}) collective-permute-start(bf16[24,128,128]{2,1,0:T(8,128)(2,1)S(1)} %get-tuple-element.12), channel_id=1, source_target_pairs={{0,1},{1,0},{2,3},{3,2},{4,5},{5,4},{6,7},{7,6},{8,9},{9,8},{10,11... | collective-permute-start | bytes 2359304 | tf_op jit(solution)/shard_map/ppermute | solution.py:34
  19.0 5.5 %integrate_near.1 = (bf16[8,128,128]{2,1,0:T(8,128)(2,1)S(1)}, bf16[8,128,128]{2,1,0:T(8,128)(2,1)S(1)}) custom-call(s32[1,384]{1,0:T(1,128)S(1)} %get-tuple-element.14.table, bf16[16,128,2048]{2,1,0:T(8,128)(2,1)S(1)} %get-tuple-element.15.lefts, bf16[16,2048,128]{2,1,0:T(8,128)(2,1)S(1)} %get-tuple-element.16.weighted), custom_call_target="tpu_custom_call" | custom-call | flops 4294967296 | bytes 16777216 | tf_op jit(solution)/shard_map/integrate_near/pallas_call | solution.py:240
  24.7 0.3 add_convert_fusion.3
  25.0 1.4 %collective-permute-start.1 = (bf16[8,128,128]{2,1,0:T(8,128)(2,1)S(1)}, bf16[8,128,128]{2,1,0:T(8,128)(2,1)S(1)}, u32[]{:S(2)}, u32[]{:S(2)}) collective-permute-start(bf16[8,128,128]{2,1,0:T(8,128)(2,1)S(1)} %get-tuple-element.19), channel_id=1, source_target_pairs={{0,8},{8,0},{16,24},{24,16},{1,9},{9,1},{17,25},{25,17},{2,10},{10... | collective-permute-start | bytes 786440 | tf_op jit(solution)/shard_map/ppermute | solution.py:34
  26.4 2.5 %collective-permute-start.2 = (bf16[8,128,128]{2,1,0:T(8,128)(2,1)S(1)}, bf16[8,128,128]{2,1,0:T(8,128)(2,1)S(1)}, u32[]{:S(2)}, u32[]{:S(2)}) collective-permute-start(bf16[8,128,128]{2,1,0:T(8,128)(2,1)S(1)} %get-tuple-element.21), channel_id=1, source_target_pairs={{0,16},{8,24},{16,0},{24,8},{1,17},{9,25},{17,1},{25,9},{2,18},{10... | collective-permute-start | bytes 786440 | tf_op jit(solution)/shard_map/ppermute | solution.py:34
  29.0 5.2 %collective-permute-done.1 = bf16[8,128,128]{2,1,0:T(8,128)(2,1)S(1)} collective-permute-done((bf16[8,128,128]{2,1,0:T(8,128)(2,1)S(1)}, bf16[8,128,128]{2,1,0:T(8,128)(2,1)S(1)}, u32[]{:S(2)}, u32[]{:S(2)}) %collective-permute-start.1) | collective-permute-done | bytes 262176 | tf_op jit(solution)/shard_map/ppermute | solution.py:34
  34.2 6.9 %collective-permute-done.2 = bf16[8,128,128]{2,1,0:T(8,128)(2,1)S(1)} collective-permute-done((bf16[8,128,128]{2,1,0:T(8,128)(2,1)S(1)}, bf16[8,128,128]{2,1,0:T(8,128)(2,1)S(1)}, u32[]{:S(2)}, u32[]{:S(2)}) %collective-permute-start.2) | collective-permute-done | bytes 262176 | tf_op jit(solution)/shard_map/ppermute | solution.py:34
  41.3 1.3 %collective-permute-start.5 = (bf16[2,128,128]{2,1,0:T(8,128)(2,1)S(1)}, bf16[2,128,128]{2,1,0:T(8,128)(2,1)S(1)}, u32[]{:S(2)}, u32[]{:S(2)}) collective-permute-start(bf16[2,128,128]{2,1,0:T(8,128)(2,1)S(1)} %get-tuple-element.22), channel_id=1, source_target_pairs={{0,2},{2,0},{4,6},{6,4},{1,3},{3,1},{5,7},{7,5},{8,10},{10,8},{12,... | collective-permute-start | bytes 196616 | tf_op jit(solution)/shard_map/ppermute | solution.py:34
  42.5 2.5 %collective-permute-start.6 = (bf16[2,128,128]{2,1,0:T(8,128)(2,1)S(1)}, bf16[2,128,128]{2,1,0:T(8,128)(2,1)S(1)}, u32[]{:S(2)}, u32[]{:S(2)}) collective-permute-start(bf16[2,128,128]{2,1,0:T(8,128)(2,1)S(1)} %get-tuple-element.24), channel_id=1, source_target_pairs={{0,4},{2,6},{4,0},{6,2},{1,5},{3,7},{5,1},{7,3},{8,12},{10,14},{12... | collective-permute-start | bytes 196616 | tf_op jit(solution)/shard_map/ppermute | solution.py:34
  45.1 0.8 collective-permute-start.7
  46.0 1.4 %collective-permute-start.15 = (bf16[256,256]{1,0:T(8,128)(2,1)S(1)}, bf16[256,256]{1,0:T(8,128)(2,1)S(1)}, u32[]{:S(2)}, u32[]{:S(2)}) collective-permute-start(bf16[256,256]{1,0:T(8,128)(2,1)S(1)} %bitcast_multiply_fusion.refs_4_), channel_id=1, source_target_pairs={{0,8},{8,0},{16,24},{24,16},{1,9},{9,1},{17,25},{25,17},{2,10},{10... | collective-permute-start | bytes 393224 | tf_op jit(solution)/shard_map/ppermute | solution.py:34
  47.4 0.6 collective-permute-start.16
  48.1 1.8 %collective-permute-done.6 = bf16[2,128,128]{2,1,0:T(8,128)(2,1)S(1)} collective-permute-done((bf16[2,128,128]{2,1,0:T(8,128)(2,1)S(1)}, bf16[2,128,128]{2,1,0:T(8,128)(2,1)S(1)}, u32[]{:S(2)}, u32[]{:S(2)}) %collective-permute-start.6) | collective-permute-done | bytes 65568 | tf_op jit(solution)/shard_map/ppermute | solution.py:34
  49.9 1.3 %collective-permute-done.7 = bf16[2,128,128]{2,1,0:T(8,128)(2,1)S(1)} collective-permute-done((bf16[2,128,128]{2,1,0:T(8,128)(2,1)S(1)}, bf16[2,128,128]{2,1,0:T(8,128)(2,1)S(1)}, u32[]{:S(2)}, u32[]{:S(2)}) %collective-permute-start.7) | collective-permute-done | bytes 65568 | tf_op jit(solution)/shard_map/ppermute | solution.py:34
  51.3 0.8 collective-permute-start.8
  52.0 1.7 %collective-permute-start.9 = (bf16[2,128,128]{2,1,0:T(8,128)(2,1)S(1)}, bf16[2,128,128]{2,1,0:T(8,128)(2,1)S(1)}, u32[]{:S(2)}, u32[]{:S(2)}) collective-permute-start(bf16[2,128,128]{2,1,0:T(8,128)(2,1)S(1)} %add_convert_fusion.4), channel_id=1, source_target_pairs={{0,4},{2,6},{4,0},{6,2},{1,5},{3,7},{5,1},{7,3},{8,12},{10,14},{12... | collective-permute-start | bytes 196616 | tf_op jit(solution)/shard_map/ppermute | solution.py:34
  53.8 2.0 %collective-permute-start.10 = (bf16[2,128,128]{2,1,0:T(8,128)(2,1)S(1)}, bf16[2,128,128]{2,1,0:T(8,128)(2,1)S(1)}, u32[]{:S(2)}, u32[]{:S(2)}) collective-permute-start(bf16[2,128,128]{2,1,0:T(8,128)(2,1)S(1)} %add_convert_fusion.4), channel_id=1, source_target_pairs={{0,6},{2,4},{4,2},{6,0},{1,7},{3,5},{5,3},{7,1},{8,14},{10,12},{12... | collective-permute-start | bytes 196616 | tf_op jit(solution)/shard_map/ppermute | solution.py:34
  55.9 1.6 %collective-permute-start.17 = (bf16[256,256]{1,0:T(8,128)(2,1)S(1)}, bf16[256,256]{1,0:T(8,128)(2,1)S(1)}, u32[]{:S(2)}, u32[]{:S(2)}) collective-permute-start(bf16[256,256]{1,0:T(8,128)(2,1)S(1)} %bitcast_multiply_fusion.refs_4_), channel_id=1, source_target_pairs={{0,24},{8,16},{16,8},{24,0},{1,25},{9,17},{17,9},{25,1},{2,26},{10... | collective-permute-start | bytes 393224 | tf_op jit(solution)/shard_map/ppermute | solution.py:34
  57.6 1.5 %collective-permute-done.9 = bf16[2,128,128]{2,1,0:T(8,128)(2,1)S(1)} collective-permute-done((bf16[2,128,128]{2,1,0:T(8,128)(2,1)S(1)}, bf16[2,128,128]{2,1,0:T(8,128)(2,1)S(1)}, u32[]{:S(2)}, u32[]{:S(2)}) %collective-permute-start.9) | collective-permute-done | bytes 65568 | tf_op jit(solution)/shard_map/ppermute | solution.py:34
  59.1 0.5 collective-permute-start.13
  59.6 0.9 %collective-permute-done.10 = bf16[2,128,128]{2,1,0:T(8,128)(2,1)S(1)} collective-permute-done((bf16[2,128,128]{2,1,0:T(8,128)(2,1)S(1)}, bf16[2,128,128]{2,1,0:T(8,128)(2,1)S(1)}, u32[]{:S(2)}, u32[]{:S(2)}) %collective-permute-start.10) | collective-permute-done | bytes 65568 | tf_op jit(solution)/shard_map/ppermute | solution.py:34
  60.6 1.9 %collective-permute-start.14 = (bf16[256,256]{1,0:T(8,128)(2,1)S(1)}, bf16[256,256]{1,0:T(8,128)(2,1)S(1)}, u32[]{:S(2)}, u32[]{:S(2)}) collective-permute-start(bf16[256,256]{1,0:T(8,128)(2,1)S(1)} %bitcast_multiply_fusion.1.refs_0_), channel_id=1, source_target_pairs={{0,6},{2,4},{4,2},{6,0},{1,7},{3,5},{5,3},{7,1},{8,14},{10,12},{12... | collective-permute-start | bytes 393224 | tf_op jit(solution)/shard_map/ppermute | solution.py:34
  62.6 0.7 collective-permute-done.12.refs_1_
  63.3 6.9 %collective-permute-done.13.refs_2_ = bf16[256,256]{1,0:T(8,128)(2,1)S(1)} collective-permute-done((bf16[256,256]{1,0:T(8,128)(2,1)S(1)}, bf16[256,256]{1,0:T(8,128)(2,1)S(1)}, u32[]{:S(2)}, u32[]{:S(2)}) %collective-permute-start.13) | collective-permute-done | bytes 131104 | tf_op jit(solution)/shard_map/ppermute | solution.py:34
  70.2 0.3 product.1.refs_0_
  70.7 2.3 %collective-permute-start.19 = (bf16[256,256]{1,0:T(8,128)(2,1)S(1)}, bf16[256,256]{1,0:T(8,128)(2,1)S(1)}, u32[]{:S(2)}, u32[]{:S(2)}) collective-permute-start(bf16[256,256]{1,0:T(8,128)(2,1)S(1)} %product.1.refs_0_), channel_id=1, source_target_pairs={{0,16},{8,24},{16,0},{24,8},{1,17},{9,25},{17,1},{25,9},{2,18},{10... | collective-permute-start | bytes 393224 | tf_op jit(solution)/shard_map/ppermute | solution.py:34
  73.0 1.2 %collective-permute-start.20 = (bf16[256,256]{1,0:T(8,128)(2,1)S(1)}, bf16[256,256]{1,0:T(8,128)(2,1)S(1)}, u32[]{:S(2)}, u32[]{:S(2)}) collective-permute-start(bf16[256,256]{1,0:T(8,128)(2,1)S(1)} %product.1.refs_0_), channel_id=1, source_target_pairs={{0,24},{8,16},{16,8},{24,0},{1,25},{9,17},{17,9},{25,1},{2,26},{10... | collective-permute-start | bytes 393224 | tf_op jit(solution)/shard_map/ppermute | solution.py:34
  74.1 1.5 %collective-permute-done.18.refs_1_ = bf16[256,256]{1,0:T(8,128)(2,1)S(1)} collective-permute-done((bf16[256,256]{1,0:T(8,128)(2,1)S(1)}, bf16[256,256]{1,0:T(8,128)(2,1)S(1)}, u32[]{:S(2)}, u32[]{:S(2)}) %collective-permute-start.18) | collective-permute-done | bytes 131104 | tf_op jit(solution)/shard_map/ppermute | solution.py:34
  75.6 1.3 %collective-permute-done.19.refs_2_ = bf16[256,256]{1,0:T(8,128)(2,1)S(1)} collective-permute-done((bf16[256,256]{1,0:T(8,128)(2,1)S(1)}, bf16[256,256]{1,0:T(8,128)(2,1)S(1)}, u32[]{:S(2)}, u32[]{:S(2)}) %collective-permute-start.19) | collective-permute-done | bytes 131104 | tf_op jit(solution)/shard_map/ppermute | solution.py:34
  76.9 1.9 %collective-permute-done.20.refs_3_ = bf16[256,256]{1,0:T(8,128)(2,1)S(1)} collective-permute-done((bf16[256,256]{1,0:T(8,128)(2,1)S(1)}, bf16[256,256]{1,0:T(8,128)(2,1)S(1)}, u32[]{:S(2)}, u32[]{:S(2)}) %collective-permute-start.20) | collective-permute-done | bytes 131104 | tf_op jit(solution)/shard_map/ppermute | solution.py:34
  78.8 1.1 %gradient.1 = f32[256,256]{1,0:T(8,128)} custom-call(bf16[4,2,128,128]{3,2,1,0:T(8,128)(2,1)S(1)} %pad_maximum_fusion.own_ref, bf16[4,2,128,128]{3,2,1,0:T(8,128)(2,1)S(1)} %collective-permute-done.11.other_ref, bf16[256,256]{1,0:T(8,128)(2,1)S(1)} %product.1.refs_0_, bf16[256,256]{1,0:T(8,128)(2,1)S(1)} %collective-permute-done.18.refs_1_, ...), custom_call_target="tpu_custom_call" | custom-call | tf_op jit(solution)/shard_map/gradient/pallas_call | solution.py:359
  (33 shorter events, 1.0 us)
Async XLA Ops:
  17.7 7.0 %collective-permute-start = (bf16[24,128,128]{2,1,0:T(8,128)(2,1)S(1)}, bf16[24,128,128]{2,1,0:T(8,128)(2,1)S(1)}, u32[]{:S(2)}, u32[]{:S(2)}) collective-permute-start(bf16[24,128,128]{2,1,0:T(8,128)(2,1)S(1)} %get-tuple-element.12), channel_id=1, source_target_pairs={{0,1},{1,0},{2,3},{3,2},{4,5},{5,4},{6,7},{7,6},{8,9},{9,8},{10,11... | collective-permute-start | bytes 2359304 | tf_op jit(solution)/shard_map/ppermute | solution.py:34
  19.0 9.8 %copy-start.2 = (s32[2,4]{1,0:T(2,128)S(1)}, s32[2,4]{1,0:T(2,128)}, u32[]{:S(2)}) copy-start(s32[2,4]{1,0:T(2,128)} %param.17) | copy-start | bytes 100
  19.0 26.9 %copy-start.1 = (bf16[256,512]{1,0:T(8,128)(2,1)S(1)}, bf16[256,512]{1,0:T(8,128)(2,1)}, u32[]{:S(2)}) copy-start(bf16[256,512]{1,0:T(8,128)(2,1)} %param.16) | copy-start | bytes 786436
  19.0 29.1 %copy-start.3 = (s32[2,2]{1,0:T(2,128)S(1)}, s32[2,2]{1,0:T(2,128)}, u32[]{:S(2)}) copy-start(s32[2,2]{1,0:T(2,128)} %param.15) | copy-start | bytes 52
  19.0 36.9 %copy-start = (bf16[256,256]{1,0:T(8,128)(2,1)S(1)}, bf16[256,256]{1,0:T(8,128)(2,1)}, u32[]{:S(2)}) copy-start(bf16[256,256]{1,0:T(8,128)(2,1)} %param.14) | copy-start | bytes 393220
  24.6 4.3 %collective-permute-start.4 = (bf16[8,128,128]{2,1,0:T(8,128)(2,1)S(1)}, bf16[8,128,128]{2,1,0:T(8,128)(2,1)S(1)}, u32[]{:S(2)}, u32[]{:S(2)}) collective-permute-start(bf16[8,128,128]{2,1,0:T(8,128)(2,1)S(1)} %get-tuple-element.17), channel_id=1, source_target_pairs={{0,1},{1,0},{2,3},{3,2},{4,5},{5,4},{6,7},{7,6},{8,9},{9,8},{10,11... | collective-permute-start | bytes 786440 | tf_op jit(solution)/shard_map/ppermute | solution.py:34
  25.0 9.2 %collective-permute-start.1 = (bf16[8,128,128]{2,1,0:T(8,128)(2,1)S(1)}, bf16[8,128,128]{2,1,0:T(8,128)(2,1)S(1)}, u32[]{:S(2)}, u32[]{:S(2)}) collective-permute-start(bf16[8,128,128]{2,1,0:T(8,128)(2,1)S(1)} %get-tuple-element.19), channel_id=1, source_target_pairs={{0,8},{8,0},{16,24},{24,16},{1,9},{9,1},{17,25},{25,17},{2,10},{10... | collective-permute-start | bytes 786440 | tf_op jit(solution)/shard_map/ppermute | solution.py:34
  26.4 14.8 %collective-permute-start.2 = (bf16[8,128,128]{2,1,0:T(8,128)(2,1)S(1)}, bf16[8,128,128]{2,1,0:T(8,128)(2,1)S(1)}, u32[]{:S(2)}, u32[]{:S(2)}) collective-permute-start(bf16[8,128,128]{2,1,0:T(8,128)(2,1)S(1)} %get-tuple-element.21), channel_id=1, source_target_pairs={{0,16},{8,24},{16,0},{24,8},{1,17},{9,25},{17,1},{25,9},{2,18},{10... | collective-permute-start | bytes 786440 | tf_op jit(solution)/shard_map/ppermute | solution.py:34
  28.8 12.3 %collective-permute-start.3 = (bf16[8,128,128]{2,1,0:T(8,128)(2,1)S(1)}, bf16[8,128,128]{2,1,0:T(8,128)(2,1)S(1)}, u32[]{:S(2)}, u32[]{:S(2)}) collective-permute-start(bf16[8,128,128]{2,1,0:T(8,128)(2,1)S(1)} %get-tuple-element.20), channel_id=1, source_target_pairs={{0,24},{8,16},{16,8},{24,0},{1,25},{9,17},{17,9},{25,1},{2,26},{10... | collective-permute-start | bytes 786440 | tf_op jit(solution)/shard_map/ppermute | solution.py:34
  41.3 6.8 %collective-permute-start.5 = (bf16[2,128,128]{2,1,0:T(8,128)(2,1)S(1)}, bf16[2,128,128]{2,1,0:T(8,128)(2,1)S(1)}, u32[]{:S(2)}, u32[]{:S(2)}) collective-permute-start(bf16[2,128,128]{2,1,0:T(8,128)(2,1)S(1)} %get-tuple-element.22), channel_id=1, source_target_pairs={{0,2},{2,0},{4,6},{6,4},{1,3},{3,1},{5,7},{7,5},{8,10},{10,8},{12,... | collective-permute-start | bytes 196616 | tf_op jit(solution)/shard_map/ppermute | solution.py:34
  42.5 7.3 %collective-permute-start.6 = (bf16[2,128,128]{2,1,0:T(8,128)(2,1)S(1)}, bf16[2,128,128]{2,1,0:T(8,128)(2,1)S(1)}, u32[]{:S(2)}, u32[]{:S(2)}) collective-permute-start(bf16[2,128,128]{2,1,0:T(8,128)(2,1)S(1)} %get-tuple-element.24), channel_id=1, source_target_pairs={{0,4},{2,6},{4,0},{6,2},{1,5},{3,7},{5,1},{7,3},{8,12},{10,14},{12... | collective-permute-start | bytes 196616 | tf_op jit(solution)/shard_map/ppermute | solution.py:34
  45.1 6.2 %collective-permute-start.7 = (bf16[2,128,128]{2,1,0:T(8,128)(2,1)S(1)}, bf16[2,128,128]{2,1,0:T(8,128)(2,1)S(1)}, u32[]{:S(2)}, u32[]{:S(2)}) collective-permute-start(bf16[2,128,128]{2,1,0:T(8,128)(2,1)S(1)} %get-tuple-element.23), channel_id=1, source_target_pairs={{0,6},{2,4},{4,2},{6,0},{1,7},{3,5},{5,3},{7,1},{8,14},{10,12},{12... | collective-permute-start | bytes 196616 | tf_op jit(solution)/shard_map/ppermute | solution.py:34
  46.0 9.9 %collective-permute-start.15 = (bf16[256,256]{1,0:T(8,128)(2,1)S(1)}, bf16[256,256]{1,0:T(8,128)(2,1)S(1)}, u32[]{:S(2)}, u32[]{:S(2)}) collective-permute-start(bf16[256,256]{1,0:T(8,128)(2,1)S(1)} %bitcast_multiply_fusion.refs_4_), channel_id=1, source_target_pairs={{0,8},{8,0},{16,24},{24,16},{1,9},{9,1},{17,25},{25,17},{2,10},{10... | collective-permute-start | bytes 393224 | tf_op jit(solution)/shard_map/ppermute | solution.py:34
  47.4 15.0 %collective-permute-start.16 = (bf16[256,256]{1,0:T(8,128)(2,1)S(1)}, bf16[256,256]{1,0:T(8,128)(2,1)S(1)}, u32[]{:S(2)}, u32[]{:S(2)}) collective-permute-start(bf16[256,256]{1,0:T(8,128)(2,1)S(1)} %bitcast_multiply_fusion.refs_4_), channel_id=1, source_target_pairs={{0,16},{8,24},{16,0},{24,8},{1,17},{9,25},{17,1},{25,9},{2,18},{10... | collective-permute-start | bytes 393224 | tf_op jit(solution)/shard_map/ppermute | solution.py:34
  51.3 6.3 %collective-permute-start.8 = (bf16[2,128,128]{2,1,0:T(8,128)(2,1)S(1)}, bf16[2,128,128]{2,1,0:T(8,128)(2,1)S(1)}, u32[]{:S(2)}, u32[]{:S(2)}) collective-permute-start(bf16[2,128,128]{2,1,0:T(8,128)(2,1)S(1)} %add_convert_fusion.4), channel_id=1, source_target_pairs={{0,2},{2,0},{4,6},{6,4},{1,3},{3,1},{5,7},{7,5},{8,10},{10,8},{12,... | collective-permute-start | bytes 196616 | tf_op jit(solution)/shard_map/ppermute | solution.py:34
  52.0 7.0 %collective-permute-start.9 = (bf16[2,128,128]{2,1,0:T(8,128)(2,1)S(1)}, bf16[2,128,128]{2,1,0:T(8,128)(2,1)S(1)}, u32[]{:S(2)}, u32[]{:S(2)}) collective-permute-start(bf16[2,128,128]{2,1,0:T(8,128)(2,1)S(1)} %add_convert_fusion.4), channel_id=1, source_target_pairs={{0,4},{2,6},{4,0},{6,2},{1,5},{3,7},{5,1},{7,3},{8,12},{10,14},{12... | collective-permute-start | bytes 196616 | tf_op jit(solution)/shard_map/ppermute | solution.py:34
  53.8 6.8 %collective-permute-start.10 = (bf16[2,128,128]{2,1,0:T(8,128)(2,1)S(1)}, bf16[2,128,128]{2,1,0:T(8,128)(2,1)S(1)}, u32[]{:S(2)}, u32[]{:S(2)}) collective-permute-start(bf16[2,128,128]{2,1,0:T(8,128)(2,1)S(1)} %add_convert_fusion.4), channel_id=1, source_target_pairs={{0,6},{2,4},{4,2},{6,0},{1,7},{3,5},{5,3},{7,1},{8,14},{10,12},{12... | collective-permute-start | bytes 196616 | tf_op jit(solution)/shard_map/ppermute | solution.py:34
  55.9 6.6 %collective-permute-start.17 = (bf16[256,256]{1,0:T(8,128)(2,1)S(1)}, bf16[256,256]{1,0:T(8,128)(2,1)S(1)}, u32[]{:S(2)}, u32[]{:S(2)}) collective-permute-start(bf16[256,256]{1,0:T(8,128)(2,1)S(1)} %bitcast_multiply_fusion.refs_4_), channel_id=1, source_target_pairs={{0,24},{8,16},{16,8},{24,0},{1,25},{9,17},{17,9},{25,1},{2,26},{10... | collective-permute-start | bytes 393224 | tf_op jit(solution)/shard_map/ppermute | solution.py:34
  57.6 5.7 %collective-permute-start.12 = (bf16[256,256]{1,0:T(8,128)(2,1)S(1)}, bf16[256,256]{1,0:T(8,128)(2,1)S(1)}, u32[]{:S(2)}, u32[]{:S(2)}) collective-permute-start(bf16[256,256]{1,0:T(8,128)(2,1)S(1)} %bitcast_multiply_fusion.1.refs_0_), channel_id=1, source_target_pairs={{0,2},{2,0},{4,6},{6,4},{1,3},{3,1},{5,7},{7,5},{8,10},{10,8},{12,... | collective-permute-start | bytes 393224 | tf_op jit(solution)/shard_map/ppermute | solution.py:34
  59.1 11.1 %collective-permute-start.13 = (bf16[256,256]{1,0:T(8,128)(2,1)S(1)}, bf16[256,256]{1,0:T(8,128)(2,1)S(1)}, u32[]{:S(2)}, u32[]{:S(2)}) collective-permute-start(bf16[256,256]{1,0:T(8,128)(2,1)S(1)} %bitcast_multiply_fusion.1.refs_0_), channel_id=1, source_target_pairs={{0,4},{2,6},{4,0},{6,2},{1,5},{3,7},{5,1},{7,3},{8,12},{10,14},{12... | collective-permute-start | bytes 393224 | tf_op jit(solution)/shard_map/ppermute | solution.py:34
  60.6 9.7 %collective-permute-start.14 = (bf16[256,256]{1,0:T(8,128)(2,1)S(1)}, bf16[256,256]{1,0:T(8,128)(2,1)S(1)}, u32[]{:S(2)}, u32[]{:S(2)}) collective-permute-start(bf16[256,256]{1,0:T(8,128)(2,1)S(1)} %bitcast_multiply_fusion.1.refs_0_), channel_id=1, source_target_pairs={{0,6},{2,4},{4,2},{6,0},{1,7},{3,5},{5,3},{7,1},{8,14},{10,12},{12... | collective-permute-start | bytes 393224 | tf_op jit(solution)/shard_map/ppermute | solution.py:34
  62.5 16.4 %collective-permute-start.11 = (bf16[4,2,128,128]{3,2,1,0:T(8,128)(2,1)S(1)}, bf16[4,2,128,128]{3,2,1,0:T(8,128)(2,1)S(1)}, u32[]{:S(2)}, u32[]{:S(2)}) collective-permute-start(bf16[4,2,128,128]{3,2,1,0:T(8,128)(2,1)S(1)} %pad_maximum_fusion.own_ref), channel_id=1, source_target_pairs={{0,1},{1,0},{2,3},{3,2},{4,5},{5,4},{6,7},{7,6},{8,9},{9,8},{10,11... | collective-permute-start | bytes 786440 | tf_op jit(solution)/shard_map/ppermute | solution.py:34
  70.6 5.0 %collective-permute-start.18 = (bf16[256,256]{1,0:T(8,128)(2,1)S(1)}, bf16[256,256]{1,0:T(8,128)(2,1)S(1)}, u32[]{:S(2)}, u32[]{:S(2)}) collective-permute-start(bf16[256,256]{1,0:T(8,128)(2,1)S(1)} %product.1.refs_0_), channel_id=1, source_target_pairs={{0,8},{8,0},{16,24},{24,16},{1,9},{9,1},{17,25},{25,17},{2,10},{10... | collective-permute-start | bytes 393224 | tf_op jit(solution)/shard_map/ppermute | solution.py:34
  70.7 6.2 %collective-permute-start.19 = (bf16[256,256]{1,0:T(8,128)(2,1)S(1)}, bf16[256,256]{1,0:T(8,128)(2,1)S(1)}, u32[]{:S(2)}, u32[]{:S(2)}) collective-permute-start(bf16[256,256]{1,0:T(8,128)(2,1)S(1)} %product.1.refs_0_), channel_id=1, source_target_pairs={{0,16},{8,24},{16,0},{24,8},{1,17},{9,25},{17,1},{25,9},{2,18},{10... | collective-permute-start | bytes 393224 | tf_op jit(solution)/shard_map/ppermute | solution.py:34
  73.0 5.9 %collective-permute-start.20 = (bf16[256,256]{1,0:T(8,128)(2,1)S(1)}, bf16[256,256]{1,0:T(8,128)(2,1)S(1)}, u32[]{:S(2)}, u32[]{:S(2)}) collective-permute-start(bf16[256,256]{1,0:T(8,128)(2,1)S(1)} %product.1.refs_0_), channel_id=1, source_target_pairs={{0,24},{8,16},{16,8},{24,0},{1,25},{9,17},{17,9},{25,1},{2,26},{10... | collective-permute-start | bytes 393224 | tf_op jit(solution)/shard_map/ppermute | solution.py:34

commit v4 on v3

--- a/solution.py
+++ b/solution.py
@@ -8,7 +8,8 @@
 from jax.sharding import PartitionSpec as P
 
 
-UNROLL = 4
+UNROLL = 8
+IN_FLIGHT = 6
 VMEM_LIMIT = 36 * 1024 * 1024
 VMEM_MARGIN = 4 * 1024 * 1024
 
@@ -142,7 +143,7 @@
     def fetch(a):
         return pltpu.make_async_copy(basis_ref.at[a], basis.at[a], arrived.at[a])
 
-    for a in range(atoms):
+    for a in range(IN_FLIGHT):
         fetch(a).start()
     clear(total)
     for copy in small:
@@ -155,6 +156,11 @@
 
     def weigh(a, carry):
         fetch(a).wait()
+
+        @pl.when(a + IN_FLIGHT < atoms)
+        def _():
+            fetch(a + IN_FLIGHT).start()
+
         for k in range(points // size):
             at = slice(k * size, (k + 1) * size)
             values = basis[a, at, :]

time: 80 us -> 75.8 us (0.948)
  waiting for transfers between devices: 30.1 us -> 26.4 us
  Pallas kernels: 24.6 us -> 22.1 us
  starting transfers between devices: 24.1 us -> 25.7 us
    ppermute x21, waiting for transfers between devices: 30.1 us -> 26.4 us  [exchange(): lax.ppermute(value, axis, [(i, target(i, slot, n)) for i in range(n)])]
    pallas_call x1, Pallas kernels: 17.7 us -> 15.7 us  [integrate(): pl.pallas_call(functools.partial(integrate_far_body, sizes, per_owner, en...]
    ppermute x21, starting transfers between devices: 24.1 us -> 25.7 us  [exchange(): lax.ppermute(value, axis, [(i, target(i, slot, n)) for i in range(n)])]
  transfers between devices with their start and end apart: 21 -> 21, of which waited for: 11 -> 10; matrix products, arithmetic and copies ran while one was open for 1% -> 1% of each run, Pallas kernels for 7% -> 7%
where the time goes in v4:
time: 75.8 us; the launch traced here: 75.4 us
  waiting for transfers between devices  26.4 us (35%)
  starting transfers between devices  25.7 us (34%)
  Pallas kernels  22.1 us (29%)
    ppermute x21, waiting for transfers between devices, exchange(): lax.ppermute(value, axis, [(i, target(i, slot, n)) for i in range(n)])  26.4 us
    ppermute x21, starting transfers between devices, exchange(): lax.ppermute(value, axis, [(i, target(i, slot, n)) for i in range(n)])  25.7 us
    pallas_call x1, Pallas kernels, integrate(): pl.pallas_call(functools.partial(integrate_far_body, sizes, per_owner, en...  15.7 us
    pallas_call x1, Pallas kernels, integrate(): pl.pallas_call(functools.partial(integrate_near_body, entries, radix), ou...  5 us
  transfers between devices with their start and end apart: 21, of which 10 were waited for; matrix products, arithmetic and copies ran while one was open for 1% of the time, Pallas kernels for 7%

profile of v4, /device:TPU:0, one launch (start us, length us, event | category | flops | bytes accessed | tf_op | source)
XLA Modules:
  0.0 75.4 jit_solution(13975136809377260823)
XLA Ops:
  0.0 15.7 %integrate_far.1 = (bf16[16,128,2048]{2,1,0:T(8,128)(2,1)S(1)}, bf16[16,2048,128]{2,1,0:T(8,128)(2,1)S(1)}, s32[1,384]{1,0:T(1,128)S(1)}, bf16[24,128,128]{2,1,0:T(8,128)(2,1)S(1)}, bf16[24,128,128]{2,1,0:T(8,128)(2,1)S(1)}) custom-call(s32[2,128]{1,0:T(2,128)} %pair_ref.1, s32[1,128]{1,0:T(1,128)} %bitcast.22, s32[1,128]{1,0:T(1,128)} %bitcast.23, ...), custom_call_target="tpu_custom_call" | custom-call | flops 12884901888 | bytes 16777216 | tf_op jit(solution)/shard_map/integrate_far/pallas_call | solution.py:214
  15.7 0.6 collective-permute-start
  16.3 5.0 %integrate_near.1 = (bf16[8,128,128]{2,1,0:T(8,128)(2,1)S(1)}, bf16[8,128,128]{2,1,0:T(8,128)(2,1)S(1)}) custom-call(s32[1,384]{1,0:T(1,128)S(1)} %get-tuple-element.14.table, bf16[16,128,2048]{2,1,0:T(8,128)(2,1)S(1)} %get-tuple-element.15.lefts, bf16[16,2048,128]{2,1,0:T(8,128)(2,1)S(1)} %get-tuple-element.16.weighted), custom_call_target="tpu_custom_call" | custom-call | flops 4294967296 | bytes 16777216 | tf_op jit(solution)/shard_map/integrate_near/pallas_call | solution.py:246
  21.4 0.3 add_convert_fusion.3
  21.7 3.0 %collective-permute-start.1 = (bf16[8,128,128]{2,1,0:T(8,128)(2,1)S(1)}, bf16[8,128,128]{2,1,0:T(8,128)(2,1)S(1)}, u32[]{:S(2)}, u32[]{:S(2)}) collective-permute-start(bf16[8,128,128]{2,1,0:T(8,128)(2,1)S(1)} %get-tuple-element.19), channel_id=1, source_target_pairs={{0,8},{8,0},{16,24},{24,16},{1,9},{9,1},{17,25},{25,17},{2,10},{10... | collective-permute-start | bytes 786440 | tf_op jit(solution)/shard_map/ppermute | solution.py:35
  24.7 1.5 %collective-permute-start.2 = (bf16[8,128,128]{2,1,0:T(8,128)(2,1)S(1)}, bf16[8,128,128]{2,1,0:T(8,128)(2,1)S(1)}, u32[]{:S(2)}, u32[]{:S(2)}) collective-permute-start(bf16[8,128,128]{2,1,0:T(8,128)(2,1)S(1)} %get-tuple-element.21), channel_id=1, source_target_pairs={{0,16},{8,24},{16,0},{24,8},{1,17},{9,25},{17,1},{25,9},{2,18},{10... | collective-permute-start | bytes 786440 | tf_op jit(solution)/shard_map/ppermute | solution.py:35
  26.4 5.5 %collective-permute-done.1 = bf16[8,128,128]{2,1,0:T(8,128)(2,1)S(1)} collective-permute-done((bf16[8,128,128]{2,1,0:T(8,128)(2,1)S(1)}, bf16[8,128,128]{2,1,0:T(8,128)(2,1)S(1)}, u32[]{:S(2)}, u32[]{:S(2)}) %collective-permute-start.1) | collective-permute-done | bytes 262176 | tf_op jit(solution)/shard_map/ppermute | solution.py:35
  31.8 6.4 %collective-permute-done.2 = bf16[8,128,128]{2,1,0:T(8,128)(2,1)S(1)} collective-permute-done((bf16[8,128,128]{2,1,0:T(8,128)(2,1)S(1)}, bf16[8,128,128]{2,1,0:T(8,128)(2,1)S(1)}, u32[]{:S(2)}, u32[]{:S(2)}) %collective-permute-start.2) | collective-permute-done | bytes 262176 | tf_op jit(solution)/shard_map/ppermute | solution.py:35
  38.4 1.6 %collective-permute-start.5 = (bf16[2,128,128]{2,1,0:T(8,128)(2,1)S(1)}, bf16[2,128,128]{2,1,0:T(8,128)(2,1)S(1)}, u32[]{:S(2)}, u32[]{:S(2)}) collective-permute-start(bf16[2,128,128]{2,1,0:T(8,128)(2,1)S(1)} %get-tuple-element.22), channel_id=1, source_target_pairs={{0,2},{2,0},{4,6},{6,4},{1,3},{3,1},{5,7},{7,5},{8,10},{10,8},{12,... | collective-permute-start | bytes 196616 | tf_op jit(solution)/shard_map/ppermute | solution.py:35
  40.0 2.6 %collective-permute-start.6 = (bf16[2,128,128]{2,1,0:T(8,128)(2,1)S(1)}, bf16[2,128,128]{2,1,0:T(8,128)(2,1)S(1)}, u32[]{:S(2)}, u32[]{:S(2)}) collective-permute-start(bf16[2,128,128]{2,1,0:T(8,128)(2,1)S(1)} %get-tuple-element.24), channel_id=1, source_target_pairs={{0,4},{2,6},{4,0},{6,2},{1,5},{3,7},{5,1},{7,3},{8,12},{10,14},{12... | collective-permute-start | bytes 196616 | tf_op jit(solution)/shard_map/ppermute | solution.py:35
  42.6 0.2 collective-permute-start.7
  42.9 0.1 mul.33
  43.1 1.3 %collective-permute-start.15 = (bf16[256,256]{1,0:T(8,128)(2,1)S(1)}, bf16[256,256]{1,0:T(8,128)(2,1)S(1)}, u32[]{:S(2)}, u32[]{:S(2)}) collective-permute-start(bf16[256,256]{1,0:T(8,128)(2,1)S(1)} %bitcast_multiply_fusion.refs_4_), channel_id=1, source_target_pairs={{0,8},{8,0},{16,24},{24,16},{1,9},{9,1},{17,25},{25,17},{2,10},{10... | collective-permute-start | bytes 393224 | tf_op jit(solution)/shard_map/ppermute | solution.py:35
  44.4 0.8 %collective-permute-start.16 = (bf16[256,256]{1,0:T(8,128)(2,1)S(1)}, bf16[256,256]{1,0:T(8,128)(2,1)S(1)}, u32[]{:S(2)}, u32[]{:S(2)}) collective-permute-start(bf16[256,256]{1,0:T(8,128)(2,1)S(1)} %bitcast_multiply_fusion.refs_4_), channel_id=1, source_target_pairs={{0,16},{8,24},{16,0},{24,8},{1,17},{9,25},{17,1},{25,9},{2,18},{10... | collective-permute-start | bytes 393224 | tf_op jit(solution)/shard_map/ppermute | solution.py:35
  45.2 1.4 %collective-permute-done.6 = bf16[2,128,128]{2,1,0:T(8,128)(2,1)S(1)} collective-permute-done((bf16[2,128,128]{2,1,0:T(8,128)(2,1)S(1)}, bf16[2,128,128]{2,1,0:T(8,128)(2,1)S(1)}, u32[]{:S(2)}, u32[]{:S(2)}) %collective-permute-start.6) | collective-permute-done | bytes 65568 | tf_op jit(solution)/shard_map/ppermute | solution.py:35
  46.6 2.4 %collective-permute-done.7 = bf16[2,128,128]{2,1,0:T(8,128)(2,1)S(1)} collective-permute-done((bf16[2,128,128]{2,1,0:T(8,128)(2,1)S(1)}, bf16[2,128,128]{2,1,0:T(8,128)(2,1)S(1)}, u32[]{:S(2)}, u32[]{:S(2)}) %collective-permute-start.7) | collective-permute-done | bytes 65568 | tf_op jit(solution)/shard_map/ppermute | solution.py:35
  49.2 1.2 %collective-permute-start.9 = (bf16[2,128,128]{2,1,0:T(8,128)(2,1)S(1)}, bf16[2,128,128]{2,1,0:T(8,128)(2,1)S(1)}, u32[]{:S(2)}, u32[]{:S(2)}) collective-permute-start(bf16[2,128,128]{2,1,0:T(8,128)(2,1)S(1)} %add_convert_fusion.4), channel_id=1, source_target_pairs={{0,4},{2,6},{4,0},{6,2},{1,5},{3,7},{5,1},{7,3},{8,12},{10,14},{12... | collective-permute-start | bytes 196616 | tf_op jit(solution)/shard_map/ppermute | solution.py:35
  50.3 3.2 %collective-permute-start.10 = (bf16[2,128,128]{2,1,0:T(8,128)(2,1)S(1)}, bf16[2,128,128]{2,1,0:T(8,128)(2,1)S(1)}, u32[]{:S(2)}, u32[]{:S(2)}) collective-permute-start(bf16[2,128,128]{2,1,0:T(8,128)(2,1)S(1)} %add_convert_fusion.4), channel_id=1, source_target_pairs={{0,6},{2,4},{4,2},{6,0},{1,7},{3,5},{5,3},{7,1},{8,14},{10,12},{12... | collective-permute-start | bytes 196616 | tf_op jit(solution)/shard_map/ppermute | solution.py:35
  53.7 1.6 %collective-permute-start.17 = (bf16[256,256]{1,0:T(8,128)(2,1)S(1)}, bf16[256,256]{1,0:T(8,128)(2,1)S(1)}, u32[]{:S(2)}, u32[]{:S(2)}) collective-permute-start(bf16[256,256]{1,0:T(8,128)(2,1)S(1)} %bitcast_multiply_fusion.refs_4_), channel_id=1, source_target_pairs={{0,24},{8,16},{16,8},{24,0},{1,25},{9,17},{17,9},{25,1},{2,26},{10... | collective-permute-start | bytes 393224 | tf_op jit(solution)/shard_map/ppermute | solution.py:35
  55.3 1.2 %collective-permute-start.13 = (bf16[256,256]{1,0:T(8,128)(2,1)S(1)}, bf16[256,256]{1,0:T(8,128)(2,1)S(1)}, u32[]{:S(2)}, u32[]{:S(2)}) collective-permute-start(bf16[256,256]{1,0:T(8,128)(2,1)S(1)} %bitcast_multiply_fusion.1.refs_0_), channel_id=1, source_target_pairs={{0,4},{2,6},{4,0},{6,2},{1,5},{3,7},{5,1},{7,3},{8,12},{10,14},{12... | collective-permute-start | bytes 393224 | tf_op jit(solution)/shard_map/ppermute | solution.py:35
  56.5 0.7 collective-permute-done.10
  57.1 3.1 %collective-permute-start.14 = (bf16[256,256]{1,0:T(8,128)(2,1)S(1)}, bf16[256,256]{1,0:T(8,128)(2,1)S(1)}, u32[]{:S(2)}, u32[]{:S(2)}) collective-permute-start(bf16[256,256]{1,0:T(8,128)(2,1)S(1)} %bitcast_multiply_fusion.1.refs_0_), channel_id=1, source_target_pairs={{0,6},{2,4},{4,2},{6,0},{1,7},{3,5},{5,3},{7,1},{8,14},{10,12},{12... | collective-permute-start | bytes 393224 | tf_op jit(solution)/shard_map/ppermute | solution.py:35
  60.4 2.2 %collective-permute-done.12.refs_1_ = bf16[256,256]{1,0:T(8,128)(2,1)S(1)} collective-permute-done((bf16[256,256]{1,0:T(8,128)(2,1)S(1)}, bf16[256,256]{1,0:T(8,128)(2,1)S(1)}, u32[]{:S(2)}, u32[]{:S(2)}) %collective-permute-start.12) | collective-permute-done | bytes 131104 | tf_op jit(solution)/shard_map/ppermute | solution.py:35
  62.6 3.3 %collective-permute-done.13.refs_2_ = bf16[256,256]{1,0:T(8,128)(2,1)S(1)} collective-permute-done((bf16[256,256]{1,0:T(8,128)(2,1)S(1)}, bf16[256,256]{1,0:T(8,128)(2,1)S(1)}, u32[]{:S(2)}, u32[]{:S(2)}) %collective-permute-start.13) | collective-permute-done | bytes 131104 | tf_op jit(solution)/shard_map/ppermute | solution.py:35
  65.9 0.3 product.1.refs_0_
  66.3 1.5 %collective-permute-start.18 = (bf16[256,256]{1,0:T(8,128)(2,1)S(1)}, bf16[256,256]{1,0:T(8,128)(2,1)S(1)}, u32[]{:S(2)}, u32[]{:S(2)}) collective-permute-start(bf16[256,256]{1,0:T(8,128)(2,1)S(1)} %product.1.refs_0_), channel_id=1, source_target_pairs={{0,8},{8,0},{16,24},{24,16},{1,9},{9,1},{17,25},{25,17},{2,10},{10... | collective-permute-start | bytes 393224 | tf_op jit(solution)/shard_map/ppermute | solution.py:35
  67.8 0.6 collective-permute-start.19
  68.4 1.4 %collective-permute-start.20 = (bf16[256,256]{1,0:T(8,128)(2,1)S(1)}, bf16[256,256]{1,0:T(8,128)(2,1)S(1)}, u32[]{:S(2)}, u32[]{:S(2)}) collective-permute-start(bf16[256,256]{1,0:T(8,128)(2,1)S(1)} %product.1.refs_0_), channel_id=1, source_target_pairs={{0,24},{8,16},{16,8},{24,0},{1,25},{9,17},{17,9},{25,1},{2,26},{10... | collective-permute-start | bytes 393224 | tf_op jit(solution)/shard_map/ppermute | solution.py:35
  69.9 1.8 %collective-permute-done.18.refs_1_ = bf16[256,256]{1,0:T(8,128)(2,1)S(1)} collective-permute-done((bf16[256,256]{1,0:T(8,128)(2,1)S(1)}, bf16[256,256]{1,0:T(8,128)(2,1)S(1)}, u32[]{:S(2)}, u32[]{:S(2)}) %collective-permute-start.18) | collective-permute-done | bytes 131104 | tf_op jit(solution)/shard_map/ppermute | solution.py:35
  71.7 1.3 %collective-permute-done.19.refs_2_ = bf16[256,256]{1,0:T(8,128)(2,1)S(1)} collective-permute-done((bf16[256,256]{1,0:T(8,128)(2,1)S(1)}, bf16[256,256]{1,0:T(8,128)(2,1)S(1)}, u32[]{:S(2)}, u32[]{:S(2)}) %collective-permute-start.19) | collective-permute-done | bytes 131104 | tf_op jit(solution)/shard_map/ppermute | solution.py:35
  72.9 1.4 %collective-permute-done.20.refs_3_ = bf16[256,256]{1,0:T(8,128)(2,1)S(1)} collective-permute-done((bf16[256,256]{1,0:T(8,128)(2,1)S(1)}, bf16[256,256]{1,0:T(8,128)(2,1)S(1)}, u32[]{:S(2)}, u32[]{:S(2)}) %collective-permute-start.20) | collective-permute-done | bytes 131104 | tf_op jit(solution)/shard_map/ppermute | solution.py:35
  74.3 1.1 %gradient.1 = f32[256,256]{1,0:T(8,128)} custom-call(bf16[4,2,128,128]{3,2,1,0:T(8,128)(2,1)S(1)} %pad_maximum_fusion.own_ref, bf16[4,2,128,128]{3,2,1,0:T(8,128)(2,1)S(1)} %collective-permute-done.11.other_ref, bf16[256,256]{1,0:T(8,128)(2,1)S(1)} %product.1.refs_0_, bf16[256,256]{1,0:T(8,128)(2,1)S(1)} %collective-permute-done.18.refs_1_, ...), custom_call_target="tpu_custom_call" | custom-call | tf_op jit(solution)/shard_map/gradient/pallas_call | solution.py:365
  (33 shorter events, 0.9 us)
Async XLA Ops:
  15.7 5.7 %collective-permute-start = (bf16[24,128,128]{2,1,0:T(8,128)(2,1)S(1)}, bf16[24,128,128]{2,1,0:T(8,128)(2,1)S(1)}, u32[]{:S(2)}, u32[]{:S(2)}) collective-permute-start(bf16[24,128,128]{2,1,0:T(8,128)(2,1)S(1)} %get-tuple-element.12), channel_id=1, source_target_pairs={{0,1},{1,0},{2,3},{3,2},{4,5},{5,4},{6,7},{7,6},{8,9},{9,8},{10,11... | collective-permute-start | bytes 2359304 | tf_op jit(solution)/shard_map/ppermute | solution.py:35
  16.3 10.0 %copy-start.2 = (s32[2,4]{1,0:T(2,128)S(1)}, s32[2,4]{1,0:T(2,128)}, u32[]{:S(2)}) copy-start(s32[2,4]{1,0:T(2,128)} %param.17) | copy-start | bytes 100
  16.3 26.7 %copy-start.1 = (bf16[256,512]{1,0:T(8,128)(2,1)S(1)}, bf16[256,512]{1,0:T(8,128)(2,1)}, u32[]{:S(2)}) copy-start(bf16[256,512]{1,0:T(8,128)(2,1)} %param.16) | copy-start | bytes 786436
  16.3 28.9 %copy-start.3 = (s32[2,2]{1,0:T(2,128)S(1)}, s32[2,2]{1,0:T(2,128)}, u32[]{:S(2)}) copy-start(s32[2,2]{1,0:T(2,128)} %param.15) | copy-start | bytes 52
  16.3 37.4 %copy-start = (bf16[256,256]{1,0:T(8,128)(2,1)S(1)}, bf16[256,256]{1,0:T(8,128)(2,1)}, u32[]{:S(2)}) copy-start(bf16[256,256]{1,0:T(8,128)(2,1)} %param.14) | copy-start | bytes 393220
  21.3 5.0 %collective-permute-start.4 = (bf16[8,128,128]{2,1,0:T(8,128)(2,1)S(1)}, bf16[8,128,128]{2,1,0:T(8,128)(2,1)S(1)}, u32[]{:S(2)}, u32[]{:S(2)}) collective-permute-start(bf16[8,128,128]{2,1,0:T(8,128)(2,1)S(1)} %get-tuple-element.17), channel_id=1, source_target_pairs={{0,1},{1,0},{2,3},{3,2},{4,5},{5,4},{6,7},{7,6},{8,9},{9,8},{10,11... | collective-permute-start | bytes 786440 | tf_op jit(solution)/shard_map/ppermute | solution.py:35
  21.7 10.2 %collective-permute-start.1 = (bf16[8,128,128]{2,1,0:T(8,128)(2,1)S(1)}, bf16[8,128,128]{2,1,0:T(8,128)(2,1)S(1)}, u32[]{:S(2)}, u32[]{:S(2)}) collective-permute-start(bf16[8,128,128]{2,1,0:T(8,128)(2,1)S(1)} %get-tuple-element.19), channel_id=1, source_target_pairs={{0,8},{8,0},{16,24},{24,16},{1,9},{9,1},{17,25},{25,17},{2,10},{10... | collective-permute-start | bytes 786440 | tf_op jit(solution)/shard_map/ppermute | solution.py:35
  24.7 13.6 %collective-permute-start.2 = (bf16[8,128,128]{2,1,0:T(8,128)(2,1)S(1)}, bf16[8,128,128]{2,1,0:T(8,128)(2,1)S(1)}, u32[]{:S(2)}, u32[]{:S(2)}) collective-permute-start(bf16[8,128,128]{2,1,0:T(8,128)(2,1)S(1)} %get-tuple-element.21), channel_id=1, source_target_pairs={{0,16},{8,24},{16,0},{24,8},{1,17},{9,25},{17,1},{25,9},{2,18},{10... | collective-permute-start | bytes 786440 | tf_op jit(solution)/shard_map/ppermute | solution.py:35
  26.2 12.1 %collective-permute-start.3 = (bf16[8,128,128]{2,1,0:T(8,128)(2,1)S(1)}, bf16[8,128,128]{2,1,0:T(8,128)(2,1)S(1)}, u32[]{:S(2)}, u32[]{:S(2)}) collective-permute-start(bf16[8,128,128]{2,1,0:T(8,128)(2,1)S(1)} %get-tuple-element.20), channel_id=1, source_target_pairs={{0,24},{8,16},{16,8},{24,0},{1,25},{9,17},{17,9},{25,1},{2,26},{10... | collective-permute-start | bytes 786440 | tf_op jit(solution)/shard_map/ppermute | solution.py:35
  38.4 6.8 %collective-permute-start.5 = (bf16[2,128,128]{2,1,0:T(8,128)(2,1)S(1)}, bf16[2,128,128]{2,1,0:T(8,128)(2,1)S(1)}, u32[]{:S(2)}, u32[]{:S(2)}) collective-permute-start(bf16[2,128,128]{2,1,0:T(8,128)(2,1)S(1)} %get-tuple-element.22), channel_id=1, source_target_pairs={{0,2},{2,0},{4,6},{6,4},{1,3},{3,1},{5,7},{7,5},{8,10},{10,8},{12,... | collective-permute-start | bytes 196616 | tf_op jit(solution)/shard_map/ppermute | solution.py:35
  40.0 6.6 %collective-permute-start.6 = (bf16[2,128,128]{2,1,0:T(8,128)(2,1)S(1)}, bf16[2,128,128]{2,1,0:T(8,128)(2,1)S(1)}, u32[]{:S(2)}, u32[]{:S(2)}) collective-permute-start(bf16[2,128,128]{2,1,0:T(8,128)(2,1)S(1)} %get-tuple-element.24), channel_id=1, source_target_pairs={{0,4},{2,6},{4,0},{6,2},{1,5},{3,7},{5,1},{7,3},{8,12},{10,14},{12... | collective-permute-start | bytes 196616 | tf_op jit(solution)/shard_map/ppermute | solution.py:35
  42.6 6.4 %collective-permute-start.7 = (bf16[2,128,128]{2,1,0:T(8,128)(2,1)S(1)}, bf16[2,128,128]{2,1,0:T(8,128)(2,1)S(1)}, u32[]{:S(2)}, u32[]{:S(2)}) collective-permute-start(bf16[2,128,128]{2,1,0:T(8,128)(2,1)S(1)} %get-tuple-element.23), channel_id=1, source_target_pairs={{0,6},{2,4},{4,2},{6,0},{1,7},{3,5},{5,3},{7,1},{8,14},{10,12},{12... | collective-permute-start | bytes 196616 | tf_op jit(solution)/shard_map/ppermute | solution.py:35
  43.1 10.7 %collective-permute-start.15 = (bf16[256,256]{1,0:T(8,128)(2,1)S(1)}, bf16[256,256]{1,0:T(8,128)(2,1)S(1)}, u32[]{:S(2)}, u32[]{:S(2)}) collective-permute-start(bf16[256,256]{1,0:T(8,128)(2,1)S(1)} %bitcast_multiply_fusion.refs_4_), channel_id=1, source_target_pairs={{0,8},{8,0},{16,24},{24,16},{1,9},{9,1},{17,25},{25,17},{2,10},{10... | collective-permute-start | bytes 393224 | tf_op jit(solution)/shard_map/ppermute | solution.py:35
  44.4 16.0 %collective-permute-start.16 = (bf16[256,256]{1,0:T(8,128)(2,1)S(1)}, bf16[256,256]{1,0:T(8,128)(2,1)S(1)}, u32[]{:S(2)}, u32[]{:S(2)}) collective-permute-start(bf16[256,256]{1,0:T(8,128)(2,1)S(1)} %bitcast_multiply_fusion.refs_4_), channel_id=1, source_target_pairs={{0,16},{8,24},{16,0},{24,8},{1,17},{9,25},{17,1},{25,9},{2,18},{10... | collective-permute-start | bytes 393224 | tf_op jit(solution)/shard_map/ppermute | solution.py:35
  49.1 6.2 %collective-permute-start.8 = (bf16[2,128,128]{2,1,0:T(8,128)(2,1)S(1)}, bf16[2,128,128]{2,1,0:T(8,128)(2,1)S(1)}, u32[]{:S(2)}, u32[]{:S(2)}) collective-permute-start(bf16[2,128,128]{2,1,0:T(8,128)(2,1)S(1)} %add_convert_fusion.4), channel_id=1, source_target_pairs={{0,2},{2,0},{4,6},{6,4},{1,3},{3,1},{5,7},{7,5},{8,10},{10,8},{12,... | collective-permute-start | bytes 196616 | tf_op jit(solution)/shard_map/ppermute | solution.py:35
  49.2 6.1 %collective-permute-start.9 = (bf16[2,128,128]{2,1,0:T(8,128)(2,1)S(1)}, bf16[2,128,128]{2,1,0:T(8,128)(2,1)S(1)}, u32[]{:S(2)}, u32[]{:S(2)}) collective-permute-start(bf16[2,128,128]{2,1,0:T(8,128)(2,1)S(1)} %add_convert_fusion.4), channel_id=1, source_target_pairs={{0,4},{2,6},{4,0},{6,2},{1,5},{3,7},{5,1},{7,3},{8,12},{10,14},{12... | collective-permute-start | bytes 196616 | tf_op jit(solution)/shard_map/ppermute | solution.py:35
  50.3 6.8 %collective-permute-start.10 = (bf16[2,128,128]{2,1,0:T(8,128)(2,1)S(1)}, bf16[2,128,128]{2,1,0:T(8,128)(2,1)S(1)}, u32[]{:S(2)}, u32[]{:S(2)}) collective-permute-start(bf16[2,128,128]{2,1,0:T(8,128)(2,1)S(1)} %add_convert_fusion.4), channel_id=1, source_target_pairs={{0,6},{2,4},{4,2},{6,0},{1,7},{3,5},{5,3},{7,1},{8,14},{10,12},{12... | collective-permute-start | bytes 196616 | tf_op jit(solution)/shard_map/ppermute | solution.py:35
  53.7 6.7 %collective-permute-start.17 = (bf16[256,256]{1,0:T(8,128)(2,1)S(1)}, bf16[256,256]{1,0:T(8,128)(2,1)S(1)}, u32[]{:S(2)}, u32[]{:S(2)}) collective-permute-start(bf16[256,256]{1,0:T(8,128)(2,1)S(1)} %bitcast_multiply_fusion.refs_4_), channel_id=1, source_target_pairs={{0,24},{8,16},{16,8},{24,0},{1,25},{9,17},{17,9},{25,1},{2,26},{10... | collective-permute-start | bytes 393224 | tf_op jit(solution)/shard_map/ppermute | solution.py:35
  55.3 7.4 %collective-permute-start.12 = (bf16[256,256]{1,0:T(8,128)(2,1)S(1)}, bf16[256,256]{1,0:T(8,128)(2,1)S(1)}, u32[]{:S(2)}, u32[]{:S(2)}) collective-permute-start(bf16[256,256]{1,0:T(8,128)(2,1)S(1)} %bitcast_multiply_fusion.1.refs_0_), channel_id=1, source_target_pairs={{0,2},{2,0},{4,6},{6,4},{1,3},{3,1},{5,7},{7,5},{8,10},{10,8},{12,... | collective-permute-start | bytes 393224 | tf_op jit(solution)/shard_map/ppermute | solution.py:35
  55.3 10.7 %collective-permute-start.13 = (bf16[256,256]{1,0:T(8,128)(2,1)S(1)}, bf16[256,256]{1,0:T(8,128)(2,1)S(1)}, u32[]{:S(2)}, u32[]{:S(2)}) collective-permute-start(bf16[256,256]{1,0:T(8,128)(2,1)S(1)} %bitcast_multiply_fusion.1.refs_0_), channel_id=1, source_target_pairs={{0,4},{2,6},{4,0},{6,2},{1,5},{3,7},{5,1},{7,3},{8,12},{10,14},{12... | collective-permute-start | bytes 393224 | tf_op jit(solution)/shard_map/ppermute | solution.py:35
  57.1 8.8 %collective-permute-start.14 = (bf16[256,256]{1,0:T(8,128)(2,1)S(1)}, bf16[256,256]{1,0:T(8,128)(2,1)S(1)}, u32[]{:S(2)}, u32[]{:S(2)}) collective-permute-start(bf16[256,256]{1,0:T(8,128)(2,1)S(1)} %bitcast_multiply_fusion.1.refs_0_), channel_id=1, source_target_pairs={{0,6},{2,4},{4,2},{6,0},{1,7},{3,5},{5,3},{7,1},{8,14},{10,12},{12... | collective-permute-start | bytes 393224 | tf_op jit(solution)/shard_map/ppermute | solution.py:35
  60.3 14.0 %collective-permute-start.11 = (bf16[4,2,128,128]{3,2,1,0:T(8,128)(2,1)S(1)}, bf16[4,2,128,128]{3,2,1,0:T(8,128)(2,1)S(1)}, u32[]{:S(2)}, u32[]{:S(2)}) collective-permute-start(bf16[4,2,128,128]{3,2,1,0:T(8,128)(2,1)S(1)} %pad_maximum_fusion.own_ref), channel_id=1, source_target_pairs={{0,1},{1,0},{2,3},{3,2},{4,5},{5,4},{6,7},{7,6},{8,9},{9,8},{10,11... | collective-permute-start | bytes 786440 | tf_op jit(solution)/shard_map/ppermute | solution.py:35
  66.3 5.4 %collective-permute-start.18 = (bf16[256,256]{1,0:T(8,128)(2,1)S(1)}, bf16[256,256]{1,0:T(8,128)(2,1)S(1)}, u32[]{:S(2)}, u32[]{:S(2)}) collective-permute-start(bf16[256,256]{1,0:T(8,128)(2,1)S(1)} %product.1.refs_0_), channel_id=1, source_target_pairs={{0,8},{8,0},{16,24},{24,16},{1,9},{9,1},{17,25},{25,17},{2,10},{10... | collective-permute-start | bytes 393224 | tf_op jit(solution)/shard_map/ppermute | solution.py:35
  67.8 5.1 %collective-permute-start.19 = (bf16[256,256]{1,0:T(8,128)(2,1)S(1)}, bf16[256,256]{1,0:T(8,128)(2,1)S(1)}, u32[]{:S(2)}, u32[]{:S(2)}) collective-permute-start(bf16[256,256]{1,0:T(8,128)(2,1)S(1)} %product.1.refs_0_), channel_id=1, source_target_pairs={{0,16},{8,24},{16,0},{24,8},{1,17},{9,25},{17,1},{25,9},{2,18},{10... | collective-permute-start | bytes 393224 | tf_op jit(solution)/shard_map/ppermute | solution.py:35
  68.4 5.9 %collective-permute-start.20 = (bf16[256,256]{1,0:T(8,128)(2,1)S(1)}, bf16[256,256]{1,0:T(8,128)(2,1)S(1)}, u32[]{:S(2)}, u32[]{:S(2)}) collective-permute-start(bf16[256,256]{1,0:T(8,128)(2,1)S(1)} %product.1.refs_0_), channel_id=1, source_target_pairs={{0,24},{8,16},{16,8},{24,0},{1,25},{9,17},{17,9},{25,1},{2,26},{10... | collective-permute-start | bytes 393224 | tf_op jit(solution)/shard_map/ppermute | solution.py:35

commit v5 on v4

--- a/solution.py
+++ b/solution.py
@@ -9,6 +9,7 @@
 
 
 UNROLL = 8
+REST = 2
 IN_FLIGHT = 6
 VMEM_LIMIT = 36 * 1024 * 1024
 VMEM_MARGIN = 4 * 1024 * 1024
@@ -90,9 +91,9 @@
 def accumulate(chunk, entries, radix, table, lefts, weighted, total):
     size = lefts.shape[1]
 
-    def step(i, carry):
-        for j in range(UNROLL):
-            at = chunk * entries + 2 * (i * UNROLL + j)
+    def units(first, number):
+        for j in range(number):
+            at = chunk * entries + 2 * (first + j)
             one, two = table[0, at], table[0, at + 1]
             rights = jnp.concatenate(
                 [weighted[(one // radix) % radix], weighted[(two // radix) % radix]], axis=1
@@ -100,10 +101,19 @@
             found = jnp.dot(lefts[one // (radix * radix)], rights, preferred_element_type=jnp.float32)
             total[one % radix] += found[:, :size]
             total[two % radix] += found[:, size:]
+
+    def many(i, carry):
+        units(i * UNROLL, UNROLL)
         return carry
 
+    def few(i, carry):
+        units(whole * UNROLL + i * REST, REST)
+        return carry
+
     count = table[0, table.shape[1] - 2 + chunk]
-    lax.fori_loop(0, (count + UNROLL - 1) // UNROLL, step, 0)
+    whole = count // UNROLL
+    lax.fori_loop(0, whole, many, 0)
+    lax.fori_loop(0, (count - whole * UNROLL + REST - 1) // REST, few, 0)
 
 
 def clear(total):
@@ -292,18 +302,21 @@
     )(*lefts, *rights)
 
 
-def gradient_body(count, own_ref, other_ref, *refs):
-    rights, out, stacked = refs[:count], refs[-2], refs[-1]
+def gradient_body(pieces, count, *refs):
+    number = len(pieces)
+    own, other, rights = refs[:number], refs[number : 2 * number], refs[2 * number : 2 * number + count]
+    out, stacked = refs[-2:]
     for s in range(count):
         stacked[s] = rights[s][...]
-    blocks, size = own_ref.shape[1], own_ref.shape[2]
+    blocks, size = own[0].shape[1], own[0].shape[2]
     row, col, side = lax.axis_index("row"), lax.axis_index("col"), lax.axis_index("panel")
-    for which, ref in ((side, own_ref), (1 - side, other_ref)):
+    for which, parts in ((side, own), (1 - side, other)):
         found = None
-        for s in range(count):
-            left = jnp.concatenate([ref[s, b] for b in range(blocks)], axis=1)
-            term = jnp.dot(left, stacked[index_of(row, col, s, count)], preferred_element_type=jnp.float32)
-            found = term if found is None else found + term
+        for slots, part in zip(pieces, parts):
+            for k, s in enumerate(slots):
+                left = jnp.concatenate([part[k, b] for b in range(blocks)], axis=1)
+                term = jnp.dot(left, stacked[index_of(row, col, s, count)], preferred_element_type=jnp.float32)
+                found = term if found is None else found + term
         out[pl.ds(which * size, size), :] = found
 
 
@@ -357,20 +370,32 @@
         added(*[p[s * per_owner : (s + 1) * per_owner] for p in [parts[0]] + got]).astype(jnp.bfloat16)
         for s in range(cols)
     ]
-    got = [exchange(parts[s], "col", s) for s in range(1, cols)]
-    mine = added(parts[0], *got).astype(jnp.bfloat16)
-    line = jnp.stack([mine] + [exchange(mine, "col", s) for s in range(1, cols)])
-    other = exchange(line, "panel", 1)
+    steps = [1 << k for k in range((cols - 1).bit_length())]
+    live = dict(enumerate(parts))
+    for step in steps[:-1]:
+        kept = [s for s in live if not s & step]
+        got = exchange(jnp.stack([live[s | step] for s in kept]), "col", step)
+        live = {s: added(live[s], got[k]).astype(jnp.bfloat16) for k, s in enumerate(kept)}
+    slots = list(live)
+    got = exchange(jnp.stack([live[s] for s in slots]), "col", steps[-1])
+    here = jnp.stack([added(live[s], got[slots.index(s ^ steps[-1])]).astype(jnp.bfloat16) for s in slots])
+    pieces, own, other = [slots], [here], []
+    for step in reversed(steps[:-1]):
+        sent = own[0] if len(own) == 1 else jnp.concatenate(own)
+        got = exchange(sent, "col", step)
+        own.append(got)
+        pieces.append([s | step for slots in pieces for s in slots])
+    other = [exchange(piece, "panel", 1) for piece in own]
     vmem = pl.BlockSpec(memory_space=pltpu.VMEM)
     return pl.pallas_call(
-        functools.partial(gradient_body, cols),
+        functools.partial(gradient_body, pieces, cols),
         out_shape=jax.ShapeDtypeStruct((layers * size, width), jnp.float32),
-        in_specs=[vmem] * (2 + cols),
+        in_specs=[vmem] * (len(own) + len(other) + rows),
         out_specs=vmem,
         scratch_shapes=[pltpu.VMEM((cols,) + panel_tile.shape, jnp.bfloat16)],
         compiler_params=pltpu.CompilerParams(vmem_limit_bytes=2 * VMEM_MARGIN),
         name="gradient",
-    )(line, other, *panels)
+    )(*own, *other, *panels)
 
 
 def solution(mesh):

time: 75.8 us -> 72.4 us (0.955)
  starting transfers between devices: 25.7 us -> 22.5 us
  waiting for transfers between devices: 26.4 us -> 27.4 us
  Pallas kernels: 22.1 us -> 21.2 us
    ppermute x21 -> x19, starting transfers between devices: 25.7 us -> 22.5 us  [exchange(): lax.ppermute(value, axis, [(i, target(i, slot, n)) for i in range(n)])]
    ppermute x21 -> x19, waiting for transfers between devices: 26.4 us -> 27.4 us  [exchange(): lax.ppermute(value, axis, [(i, target(i, slot, n)) for i in range(n)])]
    pallas_call x1, Pallas kernels: 15.7 us -> 14.8 us  [integrate(): pl.pallas_call(functools.partial(integrate_far_body, sizes, per_owner, en...]
  transfers between devices with their start and end apart: 21 -> 19, of which waited for: 10 -> 7; matrix products, arithmetic and copies ran while one was open for 1% -> 1% of each run, Pallas kernels for 7% -> 7%
where the time goes in v5:
time: 72.4 us; the launch traced here: 72.2 us
  waiting for transfers between devices  27.4 us (38%)
  starting transfers between devices  22.5 us (31%)
  Pallas kernels  21.2 us (29%)
  other arithmetic  0.74 us (1%)
    ppermute x19, waiting for transfers between devices, exchange(): lax.ppermute(value, axis, [(i, target(i, slot, n)) for i in range(n)])  27.4 us
    ppermute x19, starting transfers between devices, exchange(): lax.ppermute(value, axis, [(i, target(i, slot, n)) for i in range(n)])  22.5 us
    pallas_call x1, Pallas kernels, integrate(): pl.pallas_call(functools.partial(integrate_far_body, sizes, per_owner, en...  14.8 us
    pallas_call x1, Pallas kernels, integrate(): pl.pallas_call(functools.partial(integrate_near_body, entries, radix), ou...  5.03 us
  transfers between devices with their start and end apart: 19, of which 7 were waited for; matrix products, arithmetic and copies ran while one was open for 1% of the time, Pallas kernels for 7%

profile of v5, /device:TPU:0, one launch (start us, length us, event | category | flops | bytes accessed | tf_op | source)
XLA Modules:
  0.0 72.2 jit_solution(5538827194151452369)
XLA Ops:
  0.0 14.8 %integrate_far.1 = (bf16[16,128,2048]{2,1,0:T(8,128)(2,1)S(1)}, bf16[16,2048,128]{2,1,0:T(8,128)(2,1)S(1)}, s32[1,384]{1,0:T(1,128)S(1)}, bf16[24,128,128]{2,1,0:T(8,128)(2,1)S(1)}, bf16[24,128,128]{2,1,0:T(8,128)(2,1)S(1)}) custom-call(s32[2,128]{1,0:T(2,128)} %pair_ref.1, s32[1,128]{1,0:T(1,128)} %bitcast.46, s32[1,128]{1,0:T(1,128)} %bitcast.47, ...), custom_call_target="tpu_custom_call" | custom-call | flops 12884901888 | bytes 16777216 | tf_op jit(solution)/shard_map/integrate_far/pallas_call | solution.py:224
  14.8 1.5 %collective-permute-start = (bf16[24,128,128]{2,1,0:T(8,128)(2,1)S(1)}, bf16[24,128,128]{2,1,0:T(8,128)(2,1)S(1)}, u32[]{:S(2)}, u32[]{:S(2)}) collective-permute-start(bf16[24,128,128]{2,1,0:T(8,128)(2,1)S(1)} %get-tuple-element.12), channel_id=1, source_target_pairs={{0,1},{1,0},{2,3},{3,2},{4,5},{5,4},{6,7},{7,6},{8,9},{9,8},{10,11... | collective-permute-start | bytes 2359304 | tf_op jit(solution)/shard_map/ppermute | solution.py:36
  16.3 5.0 %integrate_near.1 = (bf16[8,128,128]{2,1,0:T(8,128)(2,1)S(1)}, bf16[8,128,128]{2,1,0:T(8,128)(2,1)S(1)}) custom-call(s32[1,384]{1,0:T(1,128)S(1)} %get-tuple-element.14.table, bf16[16,128,2048]{2,1,0:T(8,128)(2,1)S(1)} %get-tuple-element.15.lefts, bf16[16,2048,128]{2,1,0:T(8,128)(2,1)S(1)} %get-tuple-element.16.weighted), custom_call_target="tpu_custom_call" | custom-call | flops 4294967296 | bytes 16777216 | tf_op jit(solution)/shard_map/integrate_near/pallas_call | solution.py:256
  21.4 0.1 collective-permute-start.4
  21.5 0.3 add_convert_fusion.3
  21.7 2.1 %collective-permute-start.1 = (bf16[8,128,128]{2,1,0:T(8,128)(2,1)S(1)}, bf16[8,128,128]{2,1,0:T(8,128)(2,1)S(1)}, u32[]{:S(2)}, u32[]{:S(2)}) collective-permute-start(bf16[8,128,128]{2,1,0:T(8,128)(2,1)S(1)} %get-tuple-element.19), channel_id=1, source_target_pairs={{0,8},{8,0},{16,24},{24,16},{1,9},{9,1},{17,25},{25,17},{2,10},{10... | collective-permute-start | bytes 786440 | tf_op jit(solution)/shard_map/ppermute | solution.py:36
  23.8 1.8 %collective-permute-start.2 = (bf16[8,128,128]{2,1,0:T(8,128)(2,1)S(1)}, bf16[8,128,128]{2,1,0:T(8,128)(2,1)S(1)}, u32[]{:S(2)}, u32[]{:S(2)}) collective-permute-start(bf16[8,128,128]{2,1,0:T(8,128)(2,1)S(1)} %get-tuple-element.21), channel_id=1, source_target_pairs={{0,16},{8,24},{16,0},{24,8},{1,17},{9,25},{17,1},{25,9},{2,18},{10... | collective-permute-start | bytes 786440 | tf_op jit(solution)/shard_map/ppermute | solution.py:36
  25.8 5.2 %collective-permute-done.1 = bf16[8,128,128]{2,1,0:T(8,128)(2,1)S(1)} collective-permute-done((bf16[8,128,128]{2,1,0:T(8,128)(2,1)S(1)}, bf16[8,128,128]{2,1,0:T(8,128)(2,1)S(1)}, u32[]{:S(2)}, u32[]{:S(2)}) %collective-permute-start.1) | collective-permute-done | bytes 262176 | tf_op jit(solution)/shard_map/ppermute | solution.py:36
  31.0 6.9 %collective-permute-done.2 = bf16[8,128,128]{2,1,0:T(8,128)(2,1)S(1)} collective-permute-done((bf16[8,128,128]{2,1,0:T(8,128)(2,1)S(1)}, bf16[8,128,128]{2,1,0:T(8,128)(2,1)S(1)}, u32[]{:S(2)}, u32[]{:S(2)}) %collective-permute-start.2) | collective-permute-done | bytes 262176 | tf_op jit(solution)/shard_map/ppermute | solution.py:36
  38.0 1.4 %collective-permute-start.5 = (bf16[2,2,128,128]{3,2,1,0:T(8,128)(2,1)S(1)}, bf16[2,2,128,128]{3,2,1,0:T(8,128)(2,1)S(1)}, u32[]{:S(2)}, u32[]{:S(2)}) collective-permute-start(bf16[2,2,128,128]{3,2,1,0:T(8,128)(2,1)S(1)} %pad_maximum_fusion), channel_id=1, source_target_pairs={{0,2},{2,0},{4,6},{6,4},{1,3},{3,1},{5,7},{7,5},{8,10},{10,8},{12,... | collective-permute-start | bytes 393224 | tf_op jit(solution)/shard_map/ppermute | solution.py:36
  39.4 0.1 mul.33
  39.6 1.5 %collective-permute-start.13 = (bf16[256,256]{1,0:T(8,128)(2,1)S(1)}, bf16[256,256]{1,0:T(8,128)(2,1)S(1)}, u32[]{:S(2)}, u32[]{:S(2)}) collective-permute-start(bf16[256,256]{1,0:T(8,128)(2,1)S(1)} %bitcast_multiply_fusion.refs_4_), channel_id=1, source_target_pairs={{0,8},{8,0},{16,24},{24,16},{1,9},{9,1},{17,25},{25,17},{2,10},{10... | collective-permute-start | bytes 393224 | tf_op jit(solution)/shard_map/ppermute | solution.py:36
  41.1 0.6 collective-permute-start.14
  41.8 1.4 %collective-permute-start.15 = (bf16[256,256]{1,0:T(8,128)(2,1)S(1)}, bf16[256,256]{1,0:T(8,128)(2,1)S(1)}, u32[]{:S(2)}, u32[]{:S(2)}) collective-permute-start(bf16[256,256]{1,0:T(8,128)(2,1)S(1)} %bitcast_multiply_fusion.refs_4_), channel_id=1, source_target_pairs={{0,24},{8,16},{16,8},{24,0},{1,25},{9,17},{17,9},{25,1},{2,26},{10... | collective-permute-start | bytes 393224 | tf_op jit(solution)/shard_map/ppermute | solution.py:36
  43.2 0.1 fusion.3
  43.3 3.4 %collective-permute-start.6 = (bf16[2,2,128,128]{3,2,1,0:T(8,128)(2,1)S(1)}, bf16[2,2,128,128]{3,2,1,0:T(8,128)(2,1)S(1)}, u32[]{:S(2)}, u32[]{:S(2)}) collective-permute-start(bf16[2,2,128,128]{3,2,1,0:T(8,128)(2,1)S(1)} %pad_maximum_fusion.1), channel_id=1, source_target_pairs={{0,4},{2,6},{4,0},{6,2},{1,5},{3,7},{5,1},{7,3},{8,12},{10,14},{12... | collective-permute-start | bytes 393224 | tf_op jit(solution)/shard_map/ppermute | solution.py:36
  46.7 0.1 mul.28
  46.9 0.9 %collective-permute-start.10 = (bf16[256,256]{1,0:T(8,128)(2,1)S(1)}, bf16[256,256]{1,0:T(8,128)(2,1)S(1)}, u32[]{:S(2)}, u32[]{:S(2)}) collective-permute-start(bf16[256,256]{1,0:T(8,128)(2,1)S(1)} %bitcast_multiply_fusion.1.refs_0_), channel_id=1, source_target_pairs={{0,2},{2,0},{4,6},{6,4},{1,3},{3,1},{5,7},{7,5},{8,10},{10,8},{12,... | collective-permute-start | bytes 393224 | tf_op jit(solution)/shard_map/ppermute | solution.py:36
  47.8 3.7 %collective-permute-done.6 = bf16[2,2,128,128]{3,2,1,0:T(8,128)(2,1)S(1)} collective-permute-done((bf16[2,2,128,128]{3,2,1,0:T(8,128)(2,1)S(1)}, bf16[2,2,128,128]{3,2,1,0:T(8,128)(2,1)S(1)}, u32[]{:S(2)}, u32[]{:S(2)}) %collective-permute-start.6) | collective-permute-done | bytes 131104 | tf_op jit(solution)/shard_map/ppermute | solution.py:36
  51.5 1.3 %collective-permute-start.11 = (bf16[256,256]{1,0:T(8,128)(2,1)S(1)}, bf16[256,256]{1,0:T(8,128)(2,1)S(1)}, u32[]{:S(2)}, u32[]{:S(2)}) collective-permute-start(bf16[256,256]{1,0:T(8,128)(2,1)S(1)} %bitcast_multiply_fusion.1.refs_0_), channel_id=1, source_target_pairs={{0,4},{2,6},{4,0},{6,2},{1,5},{3,7},{5,1},{7,3},{8,12},{10,14},{12... | collective-permute-start | bytes 393224 | tf_op jit(solution)/shard_map/ppermute | solution.py:36
  52.8 1.7 %collective-permute-start.12 = (bf16[256,256]{1,0:T(8,128)(2,1)S(1)}, bf16[256,256]{1,0:T(8,128)(2,1)S(1)}, u32[]{:S(2)}, u32[]{:S(2)}) collective-permute-start(bf16[256,256]{1,0:T(8,128)(2,1)S(1)} %bitcast_multiply_fusion.1.refs_0_), channel_id=1, source_target_pairs={{0,6},{2,4},{4,2},{6,0},{1,7},{3,5},{5,3},{7,1},{8,14},{10,12},{12... | collective-permute-start | bytes 393224 | tf_op jit(solution)/shard_map/ppermute | solution.py:36
  54.5 0.7 collective-permute-start.7
  55.2 6.3 %collective-permute-done.11.refs_2_ = bf16[256,256]{1,0:T(8,128)(2,1)S(1)} collective-permute-done((bf16[256,256]{1,0:T(8,128)(2,1)S(1)}, bf16[256,256]{1,0:T(8,128)(2,1)S(1)}, u32[]{:S(2)}, u32[]{:S(2)}) %collective-permute-start.11) | collective-permute-done | bytes 131104 | tf_op jit(solution)/shard_map/ppermute | solution.py:36
  61.6 0.3 product.1.refs_4_
  61.9 2.0 %collective-permute-start.16 = (bf16[256,256]{1,0:T(8,128)(2,1)S(1)}, bf16[256,256]{1,0:T(8,128)(2,1)S(1)}, u32[]{:S(2)}, u32[]{:S(2)}) collective-permute-start(bf16[256,256]{1,0:T(8,128)(2,1)S(1)} %product.1.refs_4_), channel_id=1, source_target_pairs={{0,8},{8,0},{16,24},{24,16},{1,9},{9,1},{17,25},{25,17},{2,10},{10... | collective-permute-start | bytes 393224 | tf_op jit(solution)/shard_map/ppermute | solution.py:36
  63.9 1.4 %collective-permute-start.17 = (bf16[256,256]{1,0:T(8,128)(2,1)S(1)}, bf16[256,256]{1,0:T(8,128)(2,1)S(1)}, u32[]{:S(2)}, u32[]{:S(2)}) collective-permute-start(bf16[256,256]{1,0:T(8,128)(2,1)S(1)} %product.1.refs_4_), channel_id=1, source_target_pairs={{0,16},{8,24},{16,0},{24,8},{1,17},{9,25},{17,1},{25,9},{2,18},{10... | collective-permute-start | bytes 393224 | tf_op jit(solution)/shard_map/ppermute | solution.py:36
  65.3 0.2 collective-permute-start.18
  65.5 0.5 collective-permute-start.9
  66.0 1.8 %collective-permute-done.16.refs_5_ = bf16[256,256]{1,0:T(8,128)(2,1)S(1)} collective-permute-done((bf16[256,256]{1,0:T(8,128)(2,1)S(1)}, bf16[256,256]{1,0:T(8,128)(2,1)S(1)}, u32[]{:S(2)}, u32[]{:S(2)}) %collective-permute-start.16) | collective-permute-done | bytes 131104 | tf_op jit(solution)/shard_map/ppermute | solution.py:36
  67.8 1.1 %collective-permute-done.17.refs_6_ = bf16[256,256]{1,0:T(8,128)(2,1)S(1)} collective-permute-done((bf16[256,256]{1,0:T(8,128)(2,1)S(1)}, bf16[256,256]{1,0:T(8,128)(2,1)S(1)}, u32[]{:S(2)}, u32[]{:S(2)}) %collective-permute-start.17) | collective-permute-done | bytes 131104 | tf_op jit(solution)/shard_map/ppermute | solution.py:36
  68.9 2.3 %collective-permute-done.18.refs_7_ = bf16[256,256]{1,0:T(8,128)(2,1)S(1)} collective-permute-done((bf16[256,256]{1,0:T(8,128)(2,1)S(1)}, bf16[256,256]{1,0:T(8,128)(2,1)S(1)}, u32[]{:S(2)}, u32[]{:S(2)}) %collective-permute-start.18) | collective-permute-done | bytes 131104 | tf_op jit(solution)/shard_map/ppermute | solution.py:36
  71.2 1.1 %gradient.1 = f32[256,256]{1,0:T(8,128)} custom-call(bf16[2,2,128,128]{3,2,1,0:T(8,128)(2,1)S(1)} %pad_maximum_fusion.2.refs_0_, bf16[2,2,128,128]{3,2,1,0:T(8,128)(2,1)S(1)} %collective-permute-done.7.refs_1_, bf16[2,2,128,128]{3,2,1,0:T(8,128)(2,1)S(1)} %collective-permute-done.8.refs_2_, bf16[2,2,128,128]{3,2,1,0:T(8,128)(2,1)S(1)} %collective-permute-done.9.refs_3_, ...), custom_call_target="tpu_custom_call" | custom-call | tf_op jit(solution)/shard_map/gradient/pallas_call | solution.py:390
  (32 shorter events, 0.4 us)
Async XLA Ops:
  14.8 6.7 %collective-permute-start = (bf16[24,128,128]{2,1,0:T(8,128)(2,1)S(1)}, bf16[24,128,128]{2,1,0:T(8,128)(2,1)S(1)}, u32[]{:S(2)}, u32[]{:S(2)}) collective-permute-start(bf16[24,128,128]{2,1,0:T(8,128)(2,1)S(1)} %get-tuple-element.12), channel_id=1, source_target_pairs={{0,1},{1,0},{2,3},{3,2},{4,5},{5,4},{6,7},{7,6},{8,9},{9,8},{10,11... | collective-permute-start | bytes 2359304 | tf_op jit(solution)/shard_map/ppermute | solution.py:36
  16.3 9.3 %copy-start.2 = (s32[2,4]{1,0:T(2,128)S(1)}, s32[2,4]{1,0:T(2,128)}, u32[]{:S(2)}) copy-start(s32[2,4]{1,0:T(2,128)} %param.17) | copy-start | bytes 100
  16.3 23.2 %copy-start.1 = (bf16[256,512]{1,0:T(8,128)(2,1)S(1)}, bf16[256,512]{1,0:T(8,128)(2,1)}, u32[]{:S(2)}) copy-start(bf16[256,512]{1,0:T(8,128)(2,1)} %param.16) | copy-start | bytes 786436
  16.3 26.9 %copy-start.3 = (s32[2,2]{1,0:T(2,128)S(1)}, s32[2,2]{1,0:T(2,128)}, u32[]{:S(2)}) copy-start(s32[2,2]{1,0:T(2,128)} %param.15) | copy-start | bytes 52
  16.3 30.6 %copy-start = (bf16[256,256]{1,0:T(8,128)(2,1)S(1)}, bf16[256,256]{1,0:T(8,128)(2,1)}, u32[]{:S(2)}) copy-start(bf16[256,256]{1,0:T(8,128)(2,1)} %param.14) | copy-start | bytes 393220
  21.4 4.3 %collective-permute-start.4 = (bf16[8,128,128]{2,1,0:T(8,128)(2,1)S(1)}, bf16[8,128,128]{2,1,0:T(8,128)(2,1)S(1)}, u32[]{:S(2)}, u32[]{:S(2)}) collective-permute-start(bf16[8,128,128]{2,1,0:T(8,128)(2,1)S(1)} %get-tuple-element.17), channel_id=1, source_target_pairs={{0,1},{1,0},{2,3},{3,2},{4,5},{5,4},{6,7},{7,6},{8,9},{9,8},{10,11... | collective-permute-start | bytes 786440 | tf_op jit(solution)/shard_map/ppermute | solution.py:36
  21.7 9.2 %collective-permute-start.1 = (bf16[8,128,128]{2,1,0:T(8,128)(2,1)S(1)}, bf16[8,128,128]{2,1,0:T(8,128)(2,1)S(1)}, u32[]{:S(2)}, u32[]{:S(2)}) collective-permute-start(bf16[8,128,128]{2,1,0:T(8,128)(2,1)S(1)} %get-tuple-element.19), channel_id=1, source_target_pairs={{0,8},{8,0},{16,24},{24,16},{1,9},{9,1},{17,25},{25,17},{2,10},{10... | collective-permute-start | bytes 786440 | tf_op jit(solution)/shard_map/ppermute | solution.py:36
  23.8 14.1 %collective-permute-start.2 = (bf16[8,128,128]{2,1,0:T(8,128)(2,1)S(1)}, bf16[8,128,128]{2,1,0:T(8,128)(2,1)S(1)}, u32[]{:S(2)}, u32[]{:S(2)}) collective-permute-start(bf16[8,128,128]{2,1,0:T(8,128)(2,1)S(1)} %get-tuple-element.21), channel_id=1, source_target_pairs={{0,16},{8,24},{16,0},{24,8},{1,17},{9,25},{17,1},{25,9},{2,18},{10... | collective-permute-start | bytes 786440 | tf_op jit(solution)/shard_map/ppermute | solution.py:36
  25.6 12.3 %collective-permute-start.3 = (bf16[8,128,128]{2,1,0:T(8,128)(2,1)S(1)}, bf16[8,128,128]{2,1,0:T(8,128)(2,1)S(1)}, u32[]{:S(2)}, u32[]{:S(2)}) collective-permute-start(bf16[8,128,128]{2,1,0:T(8,128)(2,1)S(1)} %get-tuple-element.20), channel_id=1, source_target_pairs={{0,24},{8,16},{16,8},{24,0},{1,25},{9,17},{17,9},{25,1},{2,26},{10... | collective-permute-start | bytes 786440 | tf_op jit(solution)/shard_map/ppermute | solution.py:36
  38.0 5.2 %collective-permute-start.5 = (bf16[2,2,128,128]{3,2,1,0:T(8,128)(2,1)S(1)}, bf16[2,2,128,128]{3,2,1,0:T(8,128)(2,1)S(1)}, u32[]{:S(2)}, u32[]{:S(2)}) collective-permute-start(bf16[2,2,128,128]{3,2,1,0:T(8,128)(2,1)S(1)} %pad_maximum_fusion), channel_id=1, source_target_pairs={{0,2},{2,0},{4,6},{6,4},{1,3},{3,1},{5,7},{7,5},{8,10},{10,8},{12,... | collective-permute-start | bytes 393224 | tf_op jit(solution)/shard_map/ppermute | solution.py:36
  39.6 13.2 %collective-permute-start.13 = (bf16[256,256]{1,0:T(8,128)(2,1)S(1)}, bf16[256,256]{1,0:T(8,128)(2,1)S(1)}, u32[]{:S(2)}, u32[]{:S(2)}) collective-permute-start(bf16[256,256]{1,0:T(8,128)(2,1)S(1)} %bitcast_multiply_fusion.refs_4_), channel_id=1, source_target_pairs={{0,8},{8,0},{16,24},{24,16},{1,9},{9,1},{17,25},{25,17},{2,10},{10... | collective-permute-start | bytes 393224 | tf_op jit(solution)/shard_map/ppermute | solution.py:36
  41.1 13.4 %collective-permute-start.14 = (bf16[256,256]{1,0:T(8,128)(2,1)S(1)}, bf16[256,256]{1,0:T(8,128)(2,1)S(1)}, u32[]{:S(2)}, u32[]{:S(2)}) collective-permute-start(bf16[256,256]{1,0:T(8,128)(2,1)S(1)} %bitcast_multiply_fusion.refs_4_), channel_id=1, source_target_pairs={{0,16},{8,24},{16,0},{24,8},{1,17},{9,25},{17,1},{25,9},{2,18},{10... | collective-permute-start | bytes 393224 | tf_op jit(solution)/shard_map/ppermute | solution.py:36
  41.8 13.4 %collective-permute-start.15 = (bf16[256,256]{1,0:T(8,128)(2,1)S(1)}, bf16[256,256]{1,0:T(8,128)(2,1)S(1)}, u32[]{:S(2)}, u32[]{:S(2)}) collective-permute-start(bf16[256,256]{1,0:T(8,128)(2,1)S(1)} %bitcast_multiply_fusion.refs_4_), channel_id=1, source_target_pairs={{0,24},{8,16},{16,8},{24,0},{1,25},{9,17},{17,9},{25,1},{2,26},{10... | collective-permute-start | bytes 393224 | tf_op jit(solution)/shard_map/ppermute | solution.py:36
  43.3 8.2 %collective-permute-start.6 = (bf16[2,2,128,128]{3,2,1,0:T(8,128)(2,1)S(1)}, bf16[2,2,128,128]{3,2,1,0:T(8,128)(2,1)S(1)}, u32[]{:S(2)}, u32[]{:S(2)}) collective-permute-start(bf16[2,2,128,128]{3,2,1,0:T(8,128)(2,1)S(1)} %pad_maximum_fusion.1), channel_id=1, source_target_pairs={{0,4},{2,6},{4,0},{6,2},{1,5},{3,7},{5,1},{7,3},{8,12},{10,14},{12... | collective-permute-start | bytes 393224 | tf_op jit(solution)/shard_map/ppermute | solution.py:36
  46.9 8.3 %collective-permute-start.10 = (bf16[256,256]{1,0:T(8,128)(2,1)S(1)}, bf16[256,256]{1,0:T(8,128)(2,1)S(1)}, u32[]{:S(2)}, u32[]{:S(2)}) collective-permute-start(bf16[256,256]{1,0:T(8,128)(2,1)S(1)} %bitcast_multiply_fusion.1.refs_0_), channel_id=1, source_target_pairs={{0,2},{2,0},{4,6},{6,4},{1,3},{3,1},{5,7},{7,5},{8,10},{10,8},{12,... | collective-permute-start | bytes 393224 | tf_op jit(solution)/shard_map/ppermute | solution.py:36
  51.5 10.1 %collective-permute-start.11 = (bf16[256,256]{1,0:T(8,128)(2,1)S(1)}, bf16[256,256]{1,0:T(8,128)(2,1)S(1)}, u32[]{:S(2)}, u32[]{:S(2)}) collective-permute-start(bf16[256,256]{1,0:T(8,128)(2,1)S(1)} %bitcast_multiply_fusion.1.refs_0_), channel_id=1, source_target_pairs={{0,4},{2,6},{4,0},{6,2},{1,5},{3,7},{5,1},{7,3},{8,12},{10,14},{12... | collective-permute-start | bytes 393224 | tf_op jit(solution)/shard_map/ppermute | solution.py:36
  52.8 8.7 %collective-permute-start.12 = (bf16[256,256]{1,0:T(8,128)(2,1)S(1)}, bf16[256,256]{1,0:T(8,128)(2,1)S(1)}, u32[]{:S(2)}, u32[]{:S(2)}) collective-permute-start(bf16[256,256]{1,0:T(8,128)(2,1)S(1)} %bitcast_multiply_fusion.1.refs_0_), channel_id=1, source_target_pairs={{0,6},{2,4},{4,2},{6,0},{1,7},{3,5},{5,3},{7,1},{8,14},{10,12},{12... | collective-permute-start | bytes 393224 | tf_op jit(solution)/shard_map/ppermute | solution.py:36
  54.5 10.9 %collective-permute-start.7 = (bf16[2,2,128,128]{3,2,1,0:T(8,128)(2,1)S(1)}, bf16[2,2,128,128]{3,2,1,0:T(8,128)(2,1)S(1)}, u32[]{:S(2)}, u32[]{:S(2)}) collective-permute-start(bf16[2,2,128,128]{3,2,1,0:T(8,128)(2,1)S(1)} %pad_maximum_fusion.2.refs_0_), channel_id=1, source_target_pairs={{0,2},{2,0},{4,6},{6,4},{1,3},{3,1},{5,7},{7,5},{8,10},{10,8},{12,... | collective-permute-start | bytes 393224 | tf_op jit(solution)/shard_map/ppermute | solution.py:36
  61.9 5.9 %collective-permute-start.16 = (bf16[256,256]{1,0:T(8,128)(2,1)S(1)}, bf16[256,256]{1,0:T(8,128)(2,1)S(1)}, u32[]{:S(2)}, u32[]{:S(2)}) collective-permute-start(bf16[256,256]{1,0:T(8,128)(2,1)S(1)} %product.1.refs_4_), channel_id=1, source_target_pairs={{0,8},{8,0},{16,24},{24,16},{1,9},{9,1},{17,25},{25,17},{2,10},{10... | collective-permute-start | bytes 393224 | tf_op jit(solution)/shard_map/ppermute | solution.py:36
  63.9 5.0 %collective-permute-start.17 = (bf16[256,256]{1,0:T(8,128)(2,1)S(1)}, bf16[256,256]{1,0:T(8,128)(2,1)S(1)}, u32[]{:S(2)}, u32[]{:S(2)}) collective-permute-start(bf16[256,256]{1,0:T(8,128)(2,1)S(1)} %product.1.refs_4_), channel_id=1, source_target_pairs={{0,16},{8,24},{16,0},{24,8},{1,17},{9,25},{17,1},{25,9},{2,18},{10... | collective-permute-start | bytes 393224 | tf_op jit(solution)/shard_map/ppermute | solution.py:36
  65.3 5.9 %collective-permute-start.18 = (bf16[256,256]{1,0:T(8,128)(2,1)S(1)}, bf16[256,256]{1,0:T(8,128)(2,1)S(1)}, u32[]{:S(2)}, u32[]{:S(2)}) collective-permute-start(bf16[256,256]{1,0:T(8,128)(2,1)S(1)} %product.1.refs_4_), channel_id=1, source_target_pairs={{0,24},{8,16},{16,8},{24,0},{1,25},{9,17},{17,9},{25,1},{2,26},{10... | collective-permute-start | bytes 393224 | tf_op jit(solution)/shard_map/ppermute | solution.py:36
  65.5 5.7 %collective-permute-start.8 = (bf16[2,2,128,128]{3,2,1,0:T(8,128)(2,1)S(1)}, bf16[2,2,128,128]{3,2,1,0:T(8,128)(2,1)S(1)}, u32[]{:S(2)}, u32[]{:S(2)}) collective-permute-start(bf16[2,2,128,128]{3,2,1,0:T(8,128)(2,1)S(1)} %pad_maximum_fusion.2.refs_0_), channel_id=1, source_target_pairs={{0,1},{1,0},{2,3},{3,2},{4,5},{5,4},{6,7},{7,6},{8,9},{9,8},{10,11... | collective-permute-start | bytes 393224 | tf_op jit(solution)/shard_map/ppermute | solution.py:36
  65.5 5.7 %collective-permute-start.9 = (bf16[2,2,128,128]{3,2,1,0:T(8,128)(2,1)S(1)}, bf16[2,2,128,128]{3,2,1,0:T(8,128)(2,1)S(1)}, u32[]{:S(2)}, u32[]{:S(2)}) collective-permute-start(bf16[2,2,128,128]{3,2,1,0:T(8,128)(2,1)S(1)} %collective-permute-done.7.refs_1_), channel_id=1, source_target_pairs={{0,1},{1,0},{2,3},{3,2},{4,5},{5,4},{6,7},{7,6},{8,9},{9,8},{10,11... | collective-permute-start | bytes 393224 | tf_op jit(solution)/shard_map/ppermute | solution.py:36

commit v6 on v5

--- a/solution.py
+++ b/solution.py
@@ -8,8 +8,8 @@
 from jax.sharding import PartitionSpec as P
 
 
-UNROLL = 8
-REST = 2
+UNROLL = 16
+REST = 4
 IN_FLIGHT = 6
 VMEM_LIMIT = 36 * 1024 * 1024
 VMEM_MARGIN = 4 * 1024 * 1024
@@ -124,22 +124,26 @@
     lax.fori_loop(0, total.shape[0], zero, 0)
 
 
-def put(total, keep_ref, send_ref):
-    half = keep_ref.shape[0]
+def put(total, keep_refs, send_refs):
+    share = send_refs[0].shape[0]
+    half = share * len(send_refs)
 
     def one(i, carry):
-        keep_ref[i] = total[i + 1].astype(jnp.bfloat16)
-        send_ref[i] = total[half + i + 1].astype(jnp.bfloat16)
+        for k, (keep_ref, send_ref) in enumerate(zip(keep_refs, send_refs)):
+            keep_ref[i] = total[k * share + i + 1].astype(jnp.bfloat16)
+            send_ref[i] = total[half + k * share + i + 1].astype(jnp.bfloat16)
         return carry
 
-    lax.fori_loop(0, half, one, 0)
+    lax.fori_loop(0, share, one, 0)
 
 
 def integrate_far_body(
     sizes, per_owner, entries, radix, pair_ref, owner_ref, block_ref, basis_ref, pot_ref,
-    lefts, weighted, table_ref, keep_ref, send_ref,
-    pairs, owner, block, pot, basis, pot_cols, total, table, small_sems, arrived,
+    lefts, weighted, table_ref, *refs,
 ):
+    far_rows = sizes[0] - 1
+    keep_refs, send_refs = refs[:far_rows], refs[far_rows : 2 * far_rows]
+    pairs, owner, block, pot, basis, pot_cols, total, table, small_sems, arrived = refs[2 * far_rows :]
     atoms, points, size = basis.shape
     small = [
         pltpu.make_async_copy(source_ref, to, small_sems.at[k])
@@ -181,13 +185,13 @@
     lax.fori_loop(0, atoms, weigh, 0)
     to_scalar.wait()
     accumulate(0, entries, radix, table, lefts, weighted, total)
-    put(total, keep_ref, send_ref)
+    put(total, keep_refs, send_refs)
 
 
 def integrate_near_body(entries, radix, table, lefts, weighted, keep_ref, send_ref, total):
     clear(total)
     accumulate(1, entries, radix, table, lefts, weighted, total)
-    put(total, keep_ref, send_ref)
+    put(total, [keep_ref], [send_ref])
 
 
 def integrate(basis_values, potential, pair_atoms, target_device, target_block, sizes, per_owner):
@@ -221,17 +225,16 @@
     def in_hbm(array):
         return pltpu.with_memory_space_constraint(array, pltpu.HBM)
 
-    lefts, weighted, table, far_keep, far_send = pl.pallas_call(
+    lefts, weighted, table, *found = pl.pallas_call(
         functools.partial(integrate_far_body, sizes, per_owner, entries, radix),
         out_shape=(
             jax.ShapeDtypeStruct((atoms, size, points), jnp.bfloat16),
             jax.ShapeDtypeStruct((atoms, points, size), jnp.bfloat16),
             jax.ShapeDtypeStruct((1, width), jnp.int32),
-            half(far),
-            half(far),
+            *[half(near)] * (2 * (rows - 1)),
         ),
         in_specs=[hbm] * 5,
-        out_specs=(vmem,) * 5,
+        out_specs=(vmem,) * (2 * rows + 1),
         scratch_shapes=[
             pltpu.VMEM((2, parts), jnp.int32),
             pltpu.VMEM((1, parts), jnp.int32),
@@ -262,7 +265,7 @@
         name="integrate_near",
         **options(1 / rows),
     )(table, lefts, weighted)
-    return far_keep, far_send, near_keep, near_send
+    return found[: rows - 1], found[rows - 1 :], near_keep, near_send
 
 
 def index_of(row, col, s, count):
@@ -358,11 +361,10 @@
     def added(*terms):
         return sum(t.astype(jnp.float32) for t in terms[1:]) + terms[0].astype(jnp.float32)
 
-    per_row = cols * per_owner
-    far_got = exchange(far_send, "panel", 1)
+    far_got = [exchange(far_send[s - 1], "panel", 1) for s in range(1, rows)]
     near_got = exchange(near_send, "panel", 1)
     parts = [added(near_keep, near_got).astype(jnp.bfloat16)] + [
-        added(far_keep[s * per_row : (s + 1) * per_row], far_got[s * per_row : (s + 1) * per_row]).astype(jnp.bfloat16)
+        added(far_keep[s], far_got[s]).astype(jnp.bfloat16)
         for s in range(rows - 1)
     ]
     got = [exchange(parts[s], "row", s) for s in range(1, rows)]

time: 72.4 us -> 72.8 us (level)
  starting transfers between devices: 22.5 us -> 26.1 us
  waiting for transfers between devices: 27.4 us -> 24.2 us
    ppermute x19 -> x21, starting transfers between devices: 22.5 us -> 26.1 us  [exchange(): lax.ppermute(value, axis, [(i, target(i, slot, n)) for i in range(n)])]
    ppermute x19 -> x21, waiting for transfers between devices: 27.4 us -> 24.2 us  [exchange(): lax.ppermute(value, axis, [(i, target(i, slot, n)) for i in range(n)])]
  transfers between devices with their start and end apart: 19 -> 21, of which waited for: 7 -> 6; matrix products, arithmetic and copies ran while one was open for 1% -> 1% of each run, Pallas kernels for 7% -> 7%
where the time goes in v6:
time: 72.8 us; the launch traced here: 72.3 us
  starting transfers between devices  26.1 us (36%)
  waiting for transfers between devices  24.2 us (33%)
  Pallas kernels  20.9 us (29%)
    ppermute x21, starting transfers between devices, exchange(): lax.ppermute(value, axis, [(i, target(i, slot, n)) for i in range(n)])  26.1 us
    ppermute x21, waiting for transfers between devices, exchange(): lax.ppermute(value, axis, [(i, target(i, slot, n)) for i in range(n)])  24.2 us
    pallas_call x1, Pallas kernels, integrate(): pl.pallas_call(functools.partial(integrate_far_body, sizes, per_owner, en...  14.5 us
    pallas_call x1, Pallas kernels, integrate(): pl.pallas_call(functools.partial(integrate_near_body, entries, radix), ou...  5.01 us
  transfers between devices with their start and end apart: 21, of which 6 were waited for; matrix products, arithmetic and copies ran while one was open for 1% of the time, Pallas kernels for 7%

profile of v6, /device:TPU:0, one launch (start us, length us, event | category | flops | bytes accessed | tf_op | source)
XLA Modules:
  0.0 72.3 jit_solution(17142780456208185062)
XLA Ops:
  0.0 14.5 %integrate_far.1 = (bf16[16,128,2048]{2,1,0:T(8,128)(2,1)S(1)}, bf16[16,2048,128]{2,1,0:T(8,128)(2,1)S(1)}, s32[1,384]{1,0:T(1,128)S(1)}, bf16[8,128,128]{2,1,0:...) custom-call(s32[2,128]{1,0:T(2,128)} %pair_ref.1, ...), custom_call_target="tpu_custom_call" | custom-call | flops 12884901888 | bytes 16777216 | tf_op jit(solution)/shard_map/integrate_far/pallas_call | solution.py:228
  14.5 1.4 %collective-permute-start = (bf16[8,128,128]{2,1,0:T(8,128)(2,1)S(1)}, bf16[8,128,128]{2,1,0:T(8,128)(2,1)S(1)}, u32[]{:S(2)}, u32[]{:S(2)}) collective-permute-start(bf16[8,128,128]{2,1,0:T(8,128)(2,1)S(1)} %get-tuple-element.16), channel_id=1, source_target_pairs={{0,1},{1,0},{2,3},{3,2},{4,5},{5,4},{6,7},{7,6},{8,9},{9,8},{10,11... | collective-permute-start | bytes 786440 | tf_op jit(solution)/shard_map/ppermute | solution.py:36
  15.9 0.1 collective-permute-start.2
  16.0 5.0 %integrate_near.1 = (bf16[8,128,128]{2,1,0:T(8,128)(2,1)S(1)}, bf16[8,128,128]{2,1,0:T(8,128)(2,1)S(1)}) custom-call(s32[1,384]{1,0:T(1,128)S(1)} %get-tuple-element.22.table, bf16[16,128,2048]{2,1,0:T(8,128)(2,1)S(1)} %get-tuple-element.23.lefts, bf16[16,2048,128]{2,1,0:T(8,128)(2,1)S(1)} %get-tuple-element.24.weighted), custom_call_target="tpu_custom_call" | custom-call | flops 4294967296 | bytes 16777216 | tf_op jit(solution)/shard_map/integrate_near/pallas_call | solution.py:259
  21.0 0.5 collective-permute-start.6
  21.5 0.1 collective-permute-start.4
  21.6 1.4 %collective-permute-start.1 = (bf16[8,128,128]{2,1,0:T(8,128)(2,1)S(1)}, bf16[8,128,128]{2,1,0:T(8,128)(2,1)S(1)}, u32[]{:S(2)}, u32[]{:S(2)}) collective-permute-start(bf16[8,128,128]{2,1,0:T(8,128)(2,1)S(1)} %add_convert_fusion.3), channel_id=1, source_target_pairs={{0,8},{8,0},{16,24},{24,16},{1,9},{9,1},{17,25},{25,17},{2,10},{10... | collective-permute-start | bytes 786440 | tf_op jit(solution)/shard_map/ppermute | solution.py:36
  23.1 2.6 %collective-permute-start.3 = (bf16[8,128,128]{2,1,0:T(8,128)(2,1)S(1)}, bf16[8,128,128]{2,1,0:T(8,128)(2,1)S(1)}, u32[]{:S(2)}, u32[]{:S(2)}) collective-permute-start(bf16[8,128,128]{2,1,0:T(8,128)(2,1)S(1)} %add_convert_fusion.2), channel_id=1, source_target_pairs={{0,16},{8,24},{16,0},{24,8},{1,17},{9,25},{17,1},{25,9},{2,18},{10... | collective-permute-start | bytes 786440 | tf_op jit(solution)/shard_map/ppermute | solution.py:36
  25.8 0.6 collective-permute-start.5
  26.5 4.4 %collective-permute-done.1 = bf16[8,128,128]{2,1,0:T(8,128)(2,1)S(1)} collective-permute-done((bf16[8,128,128]{2,1,0:T(8,128)(2,1)S(1)}, bf16[8,128,128]{2,1,0:T(8,128)(2,1)S(1)}, u32[]{:S(2)}, u32[]{:S(2)}) %collective-permute-start.1) | collective-permute-done | bytes 262176 | tf_op jit(solution)/shard_map/ppermute | solution.py:36
  30.9 6.7 %collective-permute-done.3 = bf16[8,128,128]{2,1,0:T(8,128)(2,1)S(1)} collective-permute-done((bf16[8,128,128]{2,1,0:T(8,128)(2,1)S(1)}, bf16[8,128,128]{2,1,0:T(8,128)(2,1)S(1)}, u32[]{:S(2)}, u32[]{:S(2)}) %collective-permute-start.3) | collective-permute-done | bytes 262176 | tf_op jit(solution)/shard_map/ppermute | solution.py:36
  37.7 1.7 %collective-permute-start.7 = (bf16[2,2,128,128]{3,2,1,0:T(8,128)(2,1)S(1)}, bf16[2,2,128,128]{3,2,1,0:T(8,128)(2,1)S(1)}, u32[]{:S(2)}, u32[]{:S(2)}) collective-permute-start(bf16[2,2,128,128]{3,2,1,0:T(8,128)(2,1)S(1)} %pad_maximum_fusion), channel_id=1, source_target_pairs={{0,2},{2,0},{4,6},{6,4},{1,3},{3,1},{5,7},{7,5},{8,10},{10,8},{12,... | collective-permute-start | bytes 393224 | tf_op jit(solution)/shard_map/ppermute | solution.py:36
  39.3 0.1 mul.33
  39.5 1.2 %collective-permute-start.15 = (bf16[256,256]{1,0:T(8,128)(2,1)S(1)}, bf16[256,256]{1,0:T(8,128)(2,1)S(1)}, u32[]{:S(2)}, u32[]{:S(2)}) collective-permute-start(bf16[256,256]{1,0:T(8,128)(2,1)S(1)} %bitcast_multiply_fusion.refs_4_), channel_id=1, source_target_pairs={{0,8},{8,0},{16,24},{24,16},{1,9},{9,1},{17,25},{25,17},{2,10},{10... | collective-permute-start | bytes 393224 | tf_op jit(solution)/shard_map/ppermute | solution.py:36
  40.7 0.7 %collective-permute-start.16 = (bf16[256,256]{1,0:T(8,128)(2,1)S(1)}, bf16[256,256]{1,0:T(8,128)(2,1)S(1)}, u32[]{:S(2)}, u32[]{:S(2)}) collective-permute-start(bf16[256,256]{1,0:T(8,128)(2,1)S(1)} %bitcast_multiply_fusion.refs_4_), channel_id=1, source_target_pairs={{0,16},{8,24},{16,0},{24,8},{1,17},{9,25},{17,1},{25,9},{2,18},{10... | collective-permute-start | bytes 393224 | tf_op jit(solution)/shard_map/ppermute | solution.py:36
  41.4 1.7 %collective-permute-start.17 = (bf16[256,256]{1,0:T(8,128)(2,1)S(1)}, bf16[256,256]{1,0:T(8,128)(2,1)S(1)}, u32[]{:S(2)}, u32[]{:S(2)}) collective-permute-start(bf16[256,256]{1,0:T(8,128)(2,1)S(1)} %bitcast_multiply_fusion.refs_4_), channel_id=1, source_target_pairs={{0,24},{8,16},{16,8},{24,0},{1,25},{9,17},{17,9},{25,1},{2,26},{10... | collective-permute-start | bytes 393224 | tf_op jit(solution)/shard_map/ppermute | solution.py:36
  43.1 0.1 fusion.3
  43.2 3.1 %collective-permute-start.8 = (bf16[2,2,128,128]{3,2,1,0:T(8,128)(2,1)S(1)}, bf16[2,2,128,128]{3,2,1,0:T(8,128)(2,1)S(1)}, u32[]{:S(2)}, u32[]{:S(2)}) collective-permute-start(bf16[2,2,128,128]{3,2,1,0:T(8,128)(2,1)S(1)} %pad_maximum_fusion.1), channel_id=1, source_target_pairs={{0,4},{2,6},{4,0},{6,2},{1,5},{3,7},{5,1},{7,3},{8,12},{10,14},{12... | collective-permute-start | bytes 393224 | tf_op jit(solution)/shard_map/ppermute | solution.py:36
  46.3 0.1 mul.28
  46.5 1.2 %collective-permute-start.12 = (bf16[256,256]{1,0:T(8,128)(2,1)S(1)}, bf16[256,256]{1,0:T(8,128)(2,1)S(1)}, u32[]{:S(2)}, u32[]{:S(2)}) collective-permute-start(bf16[256,256]{1,0:T(8,128)(2,1)S(1)} %bitcast_multiply_fusion.1.refs_0_), channel_id=1, source_target_pairs={{0,2},{2,0},{4,6},{6,4},{1,3},{3,1},{5,7},{7,5},{8,10},{10,8},{12,... | collective-permute-start | bytes 393224 | tf_op jit(solution)/shard_map/ppermute | solution.py:36
  47.7 3.3 %collective-permute-done.8 = bf16[2,2,128,128]{3,2,1,0:T(8,128)(2,1)S(1)} collective-permute-done((bf16[2,2,128,128]{3,2,1,0:T(8,128)(2,1)S(1)}, bf16[2,2,128,128]{3,2,1,0:T(8,128)(2,1)S(1)}, u32[]{:S(2)}, u32[]{:S(2)}) %collective-permute-start.8) | collective-permute-done | bytes 131104 | tf_op jit(solution)/shard_map/ppermute | solution.py:36
  51.0 1.3 %collective-permute-start.13 = (bf16[256,256]{1,0:T(8,128)(2,1)S(1)}, bf16[256,256]{1,0:T(8,128)(2,1)S(1)}, u32[]{:S(2)}, u32[]{:S(2)}) collective-permute-start(bf16[256,256]{1,0:T(8,128)(2,1)S(1)} %bitcast_multiply_fusion.1.refs_0_), channel_id=1, source_target_pairs={{0,4},{2,6},{4,0},{6,2},{1,5},{3,7},{5,1},{7,3},{8,12},{10,14},{12... | collective-permute-start | bytes 393224 | tf_op jit(solution)/shard_map/ppermute | solution.py:36
  52.3 2.6 %collective-permute-start.14 = (bf16[256,256]{1,0:T(8,128)(2,1)S(1)}, bf16[256,256]{1,0:T(8,128)(2,1)S(1)}, u32[]{:S(2)}, u32[]{:S(2)}) collective-permute-start(bf16[256,256]{1,0:T(8,128)(2,1)S(1)} %bitcast_multiply_fusion.1.refs_0_), channel_id=1, source_target_pairs={{0,6},{2,4},{4,2},{6,0},{1,7},{3,5},{5,3},{7,1},{8,14},{10,12},{12... | collective-permute-start | bytes 393224 | tf_op jit(solution)/shard_map/ppermute | solution.py:36
  54.9 0.6 collective-permute-start.9
  55.6 5.5 %collective-permute-done.13.refs_2_ = bf16[256,256]{1,0:T(8,128)(2,1)S(1)} collective-permute-done((bf16[256,256]{1,0:T(8,128)(2,1)S(1)}, bf16[256,256]{1,0:T(8,128)(2,1)S(1)}, u32[]{:S(2)}, u32[]{:S(2)}) %collective-permute-start.13) | collective-permute-done | bytes 131104 | tf_op jit(solution)/shard_map/ppermute | solution.py:36
  61.1 0.3 product.1.refs_4_
  61.4 3.5 %collective-permute-start.18 = (bf16[256,256]{1,0:T(8,128)(2,1)S(1)}, bf16[256,256]{1,0:T(8,128)(2,1)S(1)}, u32[]{:S(2)}, u32[]{:S(2)}) collective-permute-start(bf16[256,256]{1,0:T(8,128)(2,1)S(1)} %product.1.refs_4_), channel_id=1, source_target_pairs={{0,8},{8,0},{16,24},{24,16},{1,9},{9,1},{17,25},{25,17},{2,10},{10... | collective-permute-start | bytes 393224 | tf_op jit(solution)/shard_map/ppermute | solution.py:36
  64.9 1.5 %collective-permute-start.20 = (bf16[256,256]{1,0:T(8,128)(2,1)S(1)}, bf16[256,256]{1,0:T(8,128)(2,1)S(1)}, u32[]{:S(2)}, u32[]{:S(2)}) collective-permute-start(bf16[256,256]{1,0:T(8,128)(2,1)S(1)} %product.1.refs_4_), channel_id=1, source_target_pairs={{0,24},{8,16},{16,8},{24,0},{1,25},{9,17},{17,9},{25,1},{2,26},{10... | collective-permute-start | bytes 393224 | tf_op jit(solution)/shard_map/ppermute | solution.py:36
  66.4 0.5 collective-permute-start.11
  66.9 0.9 %collective-permute-done.18.refs_5_ = bf16[256,256]{1,0:T(8,128)(2,1)S(1)} collective-permute-done((bf16[256,256]{1,0:T(8,128)(2,1)S(1)}, bf16[256,256]{1,0:T(8,128)(2,1)S(1)}, u32[]{:S(2)}, u32[]{:S(2)}) %collective-permute-start.18) | collective-permute-done | bytes 131104 | tf_op jit(solution)/shard_map/ppermute | solution.py:36
  67.8 3.4 %collective-permute-done.19.refs_6_ = bf16[256,256]{1,0:T(8,128)(2,1)S(1)} collective-permute-done((bf16[256,256]{1,0:T(8,128)(2,1)S(1)}, bf16[256,256]{1,0:T(8,128)(2,1)S(1)}, u32[]{:S(2)}, u32[]{:S(2)}) %collective-permute-start.19) | collective-permute-done | bytes 131104 | tf_op jit(solution)/shard_map/ppermute | solution.py:36
  71.3 1.1 %gradient.1 = f32[256,256]{1,0:T(8,128)} custom-call(bf16[2,2,128,128]{3,2,1,0:T(8,128)(2,1)S(1)} %pad_maximum_fusion.2.refs_0_, bf16[2,2,128,128]{3,2,1,0:T(8,128)(2,1)S(1)} %collective-permute-done.9.refs_1_, bf16[2,2,128,128]{3,2,1,0:T(8,128)(2,1)S(1)} %collective-permute-done.10.refs_2_, bf16[2,2,128,128]{3,2,1,0:T(8,128)(2,1)S(1)} %collective-permute-done.11.refs_3_, ...), custom_call_target="tpu_custom_call" | custom-call | tf_op jit(solution)/shard_map/gradient/pallas_call | solution.py:392
  (38 shorter events, 0.7 us)
Async XLA Ops:
  14.5 7.0 %collective-permute-start = (bf16[8,128,128]{2,1,0:T(8,128)(2,1)S(1)}, bf16[8,128,128]{2,1,0:T(8,128)(2,1)S(1)}, u32[]{:S(2)}, u32[]{:S(2)}) collective-permute-start(bf16[8,128,128]{2,1,0:T(8,128)(2,1)S(1)} %get-tuple-element.16), channel_id=1, source_target_pairs={{0,1},{1,0},{2,3},{3,2},{4,5},{5,4},{6,7},{7,6},{8,9},{9,8},{10,11... | collective-permute-start | bytes 786440 | tf_op jit(solution)/shard_map/ppermute | solution.py:36
  15.9 7.1 %collective-permute-start.2 = (bf16[8,128,128]{2,1,0:T(8,128)(2,1)S(1)}, bf16[8,128,128]{2,1,0:T(8,128)(2,1)S(1)}, u32[]{:S(2)}, u32[]{:S(2)}) collective-permute-start(bf16[8,128,128]{2,1,0:T(8,128)(2,1)S(1)} %get-tuple-element.18), channel_id=1, source_target_pairs={{0,1},{1,0},{2,3},{3,2},{4,5},{5,4},{6,7},{7,6},{8,9},{9,8},{10,11... | collective-permute-start | bytes 786440 | tf_op jit(solution)/shard_map/ppermute | solution.py:36
  16.0 10.4 %copy-start.2 = (s32[2,4]{1,0:T(2,128)S(1)}, s32[2,4]{1,0:T(2,128)}, u32[]{:S(2)}) copy-start(s32[2,4]{1,0:T(2,128)} %param.17) | copy-start | bytes 100
  16.0 23.5 %copy-start.1 = (bf16[256,512]{1,0:T(8,128)(2,1)S(1)}, bf16[256,512]{1,0:T(8,128)(2,1)}, u32[]{:S(2)}) copy-start(bf16[256,512]{1,0:T(8,128)(2,1)} %param.16) | copy-start | bytes 786436
  16.0 27.1 %copy-start.3 = (s32[2,2]{1,0:T(2,128)S(1)}, s32[2,2]{1,0:T(2,128)}, u32[]{:S(2)}) copy-start(s32[2,2]{1,0:T(2,128)} %param.15) | copy-start | bytes 52
  16.0 30.5 %copy-start = (bf16[256,256]{1,0:T(8,128)(2,1)S(1)}, bf16[256,256]{1,0:T(8,128)(2,1)}, u32[]{:S(2)}) copy-start(bf16[256,256]{1,0:T(8,128)(2,1)} %param.14) | copy-start | bytes 393220
  21.0 5.5 %collective-permute-start.6 = (bf16[8,128,128]{2,1,0:T(8,128)(2,1)S(1)}, bf16[8,128,128]{2,1,0:T(8,128)(2,1)S(1)}, u32[]{:S(2)}, u32[]{:S(2)}) collective-permute-start(bf16[8,128,128]{2,1,0:T(8,128)(2,1)S(1)} %get-tuple-element.25), channel_id=1, source_target_pairs={{0,1},{1,0},{2,3},{3,2},{4,5},{5,4},{6,7},{7,6},{8,9},{9,8},{10,11... | collective-permute-start | bytes 786440 | tf_op jit(solution)/shard_map/ppermute | solution.py:36
  21.5 4.2 %collective-permute-start.4 = (bf16[8,128,128]{2,1,0:T(8,128)(2,1)S(1)}, bf16[8,128,128]{2,1,0:T(8,128)(2,1)S(1)}, u32[]{:S(2)}, u32[]{:S(2)}) collective-permute-start(bf16[8,128,128]{2,1,0:T(8,128)(2,1)S(1)} %get-tuple-element.20), channel_id=1, source_target_pairs={{0,1},{1,0},{2,3},{3,2},{4,5},{5,4},{6,7},{7,6},{8,9},{9,8},{10,11... | collective-permute-start | bytes 786440 | tf_op jit(solution)/shard_map/ppermute | solution.py:36
  21.6 9.2 %collective-permute-start.1 = (bf16[8,128,128]{2,1,0:T(8,128)(2,1)S(1)}, bf16[8,128,128]{2,1,0:T(8,128)(2,1)S(1)}, u32[]{:S(2)}, u32[]{:S(2)}) collective-permute-start(bf16[8,128,128]{2,1,0:T(8,128)(2,1)S(1)} %add_convert_fusion.3), channel_id=1, source_target_pairs={{0,8},{8,0},{16,24},{24,16},{1,9},{9,1},{17,25},{25,17},{2,10},{10... | collective-permute-start | bytes 786440 | tf_op jit(solution)/shard_map/ppermute | solution.py:36
  23.1 14.5 %collective-permute-start.3 = (bf16[8,128,128]{2,1,0:T(8,128)(2,1)S(1)}, bf16[8,128,128]{2,1,0:T(8,128)(2,1)S(1)}, u32[]{:S(2)}, u32[]{:S(2)}) collective-permute-start(bf16[8,128,128]{2,1,0:T(8,128)(2,1)S(1)} %add_convert_fusion.2), channel_id=1, source_target_pairs={{0,16},{8,24},{16,0},{24,8},{1,17},{9,25},{17,1},{25,9},{2,18},{10... | collective-permute-start | bytes 786440 | tf_op jit(solution)/shard_map/ppermute | solution.py:36
  25.8 11.8 %collective-permute-start.5 = (bf16[8,128,128]{2,1,0:T(8,128)(2,1)S(1)}, bf16[8,128,128]{2,1,0:T(8,128)(2,1)S(1)}, u32[]{:S(2)}, u32[]{:S(2)}) collective-permute-start(bf16[8,128,128]{2,1,0:T(8,128)(2,1)S(1)} %add_convert_fusion.1), channel_id=1, source_target_pairs={{0,24},{8,16},{16,8},{24,0},{1,25},{9,17},{17,9},{25,1},{2,26},{10... | collective-permute-start | bytes 786440 | tf_op jit(solution)/shard_map/ppermute | solution.py:36
  37.7 5.4 %collective-permute-start.7 = (bf16[2,2,128,128]{3,2,1,0:T(8,128)(2,1)S(1)}, bf16[2,2,128,128]{3,2,1,0:T(8,128)(2,1)S(1)}, u32[]{:S(2)}, u32[]{:S(2)}) collective-permute-start(bf16[2,2,128,128]{3,2,1,0:T(8,128)(2,1)S(1)} %pad_maximum_fusion), channel_id=1, source_target_pairs={{0,2},{2,0},{4,6},{6,4},{1,3},{3,1},{5,7},{7,5},{8,10},{10,8},{12,... | collective-permute-start | bytes 393224 | tf_op jit(solution)/shard_map/ppermute | solution.py:36
  39.5 12.8 %collective-permute-start.15 = (bf16[256,256]{1,0:T(8,128)(2,1)S(1)}, bf16[256,256]{1,0:T(8,128)(2,1)S(1)}, u32[]{:S(2)}, u32[]{:S(2)}) collective-permute-start(bf16[256,256]{1,0:T(8,128)(2,1)S(1)} %bitcast_multiply_fusion.refs_4_), channel_id=1, source_target_pairs={{0,8},{8,0},{16,24},{24,16},{1,9},{9,1},{17,25},{25,17},{2,10},{10... | collective-permute-start | bytes 393224 | tf_op jit(solution)/shard_map/ppermute | solution.py:36
  40.7 14.2 %collective-permute-start.16 = (bf16[256,256]{1,0:T(8,128)(2,1)S(1)}, bf16[256,256]{1,0:T(8,128)(2,1)S(1)}, u32[]{:S(2)}, u32[]{:S(2)}) collective-permute-start(bf16[256,256]{1,0:T(8,128)(2,1)S(1)} %bitcast_multiply_fusion.refs_4_), channel_id=1, source_target_pairs={{0,16},{8,24},{16,0},{24,8},{1,17},{9,25},{17,1},{25,9},{2,18},{10... | collective-permute-start | bytes 393224 | tf_op jit(solution)/shard_map/ppermute | solution.py:36
  41.4 14.1 %collective-permute-start.17 = (bf16[256,256]{1,0:T(8,128)(2,1)S(1)}, bf16[256,256]{1,0:T(8,128)(2,1)S(1)}, u32[]{:S(2)}, u32[]{:S(2)}) collective-permute-start(bf16[256,256]{1,0:T(8,128)(2,1)S(1)} %bitcast_multiply_fusion.refs_4_), channel_id=1, source_target_pairs={{0,24},{8,16},{16,8},{24,0},{1,25},{9,17},{17,9},{25,1},{2,26},{10... | collective-permute-start | bytes 393224 | tf_op jit(solution)/shard_map/ppermute | solution.py:36
  43.2 7.8 %collective-permute-start.8 = (bf16[2,2,128,128]{3,2,1,0:T(8,128)(2,1)S(1)}, bf16[2,2,128,128]{3,2,1,0:T(8,128)(2,1)S(1)}, u32[]{:S(2)}, u32[]{:S(2)}) collective-permute-start(bf16[2,2,128,128]{3,2,1,0:T(8,128)(2,1)S(1)} %pad_maximum_fusion.1), channel_id=1, source_target_pairs={{0,4},{2,6},{4,0},{6,2},{1,5},{3,7},{5,1},{7,3},{8,12},{10,14},{12... | collective-permute-start | bytes 393224 | tf_op jit(solution)/shard_map/ppermute | solution.py:36
  46.5 9.1 %collective-permute-start.12 = (bf16[256,256]{1,0:T(8,128)(2,1)S(1)}, bf16[256,256]{1,0:T(8,128)(2,1)S(1)}, u32[]{:S(2)}, u32[]{:S(2)}) collective-permute-start(bf16[256,256]{1,0:T(8,128)(2,1)S(1)} %bitcast_multiply_fusion.1.refs_0_), channel_id=1, source_target_pairs={{0,2},{2,0},{4,6},{6,4},{1,3},{3,1},{5,7},{7,5},{8,10},{10,8},{12,... | collective-permute-start | bytes 393224 | tf_op jit(solution)/shard_map/ppermute | solution.py:36
  51.0 10.1 %collective-permute-start.13 = (bf16[256,256]{1,0:T(8,128)(2,1)S(1)}, bf16[256,256]{1,0:T(8,128)(2,1)S(1)}, u32[]{:S(2)}, u32[]{:S(2)}) collective-permute-start(bf16[256,256]{1,0:T(8,128)(2,1)S(1)} %bitcast_multiply_fusion.1.refs_0_), channel_id=1, source_target_pairs={{0,4},{2,6},{4,0},{6,2},{1,5},{3,7},{5,1},{7,3},{8,12},{10,14},{12... | collective-permute-start | bytes 393224 | tf_op jit(solution)/shard_map/ppermute | solution.py:36
  52.3 8.7 %collective-permute-start.14 = (bf16[256,256]{1,0:T(8,128)(2,1)S(1)}, bf16[256,256]{1,0:T(8,128)(2,1)S(1)}, u32[]{:S(2)}, u32[]{:S(2)}) collective-permute-start(bf16[256,256]{1,0:T(8,128)(2,1)S(1)} %bitcast_multiply_fusion.1.refs_0_), channel_id=1, source_target_pairs={{0,6},{2,4},{4,2},{6,0},{1,7},{3,5},{5,3},{7,1},{8,14},{10,12},{12... | collective-permute-start | bytes 393224 | tf_op jit(solution)/shard_map/ppermute | solution.py:36
  54.9 11.5 %collective-permute-start.9 = (bf16[2,2,128,128]{3,2,1,0:T(8,128)(2,1)S(1)}, bf16[2,2,128,128]{3,2,1,0:T(8,128)(2,1)S(1)}, u32[]{:S(2)}, u32[]{:S(2)}) collective-permute-start(bf16[2,2,128,128]{3,2,1,0:T(8,128)(2,1)S(1)} %pad_maximum_fusion.2.refs_0_), channel_id=1, source_target_pairs={{0,2},{2,0},{4,6},{6,4},{1,3},{3,1},{5,7},{7,5},{8,10},{10,8},{12,... | collective-permute-start | bytes 393224 | tf_op jit(solution)/shard_map/ppermute | solution.py:36
  61.4 6.4 %collective-permute-start.18 = (bf16[256,256]{1,0:T(8,128)(2,1)S(1)}, bf16[256,256]{1,0:T(8,128)(2,1)S(1)}, u32[]{:S(2)}, u32[]{:S(2)}) collective-permute-start(bf16[256,256]{1,0:T(8,128)(2,1)S(1)} %product.1.refs_4_), channel_id=1, source_target_pairs={{0,8},{8,0},{16,24},{24,16},{1,9},{9,1},{17,25},{25,17},{2,10},{10... | collective-permute-start | bytes 393224 | tf_op jit(solution)/shard_map/ppermute | solution.py:36
  64.9 6.4 %collective-permute-start.19 = (bf16[256,256]{1,0:T(8,128)(2,1)S(1)}, bf16[256,256]{1,0:T(8,128)(2,1)S(1)}, u32[]{:S(2)}, u32[]{:S(2)}) collective-permute-start(bf16[256,256]{1,0:T(8,128)(2,1)S(1)} %product.1.refs_4_), channel_id=1, source_target_pairs={{0,16},{8,24},{16,0},{24,8},{1,17},{9,25},{17,1},{25,9},{2,18},{10... | collective-permute-start | bytes 393224 | tf_op jit(solution)/shard_map/ppermute | solution.py:36
  64.9 6.4 %collective-permute-start.20 = (bf16[256,256]{1,0:T(8,128)(2,1)S(1)}, bf16[256,256]{1,0:T(8,128)(2,1)S(1)}, u32[]{:S(2)}, u32[]{:S(2)}) collective-permute-start(bf16[256,256]{1,0:T(8,128)(2,1)S(1)} %product.1.refs_4_), channel_id=1, source_target_pairs={{0,24},{8,16},{16,8},{24,0},{1,25},{9,17},{17,9},{25,1},{2,26},{10... | collective-permute-start | bytes 393224 | tf_op jit(solution)/shard_map/ppermute | solution.py:36
  66.4 4.8 %collective-permute-start.10 = (bf16[2,2,128,128]{3,2,1,0:T(8,128)(2,1)S(1)}, bf16[2,2,128,128]{3,2,1,0:T(8,128)(2,1)S(1)}, u32[]{:S(2)}, u32[]{:S(2)}) collective-permute-start(bf16[2,2,128,128]{3,2,1,0:T(8,128)(2,1)S(1)} %pad_maximum_fusion.2.refs_0_), channel_id=1, source_target_pairs={{0,1},{1,0},{2,3},{3,2},{4,5},{5,4},{6,7},{7,6},{8,9},{9,8},{10,11... | collective-permute-start | bytes 393224 | tf_op jit(solution)/shard_map/ppermute | solution.py:36
  66.4 4.8 %collective-permute-start.11 = (bf16[2,2,128,128]{3,2,1,0:T(8,128)(2,1)S(1)}, bf16[2,2,128,128]{3,2,1,0:T(8,128)(2,1)S(1)}, u32[]{:S(2)}, u32[]{:S(2)}) collective-permute-start(bf16[2,2,128,128]{3,2,1,0:T(8,128)(2,1)S(1)} %collective-permute-done.9.refs_1_), channel_id=1, source_target_pairs={{0,1},{1,0},{2,3},{3,2},{4,5},{5,4},{6,7},{7,6},{8,9},{9,8},{10,11... | collective-permute-start | bytes 393224 | tf_op jit(solution)/shard_map/ppermute | solution.py:36

commit v7 on v6

--- a/solution.py
+++ b/solution.py
@@ -8,7 +8,7 @@
 from jax.sharding import PartitionSpec as P
 
 
-UNROLL = 16
+UNROLLS = 24, 16
 REST = 4
 IN_FLIGHT = 6
 VMEM_LIMIT = 36 * 1024 * 1024
@@ -58,7 +58,7 @@
 
 
 def most_units(parts, atoms):
-    return (parts + atoms) // 2 + UNROLL
+    return (parts + atoms) // 2 + REST
 
 
 def plan(sizes, per_owner, atoms, radix, pairs, owner, block):
@@ -89,7 +89,7 @@
 
 
 def accumulate(chunk, entries, radix, table, lefts, weighted, total):
-    size = lefts.shape[1]
+    size, unroll = lefts.shape[1], UNROLLS[chunk]
 
     def units(first, number):
         for j in range(number):
@@ -103,17 +103,17 @@
             total[two % radix] += found[:, size:]
 
     def many(i, carry):
-        units(i * UNROLL, UNROLL)
+        units(i * unroll, unroll)
         return carry
 
     def few(i, carry):
-        units(whole * UNROLL + i * REST, REST)
+        units(whole * unroll + i * REST, REST)
         return carry
 
     count = table[0, table.shape[1] - 2 + chunk]
-    whole = count // UNROLL
+    whole = count // unroll
     lax.fori_loop(0, whole, many, 0)
-    lax.fori_loop(0, (count - whole * UNROLL + REST - 1) // REST, few, 0)
+    lax.fori_loop(0, (count - whole * unroll + REST - 1) // REST, few, 0)
 
 
 def clear(total):

time: 72.8 us -> 72.6 us (level)
  no operation moved by 1% of the time
where the time goes in v7:
time: 72.6 us; the launch traced here: 72.2 us
  starting transfers between devices  26.1 us (36%)
  waiting for transfers between devices  24.2 us (33%)
  Pallas kernels  20.7 us (29%)
    ppermute x21, starting transfers between devices, exchange(): lax.ppermute(value, axis, [(i, target(i, slot, n)) for i in range(n)])  26.1 us
    ppermute x21, waiting for transfers between devices, exchange(): lax.ppermute(value, axis, [(i, target(i, slot, n)) for i in range(n)])  24.2 us
    pallas_call x1, Pallas kernels, integrate(): pl.pallas_call(functools.partial(integrate_far_body, sizes, per_owner, en...  14.3 us
    pallas_call x1, Pallas kernels, integrate(): pl.pallas_call(functools.partial(integrate_near_body, entries, radix), ou...  5.01 us
  transfers between devices with their start and end apart: 21, of which 6 were waited for; matrix products, arithmetic and copies ran while one was open for 1% of the time, Pallas kernels for 7%

profile of v7, /device:TPU:0, one launch (start us, length us, event | category | flops | bytes accessed | tf_op | source)
XLA Modules:
  0.0 72.2 jit_solution(9862616773737704262)
XLA Ops:
  0.0 14.3 %integrate_far.1 = (bf16[16,128,2048]{2,1,0:T(8,128)(2,1)S(1)}, bf16[16,2048,128]{2,1,0:T(8,128)(2,1)S(1)}, s32[1,384]{1,0:T(1,128)S(1)}, bf16[8,128,128]{2,1,0:...) custom-call(s32[2,128]{1,0:T(2,128)} %pair_ref.1, ...), custom_call_target="tpu_custom_call" | custom-call | flops 12884901888 | bytes 16777216 | tf_op jit(solution)/shard_map/integrate_far/pallas_call | solution.py:228
  14.4 1.4 %collective-permute-start = (bf16[8,128,128]{2,1,0:T(8,128)(2,1)S(1)}, bf16[8,128,128]{2,1,0:T(8,128)(2,1)S(1)}, u32[]{:S(2)}, u32[]{:S(2)}) collective-permute-start(bf16[8,128,128]{2,1,0:T(8,128)(2,1)S(1)} %get-tuple-element.16), channel_id=1, source_target_pairs={{0,1},{1,0},{2,3},{3,2},{4,5},{5,4},{6,7},{7,6},{8,9},{9,8},{10,11... | collective-permute-start | bytes 786440 | tf_op jit(solution)/shard_map/ppermute | solution.py:36
  15.7 0.1 collective-permute-start.2
  15.8 5.0 %integrate_near.1 = (bf16[8,128,128]{2,1,0:T(8,128)(2,1)S(1)}, bf16[8,128,128]{2,1,0:T(8,128)(2,1)S(1)}) custom-call(s32[1,384]{1,0:T(1,128)S(1)} %get-tuple-element.22.table, bf16[16,128,2048]{2,1,0:T(8,128)(2,1)S(1)} %get-tuple-element.23.lefts, bf16[16,2048,128]{2,1,0:T(8,128)(2,1)S(1)} %get-tuple-element.24.weighted), custom_call_target="tpu_custom_call" | custom-call | flops 4294967296 | bytes 16777216 | tf_op jit(solution)/shard_map/integrate_near/pallas_call | solution.py:259
  20.8 0.5 collective-permute-start.6
  21.3 0.1 collective-permute-start.4
  21.5 1.4 %collective-permute-start.1 = (bf16[8,128,128]{2,1,0:T(8,128)(2,1)S(1)}, bf16[8,128,128]{2,1,0:T(8,128)(2,1)S(1)}, u32[]{:S(2)}, u32[]{:S(2)}) collective-permute-start(bf16[8,128,128]{2,1,0:T(8,128)(2,1)S(1)} %add_convert_fusion.3), channel_id=1, source_target_pairs={{0,8},{8,0},{16,24},{24,16},{1,9},{9,1},{17,25},{25,17},{2,10},{10... | collective-permute-start | bytes 786440 | tf_op jit(solution)/shard_map/ppermute | solution.py:36
  22.9 2.6 %collective-permute-start.3 = (bf16[8,128,128]{2,1,0:T(8,128)(2,1)S(1)}, bf16[8,128,128]{2,1,0:T(8,128)(2,1)S(1)}, u32[]{:S(2)}, u32[]{:S(2)}) collective-permute-start(bf16[8,128,128]{2,1,0:T(8,128)(2,1)S(1)} %add_convert_fusion.2), channel_id=1, source_target_pairs={{0,16},{8,24},{16,0},{24,8},{1,17},{9,25},{17,1},{25,9},{2,18},{10... | collective-permute-start | bytes 786440 | tf_op jit(solution)/shard_map/ppermute | solution.py:36
  25.6 0.6 collective-permute-start.5
  26.4 4.4 %collective-permute-done.1 = bf16[8,128,128]{2,1,0:T(8,128)(2,1)S(1)} collective-permute-done((bf16[8,128,128]{2,1,0:T(8,128)(2,1)S(1)}, bf16[8,128,128]{2,1,0:T(8,128)(2,1)S(1)}, u32[]{:S(2)}, u32[]{:S(2)}) %collective-permute-start.1) | collective-permute-done | bytes 262176 | tf_op jit(solution)/shard_map/ppermute | solution.py:36
  30.7 6.7 %collective-permute-done.3 = bf16[8,128,128]{2,1,0:T(8,128)(2,1)S(1)} collective-permute-done((bf16[8,128,128]{2,1,0:T(8,128)(2,1)S(1)}, bf16[8,128,128]{2,1,0:T(8,128)(2,1)S(1)}, u32[]{:S(2)}, u32[]{:S(2)}) %collective-permute-start.3) | collective-permute-done | bytes 262176 | tf_op jit(solution)/shard_map/ppermute | solution.py:36
  37.5 1.7 %collective-permute-start.7 = (bf16[2,2,128,128]{3,2,1,0:T(8,128)(2,1)S(1)}, bf16[2,2,128,128]{3,2,1,0:T(8,128)(2,1)S(1)}, u32[]{:S(2)}, u32[]{:S(2)}) collective-permute-start(bf16[2,2,128,128]{3,2,1,0:T(8,128)(2,1)S(1)} %pad_maximum_fusion), channel_id=1, source_target_pairs={{0,2},{2,0},{4,6},{6,4},{1,3},{3,1},{5,7},{7,5},{8,10},{10,8},{12,... | collective-permute-start | bytes 393224 | tf_op jit(solution)/shard_map/ppermute | solution.py:36
  39.2 0.1 mul.33
  39.4 1.1 %collective-permute-start.15 = (bf16[256,256]{1,0:T(8,128)(2,1)S(1)}, bf16[256,256]{1,0:T(8,128)(2,1)S(1)}, u32[]{:S(2)}, u32[]{:S(2)}) collective-permute-start(bf16[256,256]{1,0:T(8,128)(2,1)S(1)} %bitcast_multiply_fusion.refs_4_), channel_id=1, source_target_pairs={{0,8},{8,0},{16,24},{24,16},{1,9},{9,1},{17,25},{25,17},{2,10},{10... | collective-permute-start | bytes 393224 | tf_op jit(solution)/shard_map/ppermute | solution.py:36
  40.5 0.7 %collective-permute-start.16 = (bf16[256,256]{1,0:T(8,128)(2,1)S(1)}, bf16[256,256]{1,0:T(8,128)(2,1)S(1)}, u32[]{:S(2)}, u32[]{:S(2)}) collective-permute-start(bf16[256,256]{1,0:T(8,128)(2,1)S(1)} %bitcast_multiply_fusion.refs_4_), channel_id=1, source_target_pairs={{0,16},{8,24},{16,0},{24,8},{1,17},{9,25},{17,1},{25,9},{2,18},{10... | collective-permute-start | bytes 393224 | tf_op jit(solution)/shard_map/ppermute | solution.py:36
  41.3 1.7 %collective-permute-start.17 = (bf16[256,256]{1,0:T(8,128)(2,1)S(1)}, bf16[256,256]{1,0:T(8,128)(2,1)S(1)}, u32[]{:S(2)}, u32[]{:S(2)}) collective-permute-start(bf16[256,256]{1,0:T(8,128)(2,1)S(1)} %bitcast_multiply_fusion.refs_4_), channel_id=1, source_target_pairs={{0,24},{8,16},{16,8},{24,0},{1,25},{9,17},{17,9},{25,1},{2,26},{10... | collective-permute-start | bytes 393224 | tf_op jit(solution)/shard_map/ppermute | solution.py:36
  42.9 0.1 fusion.3
  43.1 3.1 %collective-permute-start.8 = (bf16[2,2,128,128]{3,2,1,0:T(8,128)(2,1)S(1)}, bf16[2,2,128,128]{3,2,1,0:T(8,128)(2,1)S(1)}, u32[]{:S(2)}, u32[]{:S(2)}) collective-permute-start(bf16[2,2,128,128]{3,2,1,0:T(8,128)(2,1)S(1)} %pad_maximum_fusion.1), channel_id=1, source_target_pairs={{0,4},{2,6},{4,0},{6,2},{1,5},{3,7},{5,1},{7,3},{8,12},{10,14},{12... | collective-permute-start | bytes 393224 | tf_op jit(solution)/shard_map/ppermute | solution.py:36
  46.1 0.1 mul.28
  46.3 1.2 %collective-permute-start.12 = (bf16[256,256]{1,0:T(8,128)(2,1)S(1)}, bf16[256,256]{1,0:T(8,128)(2,1)S(1)}, u32[]{:S(2)}, u32[]{:S(2)}) collective-permute-start(bf16[256,256]{1,0:T(8,128)(2,1)S(1)} %bitcast_multiply_fusion.1.refs_0_), channel_id=1, source_target_pairs={{0,2},{2,0},{4,6},{6,4},{1,3},{3,1},{5,7},{7,5},{8,10},{10,8},{12,... | collective-permute-start | bytes 393224 | tf_op jit(solution)/shard_map/ppermute | solution.py:36
  47.5 3.3 %collective-permute-done.8 = bf16[2,2,128,128]{3,2,1,0:T(8,128)(2,1)S(1)} collective-permute-done((bf16[2,2,128,128]{3,2,1,0:T(8,128)(2,1)S(1)}, bf16[2,2,128,128]{3,2,1,0:T(8,128)(2,1)S(1)}, u32[]{:S(2)}, u32[]{:S(2)}) %collective-permute-start.8) | collective-permute-done | bytes 131104 | tf_op jit(solution)/shard_map/ppermute | solution.py:36
  50.8 1.3 %collective-permute-start.13 = (bf16[256,256]{1,0:T(8,128)(2,1)S(1)}, bf16[256,256]{1,0:T(8,128)(2,1)S(1)}, u32[]{:S(2)}, u32[]{:S(2)}) collective-permute-start(bf16[256,256]{1,0:T(8,128)(2,1)S(1)} %bitcast_multiply_fusion.1.refs_0_), channel_id=1, source_target_pairs={{0,4},{2,6},{4,0},{6,2},{1,5},{3,7},{5,1},{7,3},{8,12},{10,14},{12... | collective-permute-start | bytes 393224 | tf_op jit(solution)/shard_map/ppermute | solution.py:36
  52.1 2.6 %collective-permute-start.14 = (bf16[256,256]{1,0:T(8,128)(2,1)S(1)}, bf16[256,256]{1,0:T(8,128)(2,1)S(1)}, u32[]{:S(2)}, u32[]{:S(2)}) collective-permute-start(bf16[256,256]{1,0:T(8,128)(2,1)S(1)} %bitcast_multiply_fusion.1.refs_0_), channel_id=1, source_target_pairs={{0,6},{2,4},{4,2},{6,0},{1,7},{3,5},{5,3},{7,1},{8,14},{10,12},{12... | collective-permute-start | bytes 393224 | tf_op jit(solution)/shard_map/ppermute | solution.py:36
  54.8 0.6 collective-permute-start.9
  55.4 5.5 %collective-permute-done.13.refs_2_ = bf16[256,256]{1,0:T(8,128)(2,1)S(1)} collective-permute-done((bf16[256,256]{1,0:T(8,128)(2,1)S(1)}, bf16[256,256]{1,0:T(8,128)(2,1)S(1)}, u32[]{:S(2)}, u32[]{:S(2)}) %collective-permute-start.13) | collective-permute-done | bytes 131104 | tf_op jit(solution)/shard_map/ppermute | solution.py:36
  60.9 0.3 product.1.refs_4_
  61.2 3.5 %collective-permute-start.18 = (bf16[256,256]{1,0:T(8,128)(2,1)S(1)}, bf16[256,256]{1,0:T(8,128)(2,1)S(1)}, u32[]{:S(2)}, u32[]{:S(2)}) collective-permute-start(bf16[256,256]{1,0:T(8,128)(2,1)S(1)} %product.1.refs_4_), channel_id=1, source_target_pairs={{0,8},{8,0},{16,24},{24,16},{1,9},{9,1},{17,25},{25,17},{2,10},{10... | collective-permute-start | bytes 393224 | tf_op jit(solution)/shard_map/ppermute | solution.py:36
  64.7 1.5 %collective-permute-start.20 = (bf16[256,256]{1,0:T(8,128)(2,1)S(1)}, bf16[256,256]{1,0:T(8,128)(2,1)S(1)}, u32[]{:S(2)}, u32[]{:S(2)}) collective-permute-start(bf16[256,256]{1,0:T(8,128)(2,1)S(1)} %product.1.refs_4_), channel_id=1, source_target_pairs={{0,24},{8,16},{16,8},{24,0},{1,25},{9,17},{17,9},{25,1},{2,26},{10... | collective-permute-start | bytes 393224 | tf_op jit(solution)/shard_map/ppermute | solution.py:36
  66.3 0.5 collective-permute-start.11
  66.8 0.9 %collective-permute-done.18.refs_5_ = bf16[256,256]{1,0:T(8,128)(2,1)S(1)} collective-permute-done((bf16[256,256]{1,0:T(8,128)(2,1)S(1)}, bf16[256,256]{1,0:T(8,128)(2,1)S(1)}, u32[]{:S(2)}, u32[]{:S(2)}) %collective-permute-start.18) | collective-permute-done | bytes 131104 | tf_op jit(solution)/shard_map/ppermute | solution.py:36
  67.7 3.4 %collective-permute-done.19.refs_6_ = bf16[256,256]{1,0:T(8,128)(2,1)S(1)} collective-permute-done((bf16[256,256]{1,0:T(8,128)(2,1)S(1)}, bf16[256,256]{1,0:T(8,128)(2,1)S(1)}, u32[]{:S(2)}, u32[]{:S(2)}) %collective-permute-start.19) | collective-permute-done | bytes 131104 | tf_op jit(solution)/shard_map/ppermute | solution.py:36
  71.1 1.1 %gradient.1 = f32[256,256]{1,0:T(8,128)} custom-call(bf16[2,2,128,128]{3,2,1,0:T(8,128)(2,1)S(1)} %pad_maximum_fusion.2.refs_0_, bf16[2,2,128,128]{3,2,1,0:T(8,128)(2,1)S(1)} %collective-permute-done.9.refs_1_, bf16[2,2,128,128]{3,2,1,0:T(8,128)(2,1)S(1)} %collective-permute-done.10.refs_2_, bf16[2,2,128,128]{3,2,1,0:T(8,128)(2,1)S(1)} %collective-permute-done.11.refs_3_, ...), custom_call_target="tpu_custom_call" | custom-call | tf_op jit(solution)/shard_map/gradient/pallas_call | solution.py:392
  (38 shorter events, 0.7 us)
Async XLA Ops:
  14.4 7.0 %collective-permute-start = (bf16[8,128,128]{2,1,0:T(8,128)(2,1)S(1)}, bf16[8,128,128]{2,1,0:T(8,128)(2,1)S(1)}, u32[]{:S(2)}, u32[]{:S(2)}) collective-permute-start(bf16[8,128,128]{2,1,0:T(8,128)(2,1)S(1)} %get-tuple-element.16), channel_id=1, source_target_pairs={{0,1},{1,0},{2,3},{3,2},{4,5},{5,4},{6,7},{7,6},{8,9},{9,8},{10,11... | collective-permute-start | bytes 786440 | tf_op jit(solution)/shard_map/ppermute | solution.py:36
  15.7 7.1 %collective-permute-start.2 = (bf16[8,128,128]{2,1,0:T(8,128)(2,1)S(1)}, bf16[8,128,128]{2,1,0:T(8,128)(2,1)S(1)}, u32[]{:S(2)}, u32[]{:S(2)}) collective-permute-start(bf16[8,128,128]{2,1,0:T(8,128)(2,1)S(1)} %get-tuple-element.18), channel_id=1, source_target_pairs={{0,1},{1,0},{2,3},{3,2},{4,5},{5,4},{6,7},{7,6},{8,9},{9,8},{10,11... | collective-permute-start | bytes 786440 | tf_op jit(solution)/shard_map/ppermute | solution.py:36
  15.8 10.4 %copy-start.2 = (s32[2,4]{1,0:T(2,128)S(1)}, s32[2,4]{1,0:T(2,128)}, u32[]{:S(2)}) copy-start(s32[2,4]{1,0:T(2,128)} %param.17) | copy-start | bytes 100
  15.8 23.5 %copy-start.1 = (bf16[256,512]{1,0:T(8,128)(2,1)S(1)}, bf16[256,512]{1,0:T(8,128)(2,1)}, u32[]{:S(2)}) copy-start(bf16[256,512]{1,0:T(8,128)(2,1)} %param.16) | copy-start | bytes 786436
  15.8 27.1 %copy-start.3 = (s32[2,2]{1,0:T(2,128)S(1)}, s32[2,2]{1,0:T(2,128)}, u32[]{:S(2)}) copy-start(s32[2,2]{1,0:T(2,128)} %param.15) | copy-start | bytes 52
  15.8 30.5 %copy-start = (bf16[256,256]{1,0:T(8,128)(2,1)S(1)}, bf16[256,256]{1,0:T(8,128)(2,1)}, u32[]{:S(2)}) copy-start(bf16[256,256]{1,0:T(8,128)(2,1)} %param.14) | copy-start | bytes 393220
  20.8 5.5 %collective-permute-start.6 = (bf16[8,128,128]{2,1,0:T(8,128)(2,1)S(1)}, bf16[8,128,128]{2,1,0:T(8,128)(2,1)S(1)}, u32[]{:S(2)}, u32[]{:S(2)}) collective-permute-start(bf16[8,128,128]{2,1,0:T(8,128)(2,1)S(1)} %get-tuple-element.25), channel_id=1, source_target_pairs={{0,1},{1,0},{2,3},{3,2},{4,5},{5,4},{6,7},{7,6},{8,9},{9,8},{10,11... | collective-permute-start | bytes 786440 | tf_op jit(solution)/shard_map/ppermute | solution.py:36
  21.3 4.2 %collective-permute-start.4 = (bf16[8,128,128]{2,1,0:T(8,128)(2,1)S(1)}, bf16[8,128,128]{2,1,0:T(8,128)(2,1)S(1)}, u32[]{:S(2)}, u32[]{:S(2)}) collective-permute-start(bf16[8,128,128]{2,1,0:T(8,128)(2,1)S(1)} %get-tuple-element.20), channel_id=1, source_target_pairs={{0,1},{1,0},{2,3},{3,2},{4,5},{5,4},{6,7},{7,6},{8,9},{9,8},{10,11... | collective-permute-start | bytes 786440 | tf_op jit(solution)/shard_map/ppermute | solution.py:36
  21.5 9.2 %collective-permute-start.1 = (bf16[8,128,128]{2,1,0:T(8,128)(2,1)S(1)}, bf16[8,128,128]{2,1,0:T(8,128)(2,1)S(1)}, u32[]{:S(2)}, u32[]{:S(2)}) collective-permute-start(bf16[8,128,128]{2,1,0:T(8,128)(2,1)S(1)} %add_convert_fusion.3), channel_id=1, source_target_pairs={{0,8},{8,0},{16,24},{24,16},{1,9},{9,1},{17,25},{25,17},{2,10},{10... | collective-permute-start | bytes 786440 | tf_op jit(solution)/shard_map/ppermute | solution.py:36
  22.9 14.5 %collective-permute-start.3 = (bf16[8,128,128]{2,1,0:T(8,128)(2,1)S(1)}, bf16[8,128,128]{2,1,0:T(8,128)(2,1)S(1)}, u32[]{:S(2)}, u32[]{:S(2)}) collective-permute-start(bf16[8,128,128]{2,1,0:T(8,128)(2,1)S(1)} %add_convert_fusion.2), channel_id=1, source_target_pairs={{0,16},{8,24},{16,0},{24,8},{1,17},{9,25},{17,1},{25,9},{2,18},{10... | collective-permute-start | bytes 786440 | tf_op jit(solution)/shard_map/ppermute | solution.py:36
  25.6 11.8 %collective-permute-start.5 = (bf16[8,128,128]{2,1,0:T(8,128)(2,1)S(1)}, bf16[8,128,128]{2,1,0:T(8,128)(2,1)S(1)}, u32[]{:S(2)}, u32[]{:S(2)}) collective-permute-start(bf16[8,128,128]{2,1,0:T(8,128)(2,1)S(1)} %add_convert_fusion.1), channel_id=1, source_target_pairs={{0,24},{8,16},{16,8},{24,0},{1,25},{9,17},{17,9},{25,1},{2,26},{10... | collective-permute-start | bytes 786440 | tf_op jit(solution)/shard_map/ppermute | solution.py:36
  37.5 5.4 %collective-permute-start.7 = (bf16[2,2,128,128]{3,2,1,0:T(8,128)(2,1)S(1)}, bf16[2,2,128,128]{3,2,1,0:T(8,128)(2,1)S(1)}, u32[]{:S(2)}, u32[]{:S(2)}) collective-permute-start(bf16[2,2,128,128]{3,2,1,0:T(8,128)(2,1)S(1)} %pad_maximum_fusion), channel_id=1, source_target_pairs={{0,2},{2,0},{4,6},{6,4},{1,3},{3,1},{5,7},{7,5},{8,10},{10,8},{12,... | collective-permute-start | bytes 393224 | tf_op jit(solution)/shard_map/ppermute | solution.py:36
  39.4 12.8 %collective-permute-start.15 = (bf16[256,256]{1,0:T(8,128)(2,1)S(1)}, bf16[256,256]{1,0:T(8,128)(2,1)S(1)}, u32[]{:S(2)}, u32[]{:S(2)}) collective-permute-start(bf16[256,256]{1,0:T(8,128)(2,1)S(1)} %bitcast_multiply_fusion.refs_4_), channel_id=1, source_target_pairs={{0,8},{8,0},{16,24},{24,16},{1,9},{9,1},{17,25},{25,17},{2,10},{10... | collective-permute-start | bytes 393224 | tf_op jit(solution)/shard_map/ppermute | solution.py:36
  40.5 14.2 %collective-permute-start.16 = (bf16[256,256]{1,0:T(8,128)(2,1)S(1)}, bf16[256,256]{1,0:T(8,128)(2,1)S(1)}, u32[]{:S(2)}, u32[]{:S(2)}) collective-permute-start(bf16[256,256]{1,0:T(8,128)(2,1)S(1)} %bitcast_multiply_fusion.refs_4_), channel_id=1, source_target_pairs={{0,16},{8,24},{16,0},{24,8},{1,17},{9,25},{17,1},{25,9},{2,18},{10... | collective-permute-start | bytes 393224 | tf_op jit(solution)/shard_map/ppermute | solution.py:36
  41.3 14.1 %collective-permute-start.17 = (bf16[256,256]{1,0:T(8,128)(2,1)S(1)}, bf16[256,256]{1,0:T(8,128)(2,1)S(1)}, u32[]{:S(2)}, u32[]{:S(2)}) collective-permute-start(bf16[256,256]{1,0:T(8,128)(2,1)S(1)} %bitcast_multiply_fusion.refs_4_), channel_id=1, source_target_pairs={{0,24},{8,16},{16,8},{24,0},{1,25},{9,17},{17,9},{25,1},{2,26},{10... | collective-permute-start | bytes 393224 | tf_op jit(solution)/shard_map/ppermute | solution.py:36
  43.1 7.8 %collective-permute-start.8 = (bf16[2,2,128,128]{3,2,1,0:T(8,128)(2,1)S(1)}, bf16[2,2,128,128]{3,2,1,0:T(8,128)(2,1)S(1)}, u32[]{:S(2)}, u32[]{:S(2)}) collective-permute-start(bf16[2,2,128,128]{3,2,1,0:T(8,128)(2,1)S(1)} %pad_maximum_fusion.1), channel_id=1, source_target_pairs={{0,4},{2,6},{4,0},{6,2},{1,5},{3,7},{5,1},{7,3},{8,12},{10,14},{12... | collective-permute-start | bytes 393224 | tf_op jit(solution)/shard_map/ppermute | solution.py:36
  46.3 9.1 %collective-permute-start.12 = (bf16[256,256]{1,0:T(8,128)(2,1)S(1)}, bf16[256,256]{1,0:T(8,128)(2,1)S(1)}, u32[]{:S(2)}, u32[]{:S(2)}) collective-permute-start(bf16[256,256]{1,0:T(8,128)(2,1)S(1)} %bitcast_multiply_fusion.1.refs_0_), channel_id=1, source_target_pairs={{0,2},{2,0},{4,6},{6,4},{1,3},{3,1},{5,7},{7,5},{8,10},{10,8},{12,... | collective-permute-start | bytes 393224 | tf_op jit(solution)/shard_map/ppermute | solution.py:36
  50.8 10.1 %collective-permute-start.13 = (bf16[256,256]{1,0:T(8,128)(2,1)S(1)}, bf16[256,256]{1,0:T(8,128)(2,1)S(1)}, u32[]{:S(2)}, u32[]{:S(2)}) collective-permute-start(bf16[256,256]{1,0:T(8,128)(2,1)S(1)} %bitcast_multiply_fusion.1.refs_0_), channel_id=1, source_target_pairs={{0,4},{2,6},{4,0},{6,2},{1,5},{3,7},{5,1},{7,3},{8,12},{10,14},{12... | collective-permute-start | bytes 393224 | tf_op jit(solution)/shard_map/ppermute | solution.py:36
  52.1 8.7 %collective-permute-start.14 = (bf16[256,256]{1,0:T(8,128)(2,1)S(1)}, bf16[256,256]{1,0:T(8,128)(2,1)S(1)}, u32[]{:S(2)}, u32[]{:S(2)}) collective-permute-start(bf16[256,256]{1,0:T(8,128)(2,1)S(1)} %bitcast_multiply_fusion.1.refs_0_), channel_id=1, source_target_pairs={{0,6},{2,4},{4,2},{6,0},{1,7},{3,5},{5,3},{7,1},{8,14},{10,12},{12... | collective-permute-start | bytes 393224 | tf_op jit(solution)/shard_map/ppermute | solution.py:36
  54.8 11.5 %collective-permute-start.9 = (bf16[2,2,128,128]{3,2,1,0:T(8,128)(2,1)S(1)}, bf16[2,2,128,128]{3,2,1,0:T(8,128)(2,1)S(1)}, u32[]{:S(2)}, u32[]{:S(2)}) collective-permute-start(bf16[2,2,128,128]{3,2,1,0:T(8,128)(2,1)S(1)} %pad_maximum_fusion.2.refs_0_), channel_id=1, source_target_pairs={{0,2},{2,0},{4,6},{6,4},{1,3},{3,1},{5,7},{7,5},{8,10},{10,8},{12,... | collective-permute-start | bytes 393224 | tf_op jit(solution)/shard_map/ppermute | solution.py:36
  61.2 6.4 %collective-permute-start.18 = (bf16[256,256]{1,0:T(8,128)(2,1)S(1)}, bf16[256,256]{1,0:T(8,128)(2,1)S(1)}, u32[]{:S(2)}, u32[]{:S(2)}) collective-permute-start(bf16[256,256]{1,0:T(8,128)(2,1)S(1)} %product.1.refs_4_), channel_id=1, source_target_pairs={{0,8},{8,0},{16,24},{24,16},{1,9},{9,1},{17,25},{25,17},{2,10},{10... | collective-permute-start | bytes 393224 | tf_op jit(solution)/shard_map/ppermute | solution.py:36
  64.7 6.4 %collective-permute-start.19 = (bf16[256,256]{1,0:T(8,128)(2,1)S(1)}, bf16[256,256]{1,0:T(8,128)(2,1)S(1)}, u32[]{:S(2)}, u32[]{:S(2)}) collective-permute-start(bf16[256,256]{1,0:T(8,128)(2,1)S(1)} %product.1.refs_4_), channel_id=1, source_target_pairs={{0,16},{8,24},{16,0},{24,8},{1,17},{9,25},{17,1},{25,9},{2,18},{10... | collective-permute-start | bytes 393224 | tf_op jit(solution)/shard_map/ppermute | solution.py:36
  64.7 6.4 %collective-permute-start.20 = (bf16[256,256]{1,0:T(8,128)(2,1)S(1)}, bf16[256,256]{1,0:T(8,128)(2,1)S(1)}, u32[]{:S(2)}, u32[]{:S(2)}) collective-permute-start(bf16[256,256]{1,0:T(8,128)(2,1)S(1)} %product.1.refs_4_), channel_id=1, source_target_pairs={{0,24},{8,16},{16,8},{24,0},{1,25},{9,17},{17,9},{25,1},{2,26},{10... | collective-permute-start | bytes 393224 | tf_op jit(solution)/shard_map/ppermute | solution.py:36
  66.3 4.8 %collective-permute-start.10 = (bf16[2,2,128,128]{3,2,1,0:T(8,128)(2,1)S(1)}, bf16[2,2,128,128]{3,2,1,0:T(8,128)(2,1)S(1)}, u32[]{:S(2)}, u32[]{:S(2)}) collective-permute-start(bf16[2,2,128,128]{3,2,1,0:T(8,128)(2,1)S(1)} %pad_maximum_fusion.2.refs_0_), channel_id=1, source_target_pairs={{0,1},{1,0},{2,3},{3,2},{4,5},{5,4},{6,7},{7,6},{8,9},{9,8},{10,11... | collective-permute-start | bytes 393224 | tf_op jit(solution)/shard_map/ppermute | solution.py:36
  66.3 4.8 %collective-permute-start.11 = (bf16[2,2,128,128]{3,2,1,0:T(8,128)(2,1)S(1)}, bf16[2,2,128,128]{3,2,1,0:T(8,128)(2,1)S(1)}, u32[]{:S(2)}, u32[]{:S(2)}) collective-permute-start(bf16[2,2,128,128]{3,2,1,0:T(8,128)(2,1)S(1)} %collective-permute-done.9.refs_1_), channel_id=1, source_target_pairs={{0,1},{1,0},{2,3},{3,2},{4,5},{5,4},{6,7},{7,6},{8,9},{9,8},{10,11... | collective-permute-start | bytes 393224 | tf_op jit(solution)/shard_map/ppermute | solution.py:36
